TPU v7x, 32 devices: a whole 2x2x4 slice. The times are simulated.
32 devices in a mesh: fsdp: 4 (over x, core), ctx: 4 (over z), tp: 2 (over y).
Axes of the slice: x: 2, y: 2, z: 4, core: 2. Of those that a mesh axis runs over, the one named last changes fastest.
Arguments:
- tokens: bfloat16 [4, 2048, 1536], P('fsdp', 'ctx'), may hold values from -6 to 6
- segments: int32 [4, 2048], P('fsdp', 'ctx'), may hold values from 0 to 7, never falling along the last dimension, each value on 1 to 800 neighbouring positions
- adapter_index: int32 [4], P('fsdp'), may hold values from 0 to 7
- w_qkv: bfloat16 [1536, 3, 1536], P('fsdp', None, 'tp'), may hold values from -0.15625 to 0.15625
- w_forget: bfloat16 [1536, 24], P('fsdp', 'tp'), may hold values from -0.4375 to 0.4375
- forget_bias: bfloat16 [24], P('tp'), may hold values from -2 to 8
- w_out: bfloat16 [1536, 1536], P('tp', 'fsdp'), may hold values from -0.625 to 0.625
- w_gate_up: bfloat16 [1536, 2, 4096], P('fsdp', None, 'tp'), may hold values from -0.15625 to 0.15625
- w_down: bfloat16 [4096, 1536], P('tp', 'fsdp'), may hold values from -0.09375 to 0.09375
- gain_attn: bfloat16 [1536], replicated, may hold values from 0.5 to 1.5
- gain_ffn: bfloat16 [1536], replicated, may hold values from 0.5 to 1.5
- a_qkv: bfloat16 [8, 1536, 16], replicated, may hold values from -0.15625 to 0.15625
- b_qkv: bfloat16 [8, 16, 3, 1536], replicated, may hold values from -1.5 to 1.5
- a_out: bfloat16 [8, 1536, 16], replicated, may hold values from -0.625 to 0.625
- b_out: bfloat16 [8, 16, 1536], replicated, may hold values from -1.5 to 1.5
- a_gate_up: bfloat16 [8, 1536, 16], replicated, may hold values from -0.15625 to 0.15625
- b_gate_up: bfloat16 [8, 16, 2, 4096], replicated, may hold values from -1.5 to 1.5
- a_down: bfloat16 [8, 4096, 16], replicated, may hold values from -0.09375 to 0.09375
- b_down: bfloat16 [8, 16, 1536], replicated, may hold values from -1.5 to 1.5
- cotangent: bfloat16 [4, 2048, 1536], P('fsdp', 'ctx'), may hold values from -6 to 6
Outputs:
- block_output: bfloat16 [4, 2048, 1536], P('fsdp', 'ctx')
- grad_tokens: float32 [4, 2048, 1536], P('fsdp', 'ctx')
- grad_a_qkv: float32 [8, 1536, 16], P(None, ('fsdp', 'ctx', 'tp'))
- grad_b_qkv: float32 [8, 16, 3, 1536], P(None, None, None, ('fsdp', 'ctx', 'tp'))
- grad_a_out: float32 [8, 1536, 16], P(None, ('fsdp', 'ctx', 'tp'))
- grad_b_out: float32 [8, 16, 1536], P(None, None, ('fsdp', 'ctx', 'tp'))
- grad_a_gate_up: float32 [8, 1536, 16], P(None, ('fsdp', 'ctx', 'tp'))
- grad_b_gate_up: float32 [8, 16, 2, 4096], P(None, None, None, ('fsdp', 'ctx', 'tp'))
- grad_a_down: float32 [8, 4096, 16], P(None, ('fsdp', 'ctx', 'tp'))
- grad_b_down: float32 [8, 16, 1536], P(None, None, ('fsdp', 'ctx', 'tp'))
Inputs may be any that keep to these rules, and one draw needn't show every extreme that they name: `segments`: document numbers never fall along a sequence; every document of 0 to 7 is present with 1 to 800 tokens, and one has exactly 800.
All inputs are finite; a program needn't handle non-finite values.
Results may differ from a plain program's by a relative error of at most 0.01575.
The roundings to bfloat16 on the way count: a program that leaves them out, or rounds other values in their place, can miss the bound.
Values may be sent and summed in bfloat16 or wider, within the bound.
No kernel may reach another device: no remote copies, remote signals or barrier semaphores. Data moves between devices by JAX's collectives and lax.ppermute only.
A program may use at most 576 MiB of HBM per device.

v0:
```python
import jax
import jax.numpy as jnp
from jax import lax
from jax.experimental import pallas as pl
from jax.experimental.pallas import tpu as pltpu
from jax.sharding import PartitionSpec as P

HD = 64
DOC_MOST = 800
DOCS = 8
BF = jnp.bfloat16
F32 = jnp.float32
HI = lax.Precision.HIGHEST


def dot(a, b):
    return jnp.dot(a, b, preferred_element_type=F32)


def dot_t(a, b):
    return lax.dot_general(a, b, (((1,), (1,)), ((), ())), preferred_element_type=F32)


def t_dot(a, b):
    return lax.dot_general(a, b, (((0,), (0,)), ((), ())), preferred_element_type=F32)


def xor_order(size):
    order, bit = [0], size // 2
    while bit:
        order, bit = order + [step ^ bit for step in order], bit // 2
    return order


def after(values, *done):
    return lax.optimization_barrier((values, *done))[0]


def far_blocks(shard, dim):
    size = lax.axis_size("fsdp")
    own, bit = shard, size // 2
    while True:
        got = lax.ppermute(own, "fsdp", [(i, i ^ bit) for i in range(size)])
        if bit == 2:
            return own, got
        own, bit = jnp.concatenate([own, got], axis=dim), bit // 2


def near_blocks(own, got, dim):
    both = jnp.concatenate([own, got], axis=dim)
    size = lax.axis_size("fsdp")
    return [both, lax.ppermute(both, "fsdp", [(i, i ^ 1) for i in range(size)])]


def to_xor(values, dim, size, rank):
    block = values.shape[dim] // size
    return jnp.concatenate(
        [lax.dynamic_slice_in_dim(values, (rank ^ step) * block, block, dim) for step in xor_order(size)],
        axis=dim,
    )


def from_xor(values, dim, size, rank):
    block = values.shape[dim] // size
    bits = size.bit_length() - 1
    pieces = []
    for natural in range(size):
        mixed = rank ^ natural
        place = sum(((mixed >> j) & 1) << (bits - 1 - j) for j in range(bits))
        pieces.append(lax.dynamic_slice_in_dim(values, place * block, block, dim))
    return jnp.concatenate(pieces, axis=dim)


def shift(values, hop, size):
    pairs = [(i, i + hop) for i in range(size) if 0 <= i + hop < size]
    return lax.ppermute(values, "ctx", pairs)


LANES = 128
BLK = 256
BIG = -1e30


def spec(shape, index):
    return pl.BlockSpec(shape, index)


def call(kernel, grid, ins, in_specs, outs, out_specs, scratch=(), prefetch=0, flops=0, nbytes=0, exps=0, aliases=None):
    return pl.pallas_call(
        kernel,
        out_shape=outs,
        grid_spec=pltpu.PrefetchScalarGridSpec(
            num_scalar_prefetch=prefetch, grid=grid, in_specs=in_specs, out_specs=out_specs, scratch_shapes=list(scratch)
        ),
        compiler_params=pltpu.CompilerParams(
            dimension_semantics=("arbitrary",) * len(grid), vmem_limit_bytes=56 * 2**20
        ),
        input_output_aliases=aliases or {},
        cost_estimate=pl.CostEstimate(flops=1, bytes_accessed=1, transcendentals=0),
    )(*ins)


def whole(values):
    return spec(values.shape, lambda *_: (0,) * len(values.shape))


def lane_ids(rows):
    return lax.broadcasted_iota(jnp.int32, (rows, LANES), 1)


def split3(values):
    high = values.astype(BF)
    rest = values - high.astype(F32)
    mid = rest.astype(BF)
    return high, mid, (rest - mid.astype(F32)).astype(BF)


def split_lanes(values, n):
    lane = lane_ids(values.shape[0])
    values = jnp.where(lane < n, values, 0.0)
    high, mid, low = (part.astype(F32) for part in split3(values))
    return high + pltpu.roll(mid, n, 1) + pltpu.roll(low, 2 * n, 1)


def exact_dot(mask, values):
    high, mid, low = split3(values)
    return dot(mask, high) + dot(mask, mid) + dot(mask, low)


def norm_terms(blocks):
    width = sum(b.shape[1] for b in blocks)
    total = sum(jnp.sum(b * b, axis=1, keepdims=True) for b in blocks)
    return lax.rsqrt(total / width + 1e-05)


def pair_lanes(pair, n_heads, kind):
    lane = lax.broadcasted_iota(jnp.int32, (LANES, LANES), 1)
    to = lane & (HD - 1)
    head = jnp.where(lane >= HD, 2 * pair, 2 * pair + 1)
    gate_at = 3 if kind == "k" else 0
    part = to - gate_at
    source = jnp.where((part >= 0) & (part < 3), part * n_heads + head, -1)
    if kind != "d":
        ones = to - (3 - gate_at)
        source = jnp.where((ones >= 0) & (ones < 3), 3 * n_heads + DOCS, source)
        source = jnp.where((to >= 8) & (to < 8 + DOCS), to - 8 + 3 * n_heads, source)
    return (lax.broadcasted_iota(jnp.int32, (LANES, LANES), 0) == source).astype(BF)


def pair_of(values, gate_parts, select):
    extra = dot(gate_parts, select).astype(BF)
    low = lane_ids(values.shape[0]) < HD
    return jnp.where(low, values, extra), jnp.where(low, extra, values)


def pair_ones(values):
    low = lane_ids(values.shape[0]) < HD
    one = jnp.ones((), BF)
    return jnp.where(low, values, one), jnp.where(low, one, values)


def block_at(index):
    return pl.ds(pl.multiple_of(index * BLK, BLK), BLK)


def causal_from(rows, first):
    row = lax.broadcasted_iota(jnp.int32, (rows, BLK), 0)
    return row + first >= lax.broadcasted_iota(jnp.int32, (rows, BLK), 1)


def lane_column(acc, lane_at):
    return jnp.sum(jnp.where(lane_ids(acc.shape[0]) == lane_at, acc, 0.0), axis=1, keepdims=True)


def attention_forward(bounds, q, k, v, gq, gk, gates, total, n_heads):
    rows, keys = q.shape[0], k.shape[0]
    n_before = (keys - rows) // BLK
    pairs = n_heads // 2
    assert rows == 2 * BLK

    def kernel(
        lo_ref, q_ref, k_ref, v_ref, gq_ref, gk_ref, gate_ref, tot_ref, mixed_ref, float_ref, one_ref, two_ref,
        qx, scores, tops, parts, accs, log_ref,
    ):
        pair = pl.program_id(0)
        pick_k = pair_lanes(pair, n_heads, "k")
        for side, value in enumerate(pair_of(q_ref[...], gq_ref[...], pair_lanes(pair, n_heads, "q"))):
            qx[side] = value
        both, late, early = slice(0, rows), slice(BLK, rows), slice(0, BLK)

        def score(kb, here, at, mask=None, first=False):
            for side, key in enumerate(pair_of(k_ref[here, :], gk_ref[here, :], pick_k)):
                s = dot_t(qx[side, at, :], key)
                if mask is not None:
                    s = jnp.where(mask, s, BIG)
                scores[side, at, here] = s
                top = jnp.maximum(s[:, :LANES], s[:, LANES:])
                tops[side, at, :] = top if first else jnp.maximum(tops[side, at, :], top)

        def gather(here, at, first=False):
            for side in range(2):
                w = jnp.exp(scores[side, at, here] - tops[side, at, :1])
                part = w[:, :LANES] + w[:, LANES:]
                acc = dot(w.astype(BF), v_ref[here, :])
                parts[side, at, :] = part if first else parts[side, at, :] + part
                accs[side, at, :] = acc if first else accs[side, at, :] + acc

        own = [slice(b * BLK, (b + 1) * BLK) for b in (n_before, n_before + 1)]
        low, high = lo_ref[0], jnp.minimum(lo_ref[1], n_before)
        score(n_before, own[0], both, causal_from(rows, 0), True)
        score(n_before + 1, own[1], late, causal_from(BLK, 0))
        pl.loop(high, n_before)(lambda kb: score(kb, block_at(kb), both))
        pl.loop(low, high)(lambda kb: score(kb, block_at(kb), early))
        for side in range(2):
            tops[side] = jnp.broadcast_to(jnp.max(tops[side], axis=1, keepdims=True), (rows, LANES))
        gather(own[0], both, True)
        gather(own[1], late)
        pl.loop(high, n_before)(lambda kb: gather(block_at(kb), both))
        pl.loop(low, high)(lambda kb: gather(block_at(kb), early))
        lane = lane_ids(rows)
        results, logs = [], jnp.zeros((rows, LANES), F32)
        for side in range(2):
            row_total = jnp.sum(parts[side], axis=1, keepdims=True)
            results.append(accs[side] / row_total)
            logs = jnp.where(lane == 2 * pair + side, tops[side] + jnp.log(row_total), logs)
        out = jnp.where(lane < HD, results[0], results[1])
        mixed_ref[...] = out.astype(BF)
        float_ref[...] = out

        @pl.when(pair == 0)
        def _():
            log_ref[...] = logs

        @pl.when(pair > 0)
        def _():
            log_ref[...] = jnp.where((lane >> 1) == pair, logs, log_ref[...])

        @pl.when(pair == pairs - 1)
        def _():
            values = gate_ref[...] - log_ref[...]
            rest = gq_ref[...].astype(F32)
            one_ref[...] = jnp.where(lane < 3 * n_heads, split_lanes(values, n_heads), rest).astype(BF)
            values = values + tot_ref[:1, :]
            two_ref[...] = jnp.where(lane < 3 * n_heads, split_lanes(values, n_heads), rest).astype(BF)

    here = lambda n: spec((n, LANES), lambda i, *_: (0, i))
    shared = lambda n: spec((n, LANES), lambda i, *_: (0, 0))
    return call(
        kernel,
        (pairs,),
        (bounds, q, k, v, gq, gk, gates, total),
        [here(rows), here(keys), here(keys), shared(rows), shared(keys), shared(rows), shared(8)],
        (
            jax.ShapeDtypeStruct(q.shape, BF), jax.ShapeDtypeStruct(q.shape, F32),
            jax.ShapeDtypeStruct((rows, LANES), BF), jax.ShapeDtypeStruct((rows, LANES), BF),
        ),
        (here(rows), here(rows), shared(rows), shared(rows)),
        [pltpu.VMEM((2, rows, LANES), BF), pltpu.VMEM((2, rows, keys), F32)]
        + [pltpu.VMEM((2, rows, LANES), F32)] * 3 + [pltpu.VMEM((rows, LANES), F32)],
        prefetch=1,
    )


def attention_dq(bounds, q, k, v, d, gq, gk, n_heads, n_far):
    rows, keys = q.shape[0], k.shape[0]
    n_before = (keys - rows) // BLK
    pairs = n_heads // 2

    def kernel(lo_ref, q_ref, k_ref, v_ref, d_ref, gq_ref, gk_ref, gd_ref, dq_ref, row_ref, far_ref, qx, dx, accs):
        pair = pl.program_id(0)
        lane = lane_ids(rows)
        pick_k = pair_lanes(pair, n_heads, "k")
        for side, value in enumerate(pair_of(q_ref[...], gq_ref[...], pair_lanes(pair, n_heads, "q"))):
            qx[side] = value
        for side, value in enumerate(pair_of(d_ref[...], gd_ref[...], pair_lanes(pair, n_heads, "d"))):
            dx[side] = value
        both, late, early = slice(0, rows), slice(BLK, rows), slice(0, BLK)

        @pl.when(pair == 0)
        def _():
            far_ref[...] = jnp.zeros_like(far_ref)
            row_ref[...] = jnp.zeros_like(row_ref)

        def block(here, at, mask=None, first=False):
            values = pair_ones(v_ref[here, :])
            for side, key in enumerate(pair_of(k_ref[here, :], gk_ref[here, :], pick_k)):
                s = dot_t(qx[side, at, :], key)
                if mask is not None:
                    s = jnp.where(mask, s, BIG)
                ds = (jnp.exp(s) * dot_t(dx[side, at, :], values[side])).astype(BF)
                acc = dot(ds, key)
                accs[side, at, :] = acc if first else accs[side, at, :] + acc

        low, high = lo_ref[0], jnp.minimum(lo_ref[1], n_before)

        @pl.when(low < n_far)
        def _():
            accs[...] = jnp.zeros_like(accs)
            pl.loop(high, n_far)(lambda kb: block(block_at(kb), both))
            pl.loop(low, jnp.minimum(high, n_far))(lambda kb: block(block_at(kb), early))
            for side in range(2):
                moved = jnp.sum(jnp.where(lane == HD * (1 - side), accs[side], 0.0))
                far_ref[...] += jnp.where(lane[:8] == 2 * pair + side, moved, 0.0)
            block(slice(n_before * BLK, (n_before + 1) * BLK), both, causal_from(rows, 0))

        @pl.when(low >= n_far)
        def _():
            block(slice(n_before * BLK, (n_before + 1) * BLK), both, causal_from(rows, 0), True)

        block(slice((n_before + 1) * BLK, (n_before + 2) * BLK), late, causal_from(BLK, 0))
        pl.loop(jnp.maximum(high, n_far), n_before)(lambda kb: block(block_at(kb), both))
        pl.loop(jnp.maximum(low, n_far), high)(lambda kb: block(block_at(kb), early))
        dq_ref[...] = (jnp.where(lane < HD, accs[0], accs[1]) * HD ** (-0.5)).astype(BF)
        for side in range(2):
            total = lane_column(accs[side], HD * (1 - side))
            row_ref[...] = jnp.where(lane == 2 * pair + side, total, row_ref[...])

    here = lambda n: spec((n, LANES), lambda i, *_: (0, i))
    shared = lambda n: spec((n, LANES), lambda i, *_: (0, 0))
    return call(
        kernel,
        (pairs,),
        (bounds, q, k, v, d, gq, gk, d),
        [here(rows), here(keys), here(keys), here(rows), shared(rows), shared(keys), spec((rows, LANES), lambda i, *_: (0, pairs))],
        (
            jax.ShapeDtypeStruct(q.shape, BF), jax.ShapeDtypeStruct((rows, LANES), F32),
            jax.ShapeDtypeStruct((8, LANES), F32),
        ),
        (here(rows), shared(rows), shared(8)),
        [pltpu.VMEM((2, rows, LANES), BF)] * 2 + [pltpu.VMEM((2, rows, LANES), F32)],
        prefetch=1,
    )


def score_block(kx, vx, queries, grads, at, dks, dvs, mask=None, first=False):
    for side in range(2):
        s = dot_t(kx[side, at, :], queries[side])
        if mask is not None:
            s = jnp.where(mask, s, BIG)
        w = jnp.exp(s)
        ds = (w * dot_t(vx[side, at, :], grads[side])).astype(BF)
        dk, dv = dot(ds, queries[side]), dot(w.astype(BF), grads[side])
        dks[side, at, :] = dk if first else dks[side, at, :] + dk
        dvs[side, at, :] = dv if first else dvs[side, at, :] + dv


def attention_dkv_own(k, v, q, d, gq, gk, n_heads):
    rows = q.shape[0]
    place = k.shape[0] // rows - 1
    pairs = n_heads // 2

    def kernel(k_ref, v_ref, q_ref, d_ref, gq_ref, gd_ref, gk_ref, dk_ref, dv_ref, own_ref, kx, vx, dks, dvs):
        pair = pl.program_id(0)
        lane = lane_ids(rows)
        pick_q, pick_d = (pair_lanes(pair, n_heads, "q"), pair_lanes(pair, n_heads, "d"))
        for side, value in enumerate(pair_of(k_ref[...], gk_ref[...], pair_lanes(pair, n_heads, "k"))):
            kx[side] = value
        for side, value in enumerate(pair_ones(v_ref[...])):
            vx[side] = value
        both, late, early = slice(0, rows), slice(BLK, rows), slice(0, BLK)

        @pl.when(pair == 0)
        def _():
            own_ref[...] = jnp.zeros_like(own_ref)

        def load(here):
            return pair_of(q_ref[here, :], gq_ref[here, :], pick_q), pair_of(d_ref[here, :], gd_ref[here, :], pick_d)

        keep = lax.broadcasted_iota(jnp.int32, (rows, BLK), 0) - BLK <= lax.broadcasted_iota(jnp.int32, (rows, BLK), 1)
        first_keep = lax.broadcasted_iota(jnp.int32, (BLK, BLK), 0) <= lax.broadcasted_iota(jnp.int32, (BLK, BLK), 1)
        score_block(kx, vx, *load(late), both, dks, dvs, keep, True)
        score_block(kx, vx, *load(early), early, dks, dvs, first_keep)
        for side in range(2):
            column = lane_column(dks[side], HD * (1 - side) + 3)
            own_ref[...] = jnp.where(lane == 2 * pair + side, column, own_ref[...])
        dk_ref[...] = jnp.where(lane < HD, dks[0], dks[1])
        dv_ref[...] = jnp.where(lane < HD, dvs[0], dvs[1])

    heads_spec = lambda n: spec((n, LANES), lambda i, *_: (0, i))
    shared = lambda n: spec((n, LANES), lambda i, *_: (0, 0))
    keys_spec = spec((rows, LANES), lambda i, *_: (place, i))
    return call(
        kernel, (pairs,), (k, v, q, d, gq, d, gk),
        [
            keys_spec, keys_spec, heads_spec(rows), heads_spec(rows), shared(rows),
            spec((rows, LANES), lambda i, *_: (0, pairs)), spec((rows, LANES), lambda i, *_: (place, 0)),
        ],
        (jax.ShapeDtypeStruct(q.shape, F32), jax.ShapeDtypeStruct(q.shape, F32), jax.ShapeDtypeStruct((rows, LANES), F32)),
        (heads_spec(rows), heads_spec(rows), shared(rows)),
        [pltpu.VMEM((2, rows, LANES), BF)] * 2 + [pltpu.VMEM((2, rows, LANES), F32)] * 2,
    )


def attention_dkv_next(bounds, k, v, q_one, q_two, d_one, d_two, gkn, dk, dv, n_heads):
    rows, tail = q_one.shape[0], q_two.shape[0]
    place = k.shape[0] // rows - 1
    pairs = n_heads // 2
    assert 0 < tail - BLK <= BLK

    def kernel(
        hi_ref, k_ref, v_ref, q1_ref, d1_ref, gq1_ref, gd1_ref, q2_ref, d2_ref, gq2_ref, gd2_ref, gkn_ref,
        dk_own, dv_own, dk_ref, dv_ref, next_ref, kx, vx, dks, dvs,
    ):
        pair = pl.program_id(0)
        lane = lane_ids(rows)
        both, late, early = slice(0, rows), slice(BLK, rows), slice(0, BLK)
        few, many = hi_ref[0], hi_ref[1]

        @pl.when(pair == 0)
        def _():
            next_ref[...] = jnp.zeros_like(next_ref)

        @pl.when(many > 0)
        def _():
            pick_q, pick_d = (pair_lanes(pair, n_heads, "q"), pair_lanes(pair, n_heads, "d"))
            for side, value in enumerate(pair_of(k_ref[...], gkn_ref[...], pair_lanes(pair, n_heads, "k"))):
                kx[side] = value
            for side, value in enumerate(pair_ones(v_ref[...])):
                vx[side] = value
            dks[...] = jnp.zeros_like(dks)
            dvs[...] = jnp.zeros_like(dvs)

            def block(refs, here, at):
                q_ref, gq_ref, d_ref, gd_ref = refs
                queries = pair_of(q_ref[here, :], gq_ref[here, :], pick_q)
                score_block(kx, vx, queries, pair_of(d_ref[here, :], gd_ref[here, :], pick_d), at, dks, dvs)

            one, two = (q1_ref, gq1_ref, d1_ref, gd1_ref), (q2_ref, gq2_ref, d2_ref, gd2_ref)
            pl.loop(0, jnp.minimum(few, 2))(lambda j: block(one, block_at(j), both))
            pl.loop(few, jnp.minimum(many, 2))(lambda j: block(one, block_at(j), late))
            pl.when(few > 2)(lambda: block(two, early, both))
            pl.when((few <= 2) & (many > 2))(lambda: block(two, early, late))
            pl.when(many > 3)(lambda: block(two, slice(BLK, tail), both))
            for side in range(2):
                value = lane_column(dks[side], HD * (1 - side) + 3)
                next_ref[...] = jnp.where(lane == 2 * pair + side, value, next_ref[...])
            dk_ref[...] = (dk_own[...] + jnp.where(lane < HD, dks[0], dks[1])).astype(BF)
            dv_ref[...] = (dv_own[...] + jnp.where(lane < HD, dvs[0], dvs[1])).astype(BF)

        @pl.when(many == 0)
        def _():
            dk_ref[...] = dk_own[...].astype(BF)
            dv_ref[...] = dv_own[...].astype(BF)

    heads_spec = lambda n: spec((n, LANES), lambda i, *_: (0, i))
    shared = lambda n: spec((n, LANES), lambda i, *_: (0, 0))
    last = lambda n: spec((n, LANES), lambda i, *_: (0, pairs))
    keys_spec = spec((rows, LANES), lambda i, *_: (place, i))
    return call(
        kernel, (pairs,), (bounds, k, v, q_one, d_one, q_one, d_one, q_two, d_two, q_two, d_two, gkn, dk, dv),
        [
            keys_spec, keys_spec, heads_spec(rows), heads_spec(rows), last(rows), last(rows),
            heads_spec(tail), heads_spec(tail), last(tail), last(tail), shared(rows), heads_spec(rows), heads_spec(rows),
        ],
        (jax.ShapeDtypeStruct(dk.shape, BF), jax.ShapeDtypeStruct(dk.shape, BF), jax.ShapeDtypeStruct((rows, LANES), F32)),
        (heads_spec(rows), heads_spec(rows), shared(rows)),
        [pltpu.VMEM((2, rows, LANES), BF)] * 2 + [pltpu.VMEM((2, rows, LANES), F32)] * 2,
        prefetch=1,
    )


def project(offs, x, x_far, tail, gain, w, side_w, qkv_b, bias, cols, rank_r, filled=None, before=0):
    width = gain.shape[1]
    block = width // 4
    own = filled is None
    rows = x.shape[0] // (2 * BLK) * 2 * BLK
    row_steps = 1 if own else 2
    parts = ("q", "k", "v") if own else ("k", "v")
    assert rows == 2 * BLK and BLK <= tail <= rows - 32

    def kernel(*refs):
        offs_ref, x_ref = refs[0], refs[1]
        at = 2
        if not own:
            far_ref, at = refs[2], 3
        gain_ref, *pieces, side_ref, b_ref, bias_ref = refs[at : at + 8]
        at += 8 + (0 if own else 3)
        outs, scr = refs[at:-3], refs[-3:]
        part, step = pl.program_id(0), pl.program_id(1)
        n_outs = dict(zip(("n", "low", "q", "k", "v", "logits") if own else ("k", "v", "logits"), outs))
        scr, low_scr, joint = scr
        at_rows = pl.ds(pl.multiple_of(step * rows, rows), rows)

        @pl.when(part == 0)
        def _():
            blocks = []
            for k in range(4):
                here = pl.ds(pl.multiple_of(offs_ref[k], LANES), block)
                value = x_ref[:, here]
                if not own:
                    far = jnp.concatenate([far_ref[:BLK, here], far_ref[tail + 32 - BLK : tail + 32, here]], axis=0)
                    value = jnp.where(step == 0, far, value)
                blocks.append(value.astype(F32))
            factor = norm_terms(blocks)
            for k in range(4):
                here = pl.ds(pl.multiple_of(offs_ref[k], LANES), block)
                scr[at_rows, k * block : (k + 1) * block] = (blocks[k] * factor * gain_ref[:, here]).astype(BF)
            side = dot(scr[at_rows, :], side_ref[...])
            low = side[:, LANES - rank_r :].astype(BF)
            low_scr[at_rows, :rank_r] = low
            n_outs["logits"][at_rows, :] = side + bias_ref[...]
            if own:
                n_outs["n"][...] = scr[...]
                n_outs["low"][...] = low

        @pl.when(step == 0)
        def _():
            for k in range(4):
                joint[k * block : (k + 1) * block, :] = pieces[k][...]

        value = dot(scr[at_rows, :], joint[...])
        value = (value + dot(low_scr[at_rows, :rank_r], b_ref[...])).astype(BF)
        for n, name in enumerate(parts):
            @pl.when(part == n)
            def _(name=name):
                out = n_outs[name]
                out[at_rows, :] = (value.astype(F32) * HD ** (-0.5)).astype(BF) if name == "q" else value

    keys = before + rows if own else filled[0].shape[0]
    ins = [offs, x] + ([] if own else [x_far]) + [gain, *w, side_w, qkv_b, bias] + ([] if own else list(filled))
    row_spec = spec((rows, width), lambda i, *_: (0, 0))
    in_specs = [row_spec] + ([] if own else [whole(x_far)])
    first = 0 if own else 1
    column = lambda n: spec((n, cols), lambda j, *_: (0, j + first))
    in_specs += [whole(gain), *[column(block)] * 4, whole(side_w), column(rank_r), whole(bias)]
    if not own:
        in_specs += [pl.BlockSpec(memory_space=pl.ANY)] * 3
    some = row_steps * rows
    at_keys = lambda n: spec((some, n), lambda *_: (before // some if own else 0, 0))
    outs = [jax.ShapeDtypeStruct((keys, cols), BF)] * 2 + [jax.ShapeDtypeStruct((keys, LANES), F32)]
    out_specs = [at_keys(cols), at_keys(cols), at_keys(LANES)]
    if own:
        here = lambda n: spec((rows, n), lambda *_: (0, 0))
        outs = [
            jax.ShapeDtypeStruct((rows, width), BF),
            jax.ShapeDtypeStruct((rows, rank_r), BF),
            jax.ShapeDtypeStruct((rows, cols), BF),
        ] + outs
        out_specs = [here(width), here(rank_r), here(cols)] + out_specs
    return call(
        kernel, (len(parts), row_steps), ins, in_specs, tuple(outs), tuple(out_specs),
        [pltpu.VMEM((some, width), BF), pltpu.VMEM((some, LANES), BF), pltpu.VMEM((width, cols), BF)], prefetch=1,
        aliases={} if own else {11: 0, 12: 1, 13: 2},
    )


def gate_tables(logits, seg_keys, seg_row, n_heads, rows):
    keys = logits.shape[0]
    before = keys - rows
    one = 3 * n_heads + DOCS

    def kernel(logit_ref, seg_ref, row_ref, gq_ref, gk_ref, gkn_ref, gate_ref, tot_ref):
        lane = lane_ids(BLK)
        doc = lane - 3 * n_heads + 1
        doc_lane = (doc > 0) & (doc <= DOCS)
        inner = lax.broadcasted_iota(jnp.int32, (BLK, BLK), 1) > lax.broadcasted_iota(jnp.int32, (BLK, BLK), 0)
        later = inner.astype(BF)

        def forget(at):
            value = logit_ref[at, :]
            value = jnp.minimum(value, 0.0) - jnp.log(1.0 + jnp.exp(-jnp.abs(value)))
            return jnp.where((lane < n_heads) & (seg_ref[at, :] > 0), value, 0.0)

        def lanes(values, docs):
            return (split_lanes(values, n_heads) + docs + jnp.where(lane == one, 1.0, 0.0)).astype(BF)

        def docs_k(at):
            return jnp.where(doc_lane & (doc != seg_ref[at, :]), BIG, 0.0)

        def suffix(first, last, carry, out_ref, base):
            for b in range(last - 1, first - 1, -1):
                at = slice(b * BLK, (b + 1) * BLK)
                values = forget(at)
                sums = exact_dot(later, values) + carry
                out_ref[b * BLK - base : (b + 1) * BLK - base, :] = lanes(sums, docs_k(at))
                carry = carry + jnp.sum(values, axis=0, keepdims=True)
            return carry

        n_before, n_all = before // BLK, keys // BLK
        zero = jnp.zeros((1, LANES), F32)
        near = suffix((before - rows) // BLK, n_before, zero, gk_ref, 0)
        tot_ref[...] = jnp.broadcast_to(near, tot_ref.shape)
        suffix(0, (before - rows) // BLK, near, gk_ref, 0)
        suffix(n_before, n_all, zero, gkn_ref, before)
        own = jnp.concatenate([forget(slice(b * BLK, (b + 1) * BLK)) for b in range(n_before, n_all)], axis=0)
        for b in range(rows // BLK):
            at = slice(before + b * BLK, before + (b + 1) * BLK)
            here = slice(b * BLK, (b + 1) * BLK)
            q_pos = lax.broadcasted_iota(jnp.int32, (BLK, rows), 0) + b * BLK
            k_pos = lax.broadcasted_iota(jnp.int32, (BLK, rows), 1)
            same = (row_ref[...] == seg_ref[at, :]) & (k_pos <= q_pos)
            sums = exact_dot(same.astype(BF), own)
            gate_ref[here, :] = sums
            gq_ref[here, :] = lanes(sums, jnp.where(doc_lane & (doc == seg_ref[at, :]), 1.0, 0.0))
            gk_ref[at, :] = lanes(-sums, docs_k(at))

    shape = lambda n, t: jax.ShapeDtypeStruct((n, LANES), t)
    outs = (shape(rows, BF), shape(keys, BF), shape(rows, BF), shape(rows, F32), shape(8, F32))
    return call(
        kernel, (1,), (logits, seg_keys, seg_row), [whole(logits), whole(seg_keys), whole(seg_row)],
        outs, tuple(whole(o) for o in outs), flops=10**8, nbytes=4 * 10**6,
    )


def weight_halves(w):
    half = w[0].shape[0] // 2
    at = lambda row: spec((half, w[0].shape[1]), lambda *_: (row, 0))
    return [at(0), at(0), at(1), at(1)]


def out_projection(offs, rank, x, mixed_own, mixed_far, w, a_own, a_far, out_b, gain, ffn_a):
    rows, width = x.shape
    block = width // 4
    rank_r = a_own.shape[1]

    def kernel(
        offs_ref, rank_ref, x_ref, mo, mf, wo0, wo1, wf0, wf1, ao, af, b_ref, gain_ref, fa, h_ref, n_ref, low_ref, lo_ref
    ):
        def run(m0, m1, w0, w1, a0, a1):
            low = (dot(m0[...], a0[...]) + dot(m1[...], a1[...])).astype(BF)
            lo_ref[...] = low
            for half in range(2):
                both = dot(m0[...], w0[half][...]) + dot(m1[...], w1[half][...])
                both = both + dot(low, b_ref[:, 2 * half * block : 2 * (half + 1) * block])
                for j in range(2):
                    k = 2 * half + j
                    here = pl.ds(pl.multiple_of(offs_ref[k], LANES), block)
                    value = x_ref[:, here].astype(F32) + both[:, j * block : (j + 1) * block]
                    h_ref[:, k * block : (k + 1) * block] = value

        pl.when(rank_ref[0] == 0)(lambda: run(mo, mf, (wo0, wo1), (wf0, wf1), ao, af))
        pl.when(rank_ref[0] != 0)(lambda: run(mf, mo, (wf0, wf1), (wo0, wo1), af, ao))
        value = h_ref[...]
        normed = (value * norm_terms([value]) * gain_ref[...]).astype(BF)
        n_ref[...] = normed
        low_ref[...] = dot(normed, fa[...]).astype(BF)

    rowed = whole
    outs = (
        jax.ShapeDtypeStruct((rows, width), F32), jax.ShapeDtypeStruct((rows, width), BF),
        jax.ShapeDtypeStruct((rows, rank_r), BF), jax.ShapeDtypeStruct((rows, rank_r), BF),
    )
    ins = (offs, rank, x, mixed_own, mixed_far, *w, *w, a_own, a_far, out_b, gain, ffn_a)
    return call(
        kernel, (1,), ins,
        [rowed(x), rowed(mixed_own), rowed(mixed_far)] + weight_halves(w) + [whole(v) for v in ins[9:]],
        outs, tuple(rowed(o) for o in outs), prefetch=2, flops=4 * rows * width * mixed_own.shape[1],
        nbytes=4 * width * mixed_own.shape[1] + 8 * rows * width,
    )


def feed_forward(rank, normed, low, cot, grad_low, gate_up, down, ffn_b, down_a):
    rows, width = normed.shape
    block = width // 4
    half = rows // 2
    rank_r = low.shape[1]
    unit_cols = down_a.shape[0]
    tile = 512 if unit_cols % 512 == 0 else unit_cols
    tiles = unit_cols // tile
    down_at = down[0].shape[1] // tile - tiles

    def kernel(
        rank_ref, x_ref, low_ref, cot_ref, gl_ref, *rest,
    ):
        pieces, rest = rest[:12], rest[12:]
        bg_ref, bu_ref, ad_ref, *rest, wg, wu, wd = rest
        step = pl.program_id(0)
        units_ref, gg_ref, gu_ref, far_ref, own_ref, own_low_ref, part_ref, part_low_ref = rest

        @pl.when(step == 0)
        def _():
            part_ref[...] = jnp.zeros_like(part_ref)
            part_low_ref[...] = jnp.zeros_like(part_low_ref)

        for n, joint in enumerate((wg, wu, wd)):
            for k in range(4):
                joint[k * block : (k + 1) * block, :] = pieces[4 * n + k][...]
        gate = dot(x_ref[...], wg[...]) + dot(low_ref[...], bg_ref[...])
        up = dot(x_ref[...], wu[...]) + dot(low_ref[...], bu_ref[...])
        grad = dot(cot_ref[...], wd[...]) + dot_t(gl_ref[...], ad_ref[...])
        sig = jax.nn.sigmoid(gate)
        act = gate * sig
        units_ref[...] = (act * up).astype(BF)
        gg = (grad * up * sig * (1.0 + gate * (1.0 - sig))).astype(BF)
        gu = (grad * act).astype(BF)
        gg_ref[...] = gg
        gu_ref[...] = gu
        part_low_ref[:, :rank_r] += dot_t(gg, bg_ref[...]) + dot_t(gu, bu_ref[...])
        part_ref[...] += dot_t(gg, wg[...]) + dot_t(gu, wu[...])

        @pl.when(step == tiles - 1)
        def _():
            mine = pl.ds(pl.multiple_of(rank_ref[0] * half, half), half)
            theirs = pl.ds(pl.multiple_of((1 - rank_ref[0]) * half, half), half)
            far_ref[:, :width] = part_ref[theirs, :].astype(BF)
            far_ref[:, width:] = split_lanes(part_low_ref[theirs, :], rank_r).astype(BF)
            own_ref[...] = part_ref[mine, :]
            own_low_ref[...] = part_low_ref[mine, :]

    out = jax.ShapeDtypeStruct((rows, unit_cols), BF)
    out_spec = spec((rows, tile), lambda i, *_: (0, i))
    sums = (jax.ShapeDtypeStruct((rows, width), F32), jax.ShapeDtypeStruct((rows, LANES), F32))
    ends = (
        jax.ShapeDtypeStruct((half, width + LANES), BF), jax.ShapeDtypeStruct((half, width), F32),
        jax.ShapeDtypeStruct((half, LANES), F32),
    )
    return call(
        kernel,
        (tiles,),
        (rank, normed, low, cot, grad_low, *gate_up, *gate_up, *down, ffn_b, ffn_b, down_a),
        [
            whole(normed), whole(low), whole(cot), whole(grad_low),
            *[spec((block, tile), lambda i, *_: (0, i)) for _ in range(4)],
            *[spec((block, tile), lambda i, *_: (0, i + tiles)) for _ in range(4)],
            *[spec((block, tile), lambda i, *_: (0, i + down_at)) for _ in range(4)],
            spec((rank_r, tile), lambda i, *_: (0, i)),
            spec((rank_r, tile), lambda i, *_: (0, i + tiles)),
            spec((tile, rank_r), lambda i, *_: (i, 0)),
        ],
        (out, out, out, *ends),
        (out_spec, out_spec, out_spec, *[whole(e) for e in ends]),
        [pltpu.VMEM(e.shape, F32) for e in sums] + [pltpu.VMEM((width, tile), BF)] * 3,
        prefetch=1,
    )


def whole_low(parts, n):
    parts = parts.astype(F32)
    return parts[:, :n] + parts[:, n : 2 * n] + parts[:, 2 * n : 3 * n]


def middle(rank, own, got, own_low, hidden, cot, gain, ffn_a, out_b, w, a_own, a_far):
    half, width = own.shape
    depth = width // 2
    rank_r = out_b.shape[0]
    cols = a_own.shape[0]

    def kernel(
        rank_ref, own_ref, got_ref, low_ref, h_ref, cot_ref, gain_ref, fa, b_ref, wo0, wo1, wf0, wf1, ao, af,
        gh_ref, ghb_ref, glf_ref, glo_ref, mine_ref, far_ref,
    ):
        ffn_low = (low_ref[:, :rank_r] + whole_low(got_ref[:, width:], rank_r)).astype(BF)
        glf_ref[...] = ffn_low
        incoming = own_ref[...] + got_ref[:, :width].astype(F32) + dot_t(ffn_low, fa[...])
        value = h_ref[...]
        factor = norm_terms([value])
        scaled = incoming * gain_ref[...]
        mean = jnp.mean(value * scaled, axis=1, keepdims=True)
        grad = cot_ref[...].astype(F32) + (factor * scaled - value * (factor * factor * factor * mean))
        gh_ref[...] = grad
        low_precision = grad.astype(BF)
        ghb_ref[...] = low_precision
        left, right = low_precision[:, :depth], low_precision[:, depth:]
        out_low = dot_t(low_precision, b_ref[...]).astype(BF)
        glo_ref[...] = out_low
        mine_ref[...] = (dot_t(left, wo0[...]) + dot_t(right, wo1[...]) + dot_t(out_low, ao[...])).astype(BF)
        far_ref[...] = (dot_t(left, wf0[...]) + dot_t(right, wf1[...]) + dot_t(out_low, af[...])).astype(BF)

    outs = (
        jax.ShapeDtypeStruct((half, width), F32), jax.ShapeDtypeStruct((half, width), BF),
        jax.ShapeDtypeStruct((half, rank_r), BF), jax.ShapeDtypeStruct((half, rank_r), BF),
        jax.ShapeDtypeStruct((half, cols), BF), jax.ShapeDtypeStruct((half, cols), BF),
    )
    ins = (rank, own, got, own_low, hidden, cot, gain, ffn_a, out_b, *w, *w, a_own, a_far)
    mine = lambda v: spec((half, v.shape[1]), lambda i, r: (r[0], 0))
    in_specs = [whole(own), whole(got), whole(own_low), mine(hidden), mine(cot)] + [whole(v) for v in ins[6:9]]
    in_specs += weight_halves(w) + [whole(a_own), whole(a_far)]
    return call(
        kernel, (1,), ins, in_specs, outs, tuple(whole(o) for o in outs), prefetch=1,
        flops=4 * half * width * cols, nbytes=4 * width * cols + 16 * half * width,
    )


def mixed_gradient(rank, own, far, mixed, n_heads, tail):
    half, cols = own.shape

    def kernel(rank_ref, own_ref, far_ref, mixed_ref, out_ref, tail_ref):
        lane = lane_ids(half)
        for ref, first in ((own_ref, rank_ref[0]), (far_ref, 1 - rank_ref[0])):
            at = pl.ds(pl.multiple_of(first * half, half), half)
            sums = jnp.zeros((half, LANES), F32)
            for pair in range(n_heads // 2):
                here = slice(pair * LANES, (pair + 1) * LANES)
                product = ref[:, here].astype(F32) * mixed_ref[at, here]
                a = jnp.sum(jnp.where(lane < HD, product, 0.0), axis=1, keepdims=True)
                b = jnp.sum(jnp.where(lane < HD, 0.0, product), axis=1, keepdims=True)
                sums = jnp.where(lane == 2 * pair, -a, jnp.where(lane == 2 * pair + 1, -b, sums))
            out_ref[at, :cols] = ref[...]
            out_ref[at, cols:] = split_lanes(sums, n_heads).astype(BF)
        tail_ref[...] = out_ref[:tail, :]

    outs = [jax.ShapeDtypeStruct((n, cols + LANES), BF) for n in (2 * half, tail)]
    return call(
        kernel, (1,), (rank, own, far, mixed), [whole(own), whole(far), whole(mixed)],
        tuple(outs), tuple(whole(o) for o in outs), prefetch=1,
        flops=4 * half * cols, nbytes=16 * half * cols,
    )


def input_gradient(rank, grads, logits, seg_keys, seg_row, row_lanes, own_lanes, next_lanes, across, w, side_w, qkv_b, low_qkv, n_heads):
    rows, cols = grads[0].shape
    depth = w[0].shape[0]
    half = rows // 2
    rank_r = qkv_b.shape[0]
    before = logits.shape[0] - rows
    steps = 3
    chunk = 2 * depth // (2 * steps)

    def kernel(
        rank_ref, q_ref, k_ref, v_ref, logit_ref, seg_ref, seg_row_ref, r_ref, o_ref, n_ref, a_ref, w0, w1, s0, s1, b_ref,
        lq_ref, far_ref, own_ref, low_ref, tq_ref, tk_ref, tv_ref, gl_ref,
    ):
        @pl.when(pl.program_id(0) == 0)
        def _():
            lane = lane_ids(rows)
            t = lax.broadcasted_iota(jnp.int32, (rows, rows), 0)
            i = lax.broadcasted_iota(jnp.int32, (rows, rows), 1)
            same = ((seg_row_ref[...] == seg_ref[...]) & (i >= t)).astype(BF)
            total = exact_dot(same, r_ref[...] - o_ref[...]) + exact_dot((i < t).astype(BF), n_ref[...])
            total = total + a_ref[:1, :]
            value = jnp.where(lane < n_heads, total * jax.nn.sigmoid(-logit_ref[...]), 0.0)
            gl_ref[...] = value.astype(BF)
            low = dot_t(q_ref[...], b_ref[:, :cols]) + dot_t(k_ref[...], b_ref[:, cols : 2 * cols])
            low_ref[...] = low + dot_t(v_ref[...], b_ref[:, 2 * cols :])
            for out, grad in ((tq_ref, q_ref), (tk_ref, k_ref), (tv_ref, v_ref)):
                out[...] = t_dot(lq_ref[...], grad[...])

        mine = pl.ds(pl.multiple_of(rank_ref[0] * half, half), half)
        theirs = pl.ds(pl.multiple_of((1 - rank_ref[0]) * half, half), half)
        for p, (w_ref, s_ref) in enumerate(((w0, s0), (w1, s1))):
            def part(at):
                value = dot_t(q_ref[at, :], w_ref[:, :cols]) + dot_t(k_ref[at, :], w_ref[:, cols : 2 * cols])
                return value + dot_t(v_ref[at, :], w_ref[:, 2 * cols :]) + dot_t(gl_ref[at, :], s_ref[...])

            far_ref[p] = part(theirs).astype(BF)
            own_ref[p] = part(mine)

    ins = (rank, *grads, logits, seg_keys, seg_row, row_lanes, own_lanes, next_lanes, across, w[0], w[1], side_w, side_w, qkv_b, low_qkv)
    at_own = lambda v: spec((rows, v.shape[1]), lambda i, *_: (before // rows, 0))
    in_specs = [whole(g) for g in grads] + [at_own(logits), at_own(seg_keys)]
    in_specs += [whole(v) for v in (seg_row, row_lanes, own_lanes, next_lanes, across)]
    n_col = w[0].shape[1]
    in_specs += [spec((chunk, n_col), lambda i, *_: (i, 0))] * 2
    in_specs += [spec((chunk, LANES), lambda i, *_: (i, 0)), spec((chunk, LANES), lambda i, *_: (i + steps, 0))]
    in_specs += [whole(qkv_b), whole(low_qkv)]
    outs = (
        jax.ShapeDtypeStruct((2, half, depth), BF), jax.ShapeDtypeStruct((2, half, depth), F32),
        jax.ShapeDtypeStruct((rows, rank_r), F32),
        *[jax.ShapeDtypeStruct((rank_r, cols), F32)] * 3,
    )
    halves = spec((2, half, chunk), lambda i, *_: (0, 0, i))
    return call(
        kernel, (steps,), ins, in_specs, outs, (halves, halves, *[whole(o) for o in outs[2:]]), [pltpu.VMEM((rows, LANES), BF)],
        prefetch=1, flops=2 * rows * 2 * depth * 3 * cols, nbytes=4 * depth * 3 * cols,
    )


def token_gradient(offs, rank, own, got, grad_low, a, x, gain, grad_hidden):
    half, width = grad_hidden.shape
    block = width // 4

    def kernel(offs_ref, rank_ref, own_ref, got_ref, low_ref, a_ref, x_ref, gain_ref, gh_ref, out_ref):
        blocks, scaled, product = [], [], 0.0
        for k in range(4):
            here = pl.ds(pl.multiple_of(offs_ref[k], LANES), block)
            cols = slice(k % 2 * block, (k % 2 + 1) * block)
            value = own_ref[k // 2][:, cols] + got_ref[k // 2][:, cols].astype(F32)
            value = value + dot_t(low_ref[...], a_ref[k * block : (k + 1) * block, :])
            blocks.append(x_ref[:, here].astype(F32))
            scaled.append(value * gain_ref[:, here])
            product = product + jnp.sum(blocks[k] * scaled[k], axis=1, keepdims=True)
        factor = norm_terms(blocks)
        mean = product / width
        for k in range(4):
            here = pl.ds(pl.multiple_of(offs_ref[k], LANES), block)
            back = factor * scaled[k] - blocks[k] * (factor * factor * factor * mean)
            out_ref[:, here] = (gh_ref[:, k * block : (k + 1) * block] + back).astype(BF)

    mine = lambda v: spec((half, v.shape[1]), lambda i, o, r: (r[0], 0))
    out = jax.ShapeDtypeStruct((half, width), BF)
    return call(
        kernel, (1,), (offs, rank, own, got, grad_low, a, x, gain, grad_hidden),
        [whole(own), whole(got), mine(grad_low), whole(a), mine(x), whole(gain), whole(grad_hidden)],
        out, whole(out), prefetch=2, nbytes=20 * half * width,
    )


def both_halves(rank, own, far):
    half, width = own.shape

    def kernel(rank_ref, own_ref, far_ref, out_ref):
        @pl.when(pl.program_id(0) == rank_ref[0])
        def _():
            out_ref[...] = own_ref[...].astype(F32)

        @pl.when(pl.program_id(0) != rank_ref[0])
        def _():
            out_ref[...] = far_ref[...].astype(F32)

    return call(
        kernel, (2,), (rank, own, far), [whole(own), whole(far)], jax.ShapeDtypeStruct((2 * half, width), F32),
        spec((half, width), lambda i, *_: (i, 0)), prefetch=1, nbytes=16 * half * width,
    )


def down_partial(units, down, down_a):
    rows, unit_cols = units.shape
    block = down[0].shape[0]
    width = 4 * block
    rank_r = down_a.shape[1]

    def kernel(u_ref, w0, w1, w2, w3, a_ref, out_ref, low_ref):
        low_ref[...] = jnp.zeros_like(low_ref)
        low_ref[:, :rank_r] = dot(u_ref[...], a_ref[...])
        for k, w_ref in enumerate((w0, w1, w2, w3)):
            out_ref[:, k * block : (k + 1) * block] = dot_t(u_ref[...], w_ref[...]).astype(BF)
        out_ref[:, width:] = split_lanes(low_ref[...], rank_r).astype(BF)

    rowed = lambda n: spec((BLK, n), lambda i: (i, 0))
    last = spec((block, unit_cols), lambda i: (0, 0))
    return call(
        kernel, (rows // BLK,), (units, *down, down_a), [rowed(unit_cols), last, last, last, last, whole(down_a)],
        jax.ShapeDtypeStruct((rows, width + LANES), BF), rowed(width + LANES), [pltpu.VMEM((BLK, LANES), F32)],
    )


def block_result(offs, hidden, own, got, down_b):
    rows, width = hidden.shape
    block = width // 4
    rank_r = down_b.shape[0]

    def kernel(offs_ref, h_ref, own_ref, got_ref, b_ref, out_ref):
        low = (whole_low(own_ref[:, width:], rank_r) + whole_low(got_ref[:, width:], rank_r)).astype(BF)
        for k in range(4):
            here = pl.ds(pl.multiple_of(offs_ref[k], LANES), block)
            cols = slice(k * block, (k + 1) * block)
            both = own_ref[:, cols].astype(F32) + got_ref[:, cols].astype(F32)
            out_ref[:, here] = (h_ref[:, cols] + both + dot(low, b_ref[:, cols])).astype(BF)

    rowed = lambda v: spec((BLK, v.shape[1]), lambda i, *_: (i, 0))
    out = jax.ShapeDtypeStruct((rows, width), BF)
    return call(
        kernel, (rows // BLK,), (offs, hidden, own, got, down_b),
        [rowed(hidden), rowed(own), rowed(got), whole(down_b)], out, rowed(out),
        prefetch=1, nbytes=12 * rows * width,
    )


def pack_gradients(inv, rank, xor_own, xor_both, halves, out_a, wide, owners):
    rank_r, width = xor_own[0].shape
    block = width // 4
    part, unit_part = block // 8, wide[0].shape[1] // 16
    n = len(wide) * unit_part + (len(xor_own) + len(xor_both) + len(halves) + 1) * part
    assert owners == 32 and block % LANES == 0

    def kernel(inv_ref, rank_ref, *refs):
        out_ref, refs = refs[-1], list(refs[:-1])
        take = lambda count: [refs.pop(0) for _ in range(count)]
        own_refs, both_refs = take(len(xor_own)), take(len(xor_both))
        half_refs, (ao, af), wide_refs = take(len(halves)), take(2), take(len(wide))
        for f in range(4):
            mine = rank_ref[0] == f // 2
            at = pl.ds(pl.multiple_of(inv_ref[f], LANES), block)
            cols = slice(f % 2 * block, (f % 2 + 1) * block)
            blocks = [jnp.where(mine, r[:, at], 0.0) for r in own_refs] + [r[:, at] for r in both_refs]
            blocks += [jnp.where(mine, r[:, cols], 0.0) for r in half_refs]
            blocks.append(jnp.where(mine, ao[:, cols], af[:, cols]))
            units = 8 * unit_part
            big = [jnp.where(mine, r[:, f % 2 * units : (f % 2 + 1) * units], 0.0) for r in wide_refs]
            for j in range(8):
                row = [b[:, j * unit_part : (j + 1) * unit_part] for b in big]
                row += [b[:, j * part : (j + 1) * part] for b in blocks]
                at_row = slice((8 * f + j) * rank_r, (8 * f + j + 1) * rank_r)
                out_ref[at_row, :] = jnp.concatenate(row, axis=1).astype(BF)

    ins = (inv, rank, *xor_own, *xor_both, *halves, *out_a, *wide)
    out = jax.ShapeDtypeStruct((owners * rank_r, n), BF)
    return call(kernel, (1,), ins, [whole(v) for v in ins[2:]], out, whole(out), prefetch=2)


def spread_gradients(every, landed, n_adapters, rank_r, n_wide, n_small, unit_part, part):
    n = landed.shape[1]
    senders = landed.shape[0] // (4 * rank_r)

    def kernel(every_ref, x_ref, out_ref, swap_ref):
        sums = []
        for f in range(4):
            total = 0.0
            for i in range(senders):
                at = (f * senders + i) * rank_r
                total = total + x_ref[at : at + rank_r, :].astype(F32)
            sums.append(total)
        for a in range(n_adapters):
            total = 0.0
            for f in range(4):
                total = total + jnp.where(every_ref[f] == a, sums[f], 0.0)
            out_ref[a] = total
            swap_ref[a] = total.T

    outs = (jax.ShapeDtypeStruct((n_adapters, rank_r, n), F32), jax.ShapeDtypeStruct((n_adapters, n, rank_r), F32))
    return call(kernel, (1,), (every, landed), [whole(landed)], outs, tuple(whole(o) for o in outs), prefetch=1)


def body(
    tokens, segments, adapter_index, w_qkv, w_forget, forget_bias, w_out, w_gate_up, w_down,
    gain_attn, gain_ffn, a_qkv, b_qkv, a_out, b_out, a_gate_up, b_gate_up, a_down, b_down, cotangent,
):
    count, rows, width = tokens.shape
    assert count == 1
    head_cols = w_qkv.shape[2]
    n_heads = w_forget.shape[1]
    unit_cols = w_gate_up.shape[2]
    rank_r = a_qkv.shape[2]
    n_f, n_c, n_t = (lax.axis_size("fsdp"), lax.axis_size("ctx"), lax.axis_size("tp"))
    f_rank, t_rank = (lax.axis_index("fsdp"), lax.axis_index("tp"))
    hops = -(-(DOC_MOST - 1) // rows)
    assert hops == 2 and n_c > 2 and n_t == 2 and n_f % 4 == 0
    tail = -(-(DOC_MOST - 1 - rows) // 32) * 32
    before = hops * rows
    half = rows // 2
    block = width // 4
    first = t_rank == 0
    rank = t_rank.astype(jnp.int32)[None]

    def other(values):
        return lax.ppermute(values, "tp", [(0, 1), (1, 0)])

    def four(pieces):
        return [*pieces, *[lax.ppermute(part, "fsdp", [(i, i ^ 1) for i in range(n_f)]) for part in pieces]]

    mix = lambda values, dim: to_xor(values, dim, n_f, f_rank)
    direct = n_f == 4 and block % LANES == 0
    if direct:
        offs = jnp.stack([(f_rank ^ step) * block for step in xor_order(4)]).astype(jnp.int32)
        lay = lambda values, dim: values
    else:
        offs = jnp.arange(4, dtype=jnp.int32) * block
        lay = mix

    pick = adapter_index[0]
    tok = lay(tokens[0], 1)
    seg_one = segments[0] + 1
    note = jnp.zeros((32, width), BF).at[0, :rows].set(seg_one.astype(BF))
    qkv_own = jnp.concatenate([w_qkv[:, i] for i in range(3)], axis=1)
    qkv_far = far_blocks(qkv_own, 0)
    prev_one = shift(jnp.concatenate([tok, after(note, qkv_own)], axis=0), 1, n_c)
    side = jnp.broadcast_to(pick.astype(BF), (w_forget.shape[0], 1))
    side_far = far_blocks(after(jnp.concatenate([w_forget, side], axis=1), qkv_own), 0)
    take = lambda table: lax.dynamic_index_in_dim(table, pick, 0, keepdims=False)
    mine = lambda values, n, dim: lax.dynamic_slice_in_dim(values, t_rank * n, n, dim)
    theirs = lambda values, n, dim: lax.dynamic_slice_in_dim(values, (1 - t_rank) * n, n, dim)
    qkv_a, ffn_a = (mix(take(a_qkv), 0), mix(take(a_gate_up), 0))
    out_b, down_b = (mix(take(b_out), 1), mix(take(b_down), 1))
    qkv_b = mine(take(b_qkv), head_cols, 2).reshape(rank_r, 3 * head_cols)
    out_a = take(a_out)
    out_a_own, out_a_far = (mine(out_a, head_cols, 0), theirs(out_a, head_cols, 0))
    ffn_b = mine(take(b_gate_up), unit_cols, 2).reshape(rank_r, 2 * unit_cols)
    down_a = mine(take(a_down), unit_cols, 0)
    gain_one = lay(gain_attn.astype(F32), 0)[None]
    gain_two = mix(gain_ffn.astype(F32), 0)[None]
    bias = jnp.pad(forget_bias.astype(F32), (0, LANES - n_heads))[None]
    cot = mix(cotangent[0], 1)
    grad_low_down = dot_t(cot, down_b).astype(BF)

    out_pair = jnp.concatenate([w_out, other(w_out)], axis=0)
    gate_up_own = jnp.concatenate([w_gate_up[:, 0], w_gate_up[:, 1]], axis=1)
    down_own = w_down.T
    shared = n_f == 4 and n_c % 2 == 0
    odd = lax.axis_index("ctx") % 2
    down_sent = down_own
    if shared:
        down_sent = lax.dynamic_slice_in_dim(down_own, odd * (unit_cols // 2), unit_cols // 2, 1)
    (
        prev_one, qkv_far, side_far, out_pair, qkv_a, qkv_b, gain_one, bias, ffn_a, out_b, down_b, out_a_own, out_a_far,
        ffn_b, down_a, gain_two, cot, grad_low_down, gate_up_own, down_own, down_sent,
    ) = lax.optimization_barrier((
        prev_one, qkv_far, side_far, out_pair, qkv_a, qkv_b, gain_one, bias, ffn_a, out_b, down_b, out_a_own, out_a_far,
        ffn_b, down_a, gain_two, cot, grad_low_down, gate_up_own, down_own, down_sent,
    ))
    out_far = far_blocks(out_pair, 1)
    prev_two = shift(prev_one[rows - tail :], 1, n_c)
    qkv_four = four(qkv_far)
    side_all = jnp.concatenate(near_blocks(*side_far, 0), axis=0)
    every = from_xor(side_all[:: w_forget.shape[0], n_heads], 0, n_f, f_rank).astype(jnp.int32)
    side_w = jnp.concatenate([side_all, jnp.zeros((width, LANES - n_heads - 1 - rank_r), BF), qkv_a], axis=1)
    args = (gain_one, qkv_four, side_w, qkv_b, bias, head_cols, rank_r)
    down_far = far_blocks(down_sent, 0)
    tok_in, prev_two = lax.optimization_barrier((tok, prev_two))
    normed, low_qkv, query, *filled = project(offs, tok_in, None, tail, *args, None, before)
    seg_two = prev_two[tail, :rows].astype(jnp.int32)
    seg_far = []
    for b in range(-(-tail // BLK)):
        start, end = min(b * BLK, tail + 32 - BLK), min((b + 1) * BLK, tail)
        known = seg_two[rows - tail + b * BLK : rows - tail + end]
        seg_far.append(jnp.pad(known, (b * BLK - start, BLK - (end - start))))
    seg_keys = jnp.concatenate(seg_far + [prev_one[rows, :rows].astype(jnp.int32), seg_one])
    last_keys = jnp.max(seg_keys.reshape(-1, BLK), axis=1)
    lows = jnp.sum(last_keys[None, :] < seg_one[::BLK][:, None], axis=1).astype(jnp.int32)

    gate_up_far = far_blocks(after(gate_up_own, out_far[1], down_far[1], query), 0)
    keys, vals, logits = project(offs, prev_one, prev_two, tail, *args, filled)
    out_w = near_blocks(out_far[0], after(out_far[1], query), 1)
    logits, out_w = lax.optimization_barrier((logits, out_w))
    seg_col, seg_row = (seg_keys[:, None], seg_one[None, :])
    gq, gk, gk_next, gates, total = gate_tables(logits, seg_col, seg_row, n_heads, rows)
    mixed_own, mixed_f, gq_one, gq_two = attention_forward(lows, query, keys, vals, gq, gk, gates, total, n_heads)
    mixed_far = other(mixed_own)
    sent_q1 = jnp.concatenate([query, gq_one], axis=1)
    sent_q2 = jnp.concatenate([query[:tail], gq_two[:tail]], axis=1)
    if shared:
        down_pair = lax.ppermute(after(down_far[1], keys), "ctx", [(i, i ^ 1) for i in range(n_c)])
        down_pair = after(down_pair, mixed_own)
        lower, upper = jnp.where(odd == 0, down_far[1], down_pair), jnp.where(odd == 0, down_pair, down_far[1])
        down_got = jnp.concatenate([lower, upper], axis=1)
    else:
        down_got = down_far[1]
    mixed_far, sent_q1, sent_q2, down_got = lax.optimization_barrier((mixed_far, sent_q1, sent_q2, down_got))
    next_q1 = shift(sent_q1, -1, n_c)
    next_q2 = shift(sent_q2, -2, n_c)

    gate_up_w = four((after(gate_up_own, mixed_own), after(gate_up_far[1], down_got))) if shared else four(gate_up_far)
    down_w = four((after(down_own, mixed_own), down_got)) if shared else four(down_far)
    if shared:
        mixed_far, gate_up_far = lax.optimization_barrier((mixed_far, gate_up_far))
    hidden, normed_ffn, low_ffn, low_out = out_projection(
        offs, rank, tok, mixed_own, mixed_far, out_w, out_a_own, out_a_far, out_b, gain_two, ffn_a
    )
    units, grad_gate, grad_up, far, own, own_low = feed_forward(
        rank, normed_ffn, low_ffn, cot, grad_low_down, gate_up_w, down_w, ffn_b, down_a
    )
    got = other(far)
    down_part = down_partial(after(units, far), down_w, down_a)
    qkv_w = [jnp.concatenate([after(qkv_four[i], far), qkv_four[i + 1]], axis=0) for i in (0, 2)]
    got, down_part, qkv_w = lax.optimization_barrier((got, down_part, qkv_w))
    grad_hidden, grad_hidden_b, grad_low_ffn, grad_low_out, gm_own, gm_send = middle(
        rank, own, got, own_low, hidden, cot, gain_two, ffn_a, out_b, out_w, out_a_own, out_a_far
    )
    grad_mixed, sent_d2 = mixed_gradient(rank, gm_own, other(gm_send), mixed_f, n_heads, tail)

    next_d1 = shift(grad_mixed, -1, n_c)
    next_d2 = shift(sent_d2, -2, n_c)
    grad_q, row_lanes, across = attention_dq(
        lows, query, keys, vals, grad_mixed, gq_one, gk, n_heads, (before - rows) // BLK
    )
    across = shift(across, -1, n_c)
    docs_at = head_cols + 3 * n_heads
    grad_k_own, grad_v_own, own_lanes = attention_dkv_own(keys, vals, query, after(grad_mixed, grad_q), gq_one, gk, n_heads)
    next_q1, next_q2, next_d1, next_d2, _ = lax.optimization_barrier((next_q1, next_q2, next_d1, next_d2, grad_k_own))
    next_docs = jnp.concatenate([next_q1[::BLK, docs_at : docs_at + DOCS], next_q2[::BLK, docs_at : docs_at + DOCS]])
    next_docs = next_docs.astype(F32)
    ids = jnp.arange(1, DOCS + 1).astype(F32)
    next_first = jnp.where(jnp.sum(next_docs, 1) > 0, jnp.sum(next_docs * ids[None, :], 1), 99.0)
    last_rows = seg_one[BLK - 1 :: BLK].astype(F32)
    highs = jnp.sum(next_first[None, :] <= last_rows[:, None], axis=1).astype(jnp.int32)
    lane = lax.broadcasted_iota(jnp.int32, (1, width), 1)
    own_part = lambda values: values * (lane // (width // 2) == t_rank)
    natural = lambda values: from_xor(values, 1, n_f, f_rank)
    by_tp = lambda a, b: jnp.concatenate([jnp.where(first, a, b), jnp.where(first, b, a)], axis=1)
    place = lambda values: by_tp(values, jnp.zeros_like(values))
    rows_of = lambda values: lax.dynamic_slice_in_dim(values, t_rank * half, half, 0)
    onehot = (jnp.arange(a_qkv.shape[0])[:, None] == every[None, :]).astype(F32)
    onehot = jnp.repeat(onehot, n_c * n_t, axis=1)

    owners = n_f * n_c * n_t

    def pack(tables):
        packed = jnp.concatenate([t.reshape(rank_r, owners, -1) for t in tables], axis=2).transpose(1, 0, 2)
        return packed.astype(BF).reshape(owners, -1), [t.shape[1] // owners for t in tables]

    def take_apart(spread, sizes):
        spread = spread.reshape(-1, rank_r, sum(sizes))
        outs, at = [], 0
        for size in sizes:
            outs.append(spread[:, :, at : at + size])
            at += size
        return outs

    table_out_a = [t_dot(grad_low_out, rows_of(mixed_own)), t_dot(grad_low_out, rows_of(mixed_far))]
    table_out_b = t_dot(rows_of(low_out), grad_hidden_b)
    table_ffn_a = t_dot(grad_low_ffn, rows_of(normed_ffn))
    tables_ffn = [t_dot(low_ffn, grad_gate), t_dot(low_ffn, grad_up), t_dot(grad_low_down, units)]
    highs, table_out_a, table_out_b, table_ffn_a, tables_ffn = lax.optimization_barrier(
        (highs, table_out_a, table_out_b, table_ffn_a, tables_ffn)
    )
    grad_k, grad_v, next_lanes = attention_dkv_next(
        highs, keys, vals, next_q1, next_q2, next_d1, next_d2, gk_next, grad_k_own, grad_v_own, n_heads
    )
    down_other = other(after(down_part, grad_mixed))

    grads = (grad_q, grad_k, grad_v)
    far_in, own_in, part_low_qkv, *tables_b = input_gradient(
        rank, grads, logits, seg_col, seg_row, row_lanes, own_lanes, next_lanes, across, qkv_w, side_w, qkv_b, low_qkv, n_heads
    )
    grad_low_qkv = (part_low_qkv + other(part_low_qkv)).astype(BF)
    got_in = other(far_in)
    parts = [values[:, width : width + 3 * rank_r].astype(F32).reshape(rows, 3, rank_r) for values in (down_part, down_other)]
    parts = [values[:, 0] + values[:, 1] + values[:, 2] for values in parts]
    low_down = after((parts[0] + parts[1]).astype(BF), far_in)
    grad_tok = token_gradient(offs, rank, own_in, got_in, grad_low_qkv, qkv_a, tok, gain_one, grad_hidden)
    tok_far = other(grad_tok)
    block_output = block_result(offs, hidden, down_part, after(down_other, grad_tok), down_b)
    grad_tokens = both_halves(rank, grad_tok, tok_far)
    if not direct:
        block_output = from_xor(block_output, 1, n_f, f_rank)
        grad_tokens = from_xor(grad_tokens, 1, n_f, f_rank)

    table_qkv_a, table_down_b = t_dot(grad_low_qkv, normed), t_dot(low_down, cot)
    if direct:
        bits = n_f.bit_length() - 1
        inv = [sum((((f_rank ^ i) >> j) & 1) << (bits - 1 - j) for j in range(bits)) * block for i in range(n_f)]
        packed = pack_gradients(
            jnp.stack(inv).astype(jnp.int32), rank, [table_qkv_a, table_down_b], [table_out_b, table_ffn_a], tables_b,
            table_out_a, tables_ffn, owners,
        )
        landed = lax.all_to_all(after(packed, grad_tok), ("fsdp", "ctx", "tp"), 0, 0, tiled=True)
        part, unit_part = width // owners, unit_cols * n_t // owners
        by_row, by_column = spread_gradients(every, landed, a_qkv.shape[0], rank_r, 3, 8, unit_part, part)
        at = [0, unit_part, 2 * unit_part] + [3 * unit_part + i * part for i in range(9)]
        cut = lambda i: by_row[:, :, at[i] : at[i + 1]]
        cut_t = lambda i: by_column[:, at[i] : at[i + 1]]
        return (
            block_output[None], grad_tokens[None], cut_t(3), jnp.stack([cut(7), cut(8), cut(9)], axis=2), cut_t(10),
            cut(5), cut_t(6), jnp.stack([cut(0), cut(1)], axis=2), cut_t(2), cut(4),
        )
    early, early_sizes = pack([
        by_tp(*table_out_a), natural(table_out_b), natural(table_ffn_a), *[place(t) for t in tables_ffn],
    ])
    late, late_sizes = pack([
        own_part(natural(table_qkv_a)), *[place(t) for t in tables_b], own_part(natural(table_down_b)),
    ])
    landed = lax.all_to_all(jnp.concatenate([late, early], axis=1), ("fsdp", "ctx", "tp"), 0, 0, tiled=True)
    split = rank_r * sum(late_sizes)
    spread = jnp.dot(onehot.astype(BF), landed, preferred_element_type=F32)
    done = take_apart(spread[:, :split], late_sizes) + take_apart(spread[:, split:], early_sizes)
    swap = lambda values: values.transpose(0, 2, 1)
    return (
        block_output[None],
        grad_tokens[None],
        swap(done[0]),
        jnp.stack(done[1:4], axis=2),
        swap(done[5]),
        done[6],
        swap(done[7]),
        jnp.stack(done[8:10], axis=2),
        swap(done[10]),
        done[4],
    )


def solution(mesh):
    in_specs = (
        P("fsdp", "ctx", None), P("fsdp", "ctx"), P("fsdp"), P("fsdp", None, "tp"), P("fsdp", "tp"), P("tp"),
        P("tp", "fsdp"), P("fsdp", None, "tp"), P("tp", "fsdp"),
        P(), P(), P(), P(), P(), P(), P(), P(), P(), P(),
        P("fsdp", "ctx", None),
    )
    out_specs = (
        P("fsdp", "ctx", None),
        P("fsdp", "ctx", None),
        P(None, ("fsdp", "ctx", "tp"), None),
        P(None, None, None, ("fsdp", "ctx", "tp")),
        P(None, ("fsdp", "ctx", "tp"), None),
        P(None, None, ("fsdp", "ctx", "tp")),
        P(None, ("fsdp", "ctx", "tp"), None),
        P(None, None, None, ("fsdp", "ctx", "tp")),
        P(None, ("fsdp", "ctx", "tp"), None),
        P(None, None, ("fsdp", "ctx", "tp")),
    )
    return jax.shard_map(body, mesh=mesh, in_specs=in_specs, out_specs=out_specs, check_vma=False)
```

profile of v0, /device:TPU:0, one launch (start us, length us, event | category | flops | bytes accessed | tf_op | source)
XLA Modules:
  0.0 416.9 jit_solution(10810038670171557088)
XLA Ops:
  23.7 5.8 %fusion.22 = (bf16[384,1,2048]{2,1,0:T(2,128)(2,1)}, bf16[384,1,2048]{2,1,0:T(2,128)(2,1)}) fusion(bf16[384,2,2048]{2,1,0:T(2,128)(2,1)S(1)} %copy-done.10), kind=kLoop, calls=%fused_computation.112 | loop fusion | bytes 6291456 | tf_op jit(solution)/shard_map/slice | solution.py:1066
  41.5 4.8 %copy_bitcast_fusion = (bf16[384,2048]{1,0:T(8,128)(2,1)S(1)}, bf16[384,2048]{1,0:T(8,128)(2,1)S(1)}) fusion(bf16[384,1,2048]{2,1,0:T(2,128)(2,1)} %get-tuple-element.316, bf16[384,1,2048]{2,1,0:T(2,128)(2,1)} %get-tuple-element.315), kind=kLoop, calls=%fused_computation.7 | loop fusion | bytes 6291456 | tf_op jit(solution)/shard_map/squeeze | solution.py:1066
  56.3 5.5 %collective-permute-start.4 = (bf16[320,1536]{1,0:T(8,128)(2,1)}, bf16[320,1536]{1,0:T(8,128)(2,1)}, u32[]{:S(2)}, u32[]{:S(2)}) collective-permute-start(bf16[320,1536]{1,0:T(8,128)(2,1)} %slice.135), channel_id=1, source_target_pairs={{0,2},{2,4},{4,6},{1,3},{3,5},{5,7},{8,10},{10,12},{12,14},{9,11},... | collective-permute-start | bytes 2949128 | tf_op jit(solution)/shard_map/ppermute | solution.py:76
  72.6 9.3 %collective-permute-done.4.refs_2_ = bf16[320,1536]{1,0:T(8,128)(2,1)} collective-permute-done((bf16[320,1536]{1,0:T(8,128)(2,1)}, bf16[320,1536]{1,0:T(8,128)(2,1)}, u32[]{:S(2)}, u32[]{:S(2)}) %collective-permute-start.4) | collective-permute-done | bytes 983072 | tf_op jit(solution)/shard_map/ppermute | solution.py:76
  81.9 11.6 %shard_map.267 = (bf16[512,1536]{1,0:T(8,128)(2,1)}, bf16[512,16]{1,0:T(8,128)(2,1)}, bf16[512,768]{1,0:T(8,128)(2,1)}, bf16[1536,768]{1,0:T(8,128)(2,1)}, bf16[...) custom-call(s32[4]{0:T(128)} %pad_add_fusion.1.refs_0_.offs_ref, bf16[512,1536]{1,0:T(8,128)(2,1)} %bitcast.123, ...), custom_call_target="tpu_custom_call" | custom-call | flops 1 | bytes 1 | tf_op jit(solution)/shard_map/pallas_call | solution.py:89
  97.8 14.6 %shard_map.268 = (bf16[1536,768]{1,0:T(8,128)(2,1)}, bf16[1536,768]{1,0:T(8,128)(2,1)}, f32[1536,128]{1,0:T(8,128)}) custom-call(s32[4]{0:T(128)} %pad_add_fusion.1.refs_0_.offs_ref, bf16[544,1536]{1,0:T(8,128)(2,1)} %collective-permute-done.refs_1_, ...), custom_call_target="tpu_custom_call", output_to_operand_aliasing={{0}: (11, {}), {1}: (12, {}), {2}: (13, {})} | custom-call | flops 1 | bytes 1 | tf_op jit(solution)/shard_map/pallas_call | solution.py:89
  122.8 13.7 %shard_map.270 = (bf16[512,768]{1,0:T(8,128)(2,1)}, f32[512,768]{1,0:T(8,128)}, bf16[512,128]{1,0:T(8,128)(2,1)}, bf16[512,128]{1,0:T(8,128)(2,1)}) custom-call(s32[2]{0:T(128)} %fusion.18.lo_ref, bf16[512,768]{1,0:T(8,128)(2,1)} %get-tuple-element.154.q_ref, bf16[1536,768]{1,0:T(8,128)(2,1)} %get-tuple-element.158.k_ref, ...), custom_call_target="tpu_custom_call" | custom-call | flops 1 | bytes 1 | tf_op jit(solution)/shard_map/pallas_call | solution.py:89
  142.6 12.3 %collective-permute-done.10.mf = bf16[512,768]{1,0:T(8,128)(2,1)S(1)} collective-permute-done((bf16[512,768]{1,0:T(8,128)(2,1)}, bf16[512,768]{1,0:T(8,128)(2,1)S(1)}, u32[]{:S(2)}, u32[]{:S(2)}) %collective-permute-start.10) | collective-permute-done | bytes 786464 | tf_op jit(solution)/shard_map/ppermute | solution.py:1026
  154.9 11.1 %collective-permute-done.13.rest_1_.rest_5_ = bf16[384,4096]{1,0:T(8,128)(2,1)} collective-permute-done((bf16[384,4096]{1,0:T(8,128)(2,1)}, bf16[384,4096]{1,0:T(8,128)(2,1)}, u32[]{:S(2)}, u32[]{:S(2)}) %collective-permute-start.13) | collective-permute-done | bytes 3145760 | tf_op jit(solution)/shard_map/ppermute | solution.py:43
  170.2 10.2 %shard_map.271 = (f32[512,1536]{1,0:T(8,128)}, bf16[512,1536]{1,0:T(8,128)(2,1)}, bf16[512,16]{1,0:T(8,128)(2,1)}, bf16[512,16]{1,0:T(8,128)(2,1)}) custom-call(s32[4]{0:T(128)} %pad_add_fusion.1.refs_0_.offs_ref, s32[1]{0:T(128)} %bitcast.4.rank_ref, bf16[512,1536]{1,0:T(8,128)(2,1)} %bitcast.124, bf16[512,768]{1,0:T(8,128)(2,1)} %get-tuple-element.168.mo, ...), custom_call_target="tpu_custom_call" | custom-call | flops 1 | bytes 1 | tf_op jit(solution)/shard_map/pallas_call | solution.py:89
  181.7 28.2 %shard_map.272 = (bf16[512,2048]{1,0:T(8,128)(2,1)}, bf16[512,2048]{1,0:T(8,128)(2,1)}, bf16[512,2048]{1,0:T(8,128)(2,1)}, bf16[256,1664]{1,0:T(8,128)(2,1)}, f32[256,1536]{1,0:T(8,128)}, /*index=5*/f32[256,128]{1,0:T(8,128)}) custom-call(s32[1]{0:T(128)} %bitcast.4.rank_ref, bf16[512,1536]{1,0:T(8,128)(2,1)} %get-tuple-element.186.x_ref, ...), custom_call_target="tpu_custom_call" | custom-call | flops 1 | bytes 1 | tf_op jit(solution)/shard_map/pallas_call | solution.py:89
  213.3 9.4 %shard_map.273.own_ref = bf16[512,1664]{1,0:T(8,128)(2,1)} custom-call(bf16[512,2048]{1,0:T(8,128)(2,1)} %get-tuple-element.199.u_ref, bf16[384,2048]{1,0:T(8,128)(2,1)} %bitcast.127, bf16[384,2048]{1,0:T(8,128)(2,1)} %copy-done.9, bf16[384,2048]{1,0:T(8,128)(2,1)} %collective-permute-done.16.rest_10_.w2, ...), custom_call_target="tpu_custom_call" | custom-call | flops 1 | bytes 1 | tf_op jit(solution)/shard_map/pallas_call | solution.py:89
  234.9 7.6 %shard_map.274 = (f32[256,1536]{1,0:T(8,128)}, bf16[256,1536]{1,0:T(8,128)(2,1)}, bf16[256,16]{1,0:T(8,128)(2,1)}, bf16[256,16]{1,0:T(8,128)(2,1)}, bf16[256,768]{1,0:T(8,128)(2,1)}, /*index=5*/bf16[256,768]{1,0:T(8,128)(2,1)}) custom-call(s32[1]{0:T(128)} %bitcast.4.rank_ref, f32[256,1536]{1,0:T(8,128)} %get-tuple-element.203.own_ref, ...), custom_call_target="tpu_custom_call" | custom-call | flops 1 | bytes 1 | tf_op jit(solution)/shard_map/pallas_call | solution.py:89
  245.4 8.1 %collective-permute-done.19.far_ref = bf16[256,768]{1,0:T(8,128)(2,1)S(1)} collective-permute-done((bf16[256,768]{1,0:T(8,128)(2,1)}, bf16[256,768]{1,0:T(8,128)(2,1)S(1)}, u32[]{:S(2)}, u32[]{:S(2)}) %collective-permute-start.19) | collective-permute-done | bytes 393248 | tf_op jit(solution)/shard_map/ppermute | solution.py:1026
  265.2 15.3 %shard_map.276 = (bf16[512,768]{1,0:T(8,128)(2,1)}, f32[512,128]{1,0:T(8,128)}, f32[8,128]{1,0:T(8,128)}) custom-call(s32[2]{0:T(128)} %fusion.18.lo_ref, bf16[512,768]{1,0:T(8,128)(2,1)} %get-tuple-element.154.q_ref, bf16[1536,768]{1,0:T(8,128)(2,1)} %get-tuple-element.158.k_ref, bf16[1536,768]{1,0:T(8,128)(2,1)} %get-tuple-element.159.v_ref, ...), custom_call_target="tpu_custom_call" | custom-call | flops 1 | bytes 1 | tf_op jit(solution)/shard_map/pallas_call | solution.py:89
  280.6 13.4 %shard_map.277 = (f32[512,768]{1,0:T(8,128)}, f32[512,768]{1,0:T(8,128)}, f32[512,128]{1,0:T(8,128)}) custom-call(bf16[1536,768]{1,0:T(8,128)(2,1)} %get-tuple-element.158.k_ref, bf16[1536,768]{1,0:T(8,128)(2,1)} %get-tuple-element.159.v_ref, bf16[512,768]{1,0:T(8,128)(2,1)} %get-tuple-element.154.q_ref, bf16[512,896]{1,0:T(8,128)(2,1)} %get-tuple-element.215.d_ref.gd_ref, ...), custom_call_target="tpu_custom_call" | custom-call | flops 1 | bytes 1 | tf_op jit(solution)/shard_map/pallas_call | solution.py:89
  295.3 10.8 %collective-permute-done.24.d2_ref.gd2_ref = bf16[288,896]{1,0:T(8,128)(2,1)S(1)} collective-permute-done((bf16[288,896]{1,0:T(8,128)(2,1)}, bf16[288,896]{1,0:T(8,128)(2,1)S(1)}, u32[]{:S(2)}, u32[]{:S(2)}) %collective-permute-start.24) | collective-permute-done | bytes 516128 | tf_op jit(solution)/shard_map/ppermute | solution.py:76
  308.2 20.3 %shard_map.278 = (bf16[512,768]{1,0:T(8,128)(2,1)}, bf16[512,768]{1,0:T(8,128)(2,1)}, f32[512,128]{1,0:T(8,128)}) custom-call(s32[2]{0:T(128)} %fusion.19.hi_ref, bf16[1536,768]{1,0:T(8,128)(2,1)} %get-tuple-element.158.k_ref, bf16[1536,768]{1,0:T(8,128)(2,1)} %get-tuple-element.159.v_ref, bf16[512,896]{1,0:T(8,128)(2,1)} %copy-done.12, ...), custom_call_target="tpu_custom_call" | custom-call | flops 1 | bytes 1 | tf_op jit(solution)/shard_map/pallas_call | solution.py:89
  329.1 11.0 %shard_map.279 = (bf16[2,256,768]{2,1,0:T(8,128)(2,1)}, f32[2,256,768]{2,1,0:T(8,128)}, f32[512,16]{1,0:T(8,128)}, f32[16,768]{1,0:T(8,128)}, f32[16,768]{1,0:T(8,128)}, /*index=5*/f32[16,768]{1,0:T(8,128)}) custom-call(s32[1]{0:T(128)} %bitcast.4.rank_ref, bf16[512,768]{1,0:T(8,128)(2,1)} %get-tuple-element.211.q_ref, ...), custom_call_target="tpu_custom_call" | custom-call | flops 1 | bytes 1 | tf_op jit(solution)/shard_map/pallas_call | solution.py:89
  343.1 6.8 %collective-permute-done.27 = f32[512,16]{1,0:T(8,128)} collective-permute-done((f32[512,16]{1,0:T(8,128)}, f32[512,16]{1,0:T(8,128)}, u32[]{:S(2)}, u32[]{:S(2)}) %collective-permute-start.27) | collective-permute-done | bytes 32800 | tf_op jit(solution)/shard_map/ppermute | solution.py:1026
  359.1 5.0 %shard_map.280.own_ref = bf16[256,1536]{1,0:T(8,128)(2,1)} custom-call(s32[4]{0:T(128)} %pad_add_fusion.1.refs_0_.offs_ref, s32[1]{0:T(128)} %bitcast.4.rank_ref, f32[2,256,768]{2,1,0:T(8,128)} %get-tuple-element.239.own_ref, bf16[2,256,768]{2,1,0:T(8,128)(2,1)} %collective-permute-done.26.got_ref, bf16[512,16]{1,0:T(8,128)(2,1)} %copy-done.24, ...), custom_call_target="tpu_custom_call" | custom-call | flops 1 | bytes 1 | tf_op jit(solution)/shard_map/pallas_call | solution.py:89
  364.1 5.5 %all-to-all-start = ((bf16[32,16,768]{2,1,0:T(8,128)(2,1)}), bf16[32,16,768]{2,1,0:T(8,128)(2,1)S(1)}, u32[]{:S(2)}, u32[]{:S(2)}) async-start(bf16[32,16,768]{2,1,0:T(8,128)(2,1)} %bitcast.55), calls=%async_computation | async-start | bytes 1572864 | tf_op jit(solution)/shard_map/all_to_all | solution.py:1215
  376.1 4.9 %shard_map.281 = bf16[512,1536]{1,0:T(8,128)(2,1)} custom-call(s32[4]{0:T(128)} %pad_add_fusion.1.refs_0_.offs_ref, f32[512,1536]{1,0:T(8,128)} %get-tuple-element.185.h_ref, bf16[512,1664]{1,0:T(8,128)(2,1)} %shard_map.273.own_ref, bf16[512,1664]{1,0:T(8,128)(2,1)} %collective-permute-done.20.got_ref, bf16[16,1536]{1,0:T(8,128)(2,1)} %pad_maximum_fusion.16.b_ref), custom_call_target="tpu_custom_call" | custom-call | flops 1 | bytes 1 | tf_op jit(solution)/shard_map/pallas_call | solution.py:89
  381.0 16.9 %collective-permute-done.28.far_ref = bf16[256,1536]{1,0:T(8,128)(2,1)S(1)} collective-permute-done((bf16[256,1536]{1,0:T(8,128)(2,1)}, bf16[256,1536]{1,0:T(8,128)(2,1)S(1)}, u32[]{:S(2)}, u32[]{:S(2)}) %collective-permute-start.28) | collective-permute-done | bytes 786464 | tf_op jit(solution)/shard_map/ppermute | solution.py:1026
  (251 shorter events, 152.7 us)
Async XLA Ops:
  0.7 48.3 %collective-permute-start.3 = (bf16[768,384]{1,0:T(8,128)(2,1)}, bf16[768,384]{1,0:T(8,128)(2,1)}, u32[]{:S(2)}, u32[]{:S(2)}) collective-permute-start(bf16[768,384]{1,0:T(8,128)(2,1)} %param.28), channel_id=1, source_target_pairs={{0,1},{1,0},{2,3},{3,2},{4,5},{5,4},{6,7},{7,6},{8,9},{9,8},{10,11... | collective-permute-start | bytes 1769480 | tf_op jit(solution)/shard_map/ppermute | solution.py:1026
  6.6 44.2 %collective-permute-start.1 = (bf16[384,2304]{1,0:T(8,128)(2,1)}, bf16[384,2304]{1,0:T(8,128)(2,1)}, u32[]{:S(2)}, u32[]{:S(2)}) collective-permute-start(bf16[384,2304]{1,0:T(8,128)(2,1)} %pad_maximum_fusion.3.refs_3_.refs_4_), channel_id=1, source_target_pairs={{0,16},{8,24},{16,0},{24,8},{1,17},{9,25},{17,1},{25,9},{2,18},{10... | collective-permute-start | bytes 5308424 | tf_op jit(solution)/shard_map/ppermute | solution.py:43
  8.8 41.4 %collective-permute-start.2 = (bf16[384,13]{0,1:T(8,128)(2,1)S(1)}, bf16[384,13]{0,1:T(8,128)(2,1)}, u32[]{:S(2)}, u32[]{:S(2)}) collective-permute-start(bf16[384,13]{0,1:T(8,128)(2,1)S(1)} %concatenate.74), channel_id=1, source_target_pairs={{0,16},{8,24},{16,0},{24,8},{1,17},{9,25},{17,1},{25,9},{2,18},{10... | collective-permute-start | bytes 29960 | tf_op jit(solution)/shard_map/ppermute | solution.py:43
  12.1 38.7 %collective-permute-start = (bf16[544,1536]{1,0:T(8,128)(2,1)}, bf16[544,1536]{1,0:T(8,128)(2,1)}, u32[]{:S(2)}, u32[]{:S(2)}) collective-permute-start(bf16[544,1536]{1,0:T(8,128)(2,1)} %pad_maximum_fusion.4), channel_id=1, source_target_pairs={{0,2},{2,4},{4,6},{1,3},{3,5},{5,7},{8,10},{10,12},{12,14},{9,11},... | collective-permute-start | bytes 5013512 | tf_op jit(solution)/shard_map/ppermute | solution.py:76
  50.8 31.0 %collective-permute-start.5 = (bf16[384,2304]{1,0:T(8,128)(2,1)}, bf16[384,2304]{1,0:T(8,128)(2,1)}, u32[]{:S(2)}, u32[]{:S(2)}) collective-permute-start(bf16[384,2304]{1,0:T(8,128)(2,1)} %pad_maximum_fusion.3.refs_3_.refs_4_), channel_id=1, source_target_pairs={{0,8},{8,0},{16,24},{24,16},{1,9},{9,1},{17,25},{25,17},{2,10},{10... | collective-permute-start | bytes 5308424 | tf_op jit(solution)/shard_map/ppermute | solution.py:1029
  50.8 31.0 %collective-permute-start.6 = (bf16[384,2304]{1,0:T(8,128)(2,1)}, bf16[384,2304]{1,0:T(8,128)(2,1)}, u32[]{:S(2)}, u32[]{:S(2)}) collective-permute-start(bf16[384,2304]{1,0:T(8,128)(2,1)} %collective-permute-done.1.refs_4_.refs_5_), channel_id=1, source_target_pairs={{0,8},{8,0},{16,24},{24,16},{1,9},{9,1},{17,25},{25,17},{2,10},{10... | collective-permute-start | bytes 5308424 | tf_op jit(solution)/shard_map/ppermute | solution.py:1029
  51.3 42.2 %collective-permute-start.8 = (bf16[1536,384]{1,0:T(8,128)(2,1)S(1)}, bf16[1536,384]{1,0:T(8,128)(2,1)}, u32[]{:S(2)}, u32[]{:S(2)}) collective-permute-start(bf16[1536,384]{1,0:T(8,128)(2,1)S(1)} %pad_maximum_fusion.7), channel_id=1, source_target_pairs={{0,16},{8,24},{16,0},{24,8},{1,17},{9,25},{17,1},{25,9},{2,18},{10... | collective-permute-start | bytes 3538952 | tf_op jit(solution)/shard_map/ppermute | solution.py:43
  56.3 25.6 %collective-permute-start.4 = (bf16[320,1536]{1,0:T(8,128)(2,1)}, bf16[320,1536]{1,0:T(8,128)(2,1)}, u32[]{:S(2)}, u32[]{:S(2)}) collective-permute-start(bf16[320,1536]{1,0:T(8,128)(2,1)} %slice.135), channel_id=1, source_target_pairs={{0,2},{2,4},{4,6},{1,3},{3,5},{5,7},{8,10},{10,12},{12,14},{9,11},... | collective-permute-start | bytes 2949128 | tf_op jit(solution)/shard_map/ppermute | solution.py:76
  66.9 29.3 %collective-permute-start.11 = (bf16[384,1024]{1,0:T(8,128)(2,1)}, bf16[384,1024]{1,0:T(8,128)(2,1)}, u32[]{:S(2)}, u32[]{:S(2)}) collective-permute-start(bf16[384,1024]{1,0:T(8,128)(2,1)} %dynamic-slice_bitcast_fusion), channel_id=1, source_target_pairs={{0,16},{8,24},{16,0},{24,8},{1,17},{9,25},{17,1},{25,9},{2,18},{10... | collective-permute-start | bytes 2359304 | tf_op jit(solution)/shard_map/ppermute | solution.py:43
  95.0 23.6 %collective-permute-start.9 = (bf16[1536,768]{1,0:T(8,128)(2,1)S(1)}, bf16[1536,768]{1,0:T(8,128)(2,1)}, u32[]{:S(2)}, u32[]{:S(2)}) collective-permute-start(bf16[1536,768]{1,0:T(8,128)(2,1)S(1)} %constant_dynamic-update-slice_fusion.3.wo0.wf0), channel_id=1, source_target_pairs={{0,8},{8,0},{16,24},{24,16},{1,9},{9,1},{17,25},{25,17},{2,10},{10... | collective-permute-start | bytes 7077896 | tf_op jit(solution)/shard_map/ppermute | solution.py:52
  96.2 69.8 %collective-permute-start.13 = (bf16[384,4096]{1,0:T(8,128)(2,1)}, bf16[384,4096]{1,0:T(8,128)(2,1)}, u32[]{:S(2)}, u32[]{:S(2)}) collective-permute-start(bf16[384,4096]{1,0:T(8,128)(2,1)} %pad_maximum_fusion.2.rest_0_.rest_4_), channel_id=1, source_target_pairs={{0,16},{8,24},{16,0},{24,8},{1,17},{9,25},{17,1},{25,9},{2,18},{10... | collective-permute-start | bytes 9437192 | tf_op jit(solution)/shard_map/ppermute | solution.py:43
  112.3 25.8 %collective-permute-start.12 = (bf16[384,1024]{1,0:T(8,128)(2,1)}, bf16[384,1024]{1,0:T(8,128)(2,1)}, u32[]{:S(2)}, u32[]{:S(2)}) collective-permute-start(bf16[384,1024]{1,0:T(8,128)(2,1)} %collective-permute-done.11), channel_id=1, source_target_pairs={{0,2},{2,0},{4,6},{6,4},{1,3},{3,1},{5,7},{7,5},{8,10},{10,8},{12,... | collective-permute-start | bytes 2359304 | tf_op jit(solution)/shard_map/ppermute | solution.py:1111
  136.5 18.3 %collective-permute-start.10 = (bf16[512,768]{1,0:T(8,128)(2,1)}, bf16[512,768]{1,0:T(8,128)(2,1)S(1)}, u32[]{:S(2)}, u32[]{:S(2)}) collective-permute-start(bf16[512,768]{1,0:T(8,128)(2,1)} %get-tuple-element.168.mo), channel_id=1, source_target_pairs={{0,1},{1,0},{2,3},{3,2},{4,5},{5,4},{6,7},{7,6},{8,9},{9,8},{10,11... | collective-permute-start | bytes 2359304 | tf_op jit(solution)/shard_map/ppermute | solution.py:1026
  138.2 43.5 %collective-permute-start.14 = (bf16[384,4096]{1,0:T(8,128)(2,1)}, bf16[384,4096]{1,0:T(8,128)(2,1)}, u32[]{:S(2)}, u32[]{:S(2)}) collective-permute-start(bf16[384,4096]{1,0:T(8,128)(2,1)} %pad_maximum_fusion.2.rest_0_.rest_4_), channel_id=1, source_target_pairs={{0,8},{8,0},{16,24},{24,16},{1,9},{9,1},{17,25},{25,17},{2,10},{10... | collective-permute-start | bytes 9437192 | tf_op jit(solution)/shard_map/ppermute | solution.py:1029
  168.9 125.1 %collective-permute-start.22 = (bf16[288,896]{1,0:T(8,128)(2,1)}, bf16[288,896]{1,0:T(8,128)(2,1)S(1)}, u32[]{:S(2)}, u32[]{:S(2)}) collective-permute-start(bf16[288,896]{1,0:T(8,128)(2,1)} %pad_maximum_fusion.9), channel_id=1, source_target_pairs={{4,0},{6,2},{5,1},{7,3},{12,8},{14,10},{13,9},{15,11},{20,16},{22,... | collective-permute-start | bytes 1548296 | tf_op jit(solution)/shard_map/ppermute | solution.py:76
  180.4 114.9 %collective-permute-start.21 = (bf16[512,896]{1,0:T(8,128)(2,1)}, bf16[512,896]{1,0:T(8,128)(2,1)S(1)}, u32[]{:S(2)}, u32[]{:S(2)}) collective-permute-start(bf16[512,896]{1,0:T(8,128)(2,1)} %pad_maximum_fusion.8), channel_id=1, source_target_pairs={{2,0},{4,2},{6,4},{3,1},{5,3},{7,5},{10,8},{12,10},{14,12},{11,9},... | collective-permute-start | bytes 2752520 | tf_op jit(solution)/shard_map/ppermute | solution.py:76
  212.6 21.3 %collective-permute-start.18 = (bf16[256,1664]{1,0:T(8,128)(2,1)S(1)}, bf16[256,1664]{1,0:T(8,128)(2,1)S(1)}, u32[]{:S(2)}, u32[]{:S(2)}) collective-permute-start(bf16[256,1664]{1,0:T(8,128)(2,1)S(1)} %copy-done.42), channel_id=1, source_target_pairs={{0,1},{1,0},{2,3},{3,2},{4,5},{5,4},{6,7},{7,6},{8,9},{9,8},{10,11... | collective-permute-start | bytes 2555912 | tf_op jit(solution)/shard_map/ppermute | solution.py:1026
  258.2 48.0 %collective-permute-start.23 = (bf16[512,896]{1,0:T(8,128)(2,1)}, bf16[512,896]{1,0:T(8,128)(2,1)}, u32[]{:S(2)}, u32[]{:S(2)}) collective-permute-start(bf16[512,896]{1,0:T(8,128)(2,1)} %get-tuple-element.215.d_ref.gd_ref), channel_id=1, source_target_pairs={{2,0},{4,2},{6,4},{3,1},{5,3},{7,5},{10,8},{12,10},{14,12},{11,9},... | collective-permute-start | bytes 2752520 | tf_op jit(solution)/shard_map/ppermute | solution.py:76
  260.5 45.7 %collective-permute-start.24 = (bf16[288,896]{1,0:T(8,128)(2,1)}, bf16[288,896]{1,0:T(8,128)(2,1)S(1)}, u32[]{:S(2)}, u32[]{:S(2)}) collective-permute-start(bf16[288,896]{1,0:T(8,128)(2,1)} %get-tuple-element.214), channel_id=1, source_target_pairs={{4,0},{6,2},{5,1},{7,3},{12,8},{14,10},{13,9},{15,11},{20,16},{22,... | collective-permute-start | bytes 1548296 | tf_op jit(solution)/shard_map/ppermute | solution.py:76
  261.9 91.4 %collective-permute-start.20 = (bf16[512,1664]{1,0:T(8,128)(2,1)S(1)}, bf16[512,1664]{1,0:T(8,128)(2,1)}, u32[]{:S(2)}, u32[]{:S(2)}) collective-permute-start(bf16[512,1664]{1,0:T(8,128)(2,1)S(1)} %copy-done.11), channel_id=1, source_target_pairs={{0,1},{1,0},{2,3},{3,2},{4,5},{5,4},{6,7},{7,6},{8,9},{9,8},{10,11... | collective-permute-start | bytes 5111816 | tf_op jit(solution)/shard_map/ppermute | solution.py:1026
  294.0 34.6 %collective-permute-start.25 = (f32[8,128]{1,0:T(8,128)S(1)}, f32[8,128]{1,0:T(8,128)S(1)}, u32[]{:S(2)}, u32[]{:S(2)}) collective-permute-start(f32[8,128]{1,0:T(8,128)S(1)} %copy-done.43), channel_id=1, source_target_pairs={{2,0},{4,2},{6,4},{3,1},{5,3},{7,5},{10,8},{12,10},{14,12},{11,9},... | collective-permute-start | bytes 12296 | tf_op jit(solution)/shard_map/ppermute | solution.py:76
  341.7 17.4 %collective-permute-start.26 = (bf16[2,256,768]{2,1,0:T(8,128)(2,1)}, bf16[2,256,768]{2,1,0:T(8,128)(2,1)}, u32[]{:S(2)}, u32[]{:S(2)}) collective-permute-start(bf16[2,256,768]{2,1,0:T(8,128)(2,1)} %get-tuple-element.240), channel_id=1, source_target_pairs={{0,1},{1,0},{2,3},{3,2},{4,5},{5,4},{6,7},{7,6},{8,9},{9,8},{10,11... | collective-permute-start | bytes 2359304 | tf_op jit(solution)/shard_map/ppermute | solution.py:1026
  364.1 37.7 %all-to-all-start = ((bf16[32,16,768]{2,1,0:T(8,128)(2,1)}), bf16[32,16,768]{2,1,0:T(8,128)(2,1)S(1)}, u32[]{:S(2)}, u32[]{:S(2)}) async-start(bf16[32,16,768]{2,1,0:T(8,128)(2,1)} %bitcast.55), calls=%async_computation | async-start | bytes 1572864 | tf_op jit(solution)/shard_map/all_to_all | solution.py:1215
  369.6 28.2 %collective-permute-start.28 = (bf16[256,1536]{1,0:T(8,128)(2,1)}, bf16[256,1536]{1,0:T(8,128)(2,1)S(1)}, u32[]{:S(2)}, u32[]{:S(2)}) collective-permute-start(bf16[256,1536]{1,0:T(8,128)(2,1)} %shard_map.280.own_ref), channel_id=1, source_target_pairs={{0,1},{1,0},{2,3},{3,2},{4,5},{5,4},{6,7},{7,6},{8,9},{9,8},{10,11... | collective-permute-start | bytes 2359304 | tf_op jit(solution)/shard_map/ppermute | solution.py:1026
  (51 other events, 649.3 us)
where the time goes:
time: 424 us; the launch traced here: 417 us
  Pallas kernels  184 us (43%)
  waiting for transfers between devices  80.6 us (19%)
  local copies, waits for them, and re-layouts  59.5 us (14%)
  starting transfers between devices  41.7 us (10%)
  other arithmetic  36 us (8%)
  matrix products  12.8 us (3%)
    pallas_call x18, Pallas kernels, call(): pl.pallas_call(kernel, out_shape=outs, grid_spec=pltpu.PrefetchScalarGrid...  184 us
    ppermute x8, waiting for transfers between devices, other(): return lax.ppermute(values, 'tp', [(0, 1), (1, 0)])  47.7 us
    ppermute x7, waiting for transfers between devices, shift(): return lax.ppermute(values, 'ctx', pairs)  20.8 us
    ppermute x7, starting transfers between devices, shift(): return lax.ppermute(values, 'ctx', pairs)  16.9 us
    unnamed x102, local copies, waits for them, and re-layouts  14 us
    ppermute x5, waiting for transfers between devices, far_blocks(): got = lax.ppermute(own, 'fsdp', [(i, i ^ bit) for i in range(size)])  12.1 us
    dot_general x9, matrix products, t_dot(): lax.dot_general(a, b, (((0,), (0,)), ((), ())), preferred_element_type=F32)  11.6 us
    ppermute x8, starting transfers between devices, other(): return lax.ppermute(values, 'tp', [(0, 1), (1, 0)])  9.79 us
  transfers between devices with their start and end apart: 30, of which 11 were waited for; matrix products, arithmetic and copies ran while one was open for 22% of the time, Pallas kernels for 42%

commit v1 on v0

--- a/solution.py
+++ b/solution.py
@@ -85,7 +85,7 @@
     return pl.BlockSpec(shape, index)
 
 
-def call(kernel, grid, ins, in_specs, outs, out_specs, scratch=(), prefetch=0, flops=0, nbytes=0, exps=0, aliases=None):
+def call(kernel, grid, ins, in_specs, outs, out_specs, scratch=(), prefetch=0, flops=0, nbytes=0, exps=0, aliases=None, cost=1):
     return pl.pallas_call(
         kernel,
         out_shape=outs,
@@ -96,7 +96,7 @@
             dimension_semantics=("arbitrary",) * len(grid), vmem_limit_bytes=56 * 2**20
         ),
         input_output_aliases=aliases or {},
-        cost_estimate=pl.CostEstimate(flops=1, bytes_accessed=1, transcendentals=0),
+        cost_estimate=pl.CostEstimate(flops=cost, bytes_accessed=1, transcendentals=0),
     )(*ins)
 
 
@@ -328,7 +328,7 @@
         ),
         (here(rows), shared(rows), shared(8)),
         [pltpu.VMEM((2, rows, LANES), BF)] * 2 + [pltpu.VMEM((2, rows, LANES), F32)],
-        prefetch=1,
+        prefetch=1, cost=3363750000
     )
 
 
@@ -387,7 +387,7 @@
         ],
         (jax.ShapeDtypeStruct(q.shape, F32), jax.ShapeDtypeStruct(q.shape, F32), jax.ShapeDtypeStruct((rows, LANES), F32)),
         (heads_spec(rows), heads_spec(rows), shared(rows)),
-        [pltpu.VMEM((2, rows, LANES), BF)] * 2 + [pltpu.VMEM((2, rows, LANES), F32)] * 2,
+        [pltpu.VMEM((2, rows, LANES), BF)] * 2 + [pltpu.VMEM((2, rows, LANES), F32)] * 2, cost=2294250000
     )
 
 
@@ -455,7 +455,7 @@
         (jax.ShapeDtypeStruct(dk.shape, BF), jax.ShapeDtypeStruct(dk.shape, BF), jax.ShapeDtypeStruct((rows, LANES), F32)),
         (heads_spec(rows), heads_spec(rows), shared(rows)),
         [pltpu.VMEM((2, rows, LANES), BF)] * 2 + [pltpu.VMEM((2, rows, LANES), F32)] * 2,
-        prefetch=1,
+        prefetch=1, cost=2932500000
     )
 
 
@@ -645,7 +645,7 @@
         kernel, (1,), ins,
         [rowed(x), rowed(mixed_own), rowed(mixed_far)] + weight_halves(w) + [whole(v) for v in ins[9:]],
         outs, tuple(rowed(o) for o in outs), prefetch=2, flops=4 * rows * width * mixed_own.shape[1],
-        nbytes=4 * width * mixed_own.shape[1] + 8 * rows * width,
+        nbytes=4 * width * mixed_own.shape[1] + 8 * rows * width, cost=1725000000
     )
 
 
@@ -720,7 +720,7 @@
         (out, out, out, *ends),
         (out_spec, out_spec, out_spec, *[whole(e) for e in ends]),
         [pltpu.VMEM(e.shape, F32) for e in sums] + [pltpu.VMEM((width, tile), BF)] * 3,
-        prefetch=1,
+        prefetch=1, cost=4657500000
     )
 
 
@@ -767,7 +767,7 @@
     in_specs += weight_halves(w) + [whole(a_own), whole(a_far)]
     return call(
         kernel, (1,), ins, in_specs, outs, tuple(whole(o) for o in outs), prefetch=1,
-        flops=4 * half * width * cols, nbytes=4 * width * cols + 16 * half * width,
+        flops=4 * half * width * cols, nbytes=4 * width * cols + 16 * half * width, cost=1311000000
     )
 
 
@@ -793,23 +793,28 @@
     return call(
         kernel, (1,), (rank, own, far, mixed), [whole(own), whole(far), whole(mixed)],
         tuple(outs), tuple(whole(o) for o in outs), prefetch=1,
-        flops=4 * half * cols, nbytes=16 * half * cols,
+        flops=4 * half * cols, nbytes=16 * half * cols, cost=672750000
     )
 
 
 def input_gradient(rank, grads, logits, seg_keys, seg_row, row_lanes, own_lanes, next_lanes, across, w, side_w, qkv_b, low_qkv, n_heads):
     rows, cols = grads[0].shape
-    depth = w[0].shape[0]
+    block = w[0].shape[0]
     half = rows // 2
     rank_r = qkv_b.shape[0]
     before = logits.shape[0] - rows
     steps = 3
-    chunk = 2 * depth // (2 * steps)
+    chunk = block // steps
 
     def kernel(
-        rank_ref, q_ref, k_ref, v_ref, logit_ref, seg_ref, seg_row_ref, r_ref, o_ref, n_ref, a_ref, w0, w1, s0, s1, b_ref,
-        lq_ref, far_ref, own_ref, low_ref, tq_ref, tk_ref, tv_ref, gl_ref,
+        rank_ref, q_ref, k_ref, v_ref, logit_ref, seg_ref, seg_row_ref, r_ref, o_ref, n_ref, a_ref, *refs,
     ):
+        pieces, sides, refs = refs[:4], refs[4:8], refs[8:]
+        (
+            b_ref, lq_ref, far_ref, own_ref, low_ref, tq_ref, tk_ref, tv_ref, gl_ref, sum_ref, joint,
+            side,
+        ) = refs
+
         @pl.when(pl.program_id(0) == 0)
         def _():
             lane = lane_ids(rows)
@@ -827,31 +832,34 @@
 
         mine = pl.ds(pl.multiple_of(rank_ref[0] * half, half), half)
         theirs = pl.ds(pl.multiple_of((1 - rank_ref[0]) * half, half), half)
-        for p, (w_ref, s_ref) in enumerate(((w0, s0), (w1, s1))):
-            def part(at):
-                value = dot_t(q_ref[at, :], w_ref[:, :cols]) + dot_t(k_ref[at, :], w_ref[:, cols : 2 * cols])
-                return value + dot_t(v_ref[at, :], w_ref[:, 2 * cols :]) + dot_t(gl_ref[at, :], s_ref[...])
-
-            far_ref[p] = part(theirs).astype(BF)
-            own_ref[p] = part(mine)
-
-    ins = (rank, *grads, logits, seg_keys, seg_row, row_lanes, own_lanes, next_lanes, across, w[0], w[1], side_w, side_w, qkv_b, low_qkv)
+        for k in range(4):
+            joint[k * chunk : (k + 1) * chunk, :] = pieces[k][...]
+            side[k * chunk : (k + 1) * chunk, :] = sides[k][...]
+        value = dot_t(q_ref[...], joint[:, :cols]) + dot_t(k_ref[...], joint[:, cols : 2 * cols])
+        sum_ref[...] = value + dot_t(v_ref[...], joint[:, 2 * cols :]) + dot_t(gl_ref[...], side[...])
+        for k in range(4):
+            at = slice(k * chunk, (k + 1) * chunk)
+            far_ref[k] = sum_ref[theirs, at].astype(BF)
+            own_ref[k] = sum_ref[mine, at]
+
+    ins = (rank, *grads, logits, seg_keys, seg_row, row_lanes, own_lanes, next_lanes, across, *w, *[side_w] * 4, qkv_b, low_qkv)
     at_own = lambda v: spec((rows, v.shape[1]), lambda i, *_: (before // rows, 0))
     in_specs = [whole(g) for g in grads] + [at_own(logits), at_own(seg_keys)]
     in_specs += [whole(v) for v in (seg_row, row_lanes, own_lanes, next_lanes, across)]
     n_col = w[0].shape[1]
-    in_specs += [spec((chunk, n_col), lambda i, *_: (i, 0))] * 2
-    in_specs += [spec((chunk, LANES), lambda i, *_: (i, 0)), spec((chunk, LANES), lambda i, *_: (i + steps, 0))]
+    in_specs += [spec((chunk, n_col), lambda i, *_: (i, 0))] * 4
+    in_specs += [spec((chunk, LANES), lambda i, *_, k=k: (i + k * steps, 0)) for k in range(4)]
     in_specs += [whole(qkv_b), whole(low_qkv)]
     outs = (
-        jax.ShapeDtypeStruct((2, half, depth), BF), jax.ShapeDtypeStruct((2, half, depth), F32),
+        jax.ShapeDtypeStruct((4, half, block), BF), jax.ShapeDtypeStruct((4, half, block), F32),
         jax.ShapeDtypeStruct((rows, rank_r), F32),
         *[jax.ShapeDtypeStruct((rank_r, cols), F32)] * 3,
     )
-    halves = spec((2, half, chunk), lambda i, *_: (0, 0, i))
-    return call(
-        kernel, (steps,), ins, in_specs, outs, (halves, halves, *[whole(o) for o in outs[2:]]), [pltpu.VMEM((rows, LANES), BF)],
-        prefetch=1, flops=2 * rows * 2 * depth * 3 * cols, nbytes=4 * depth * 3 * cols,
+    halves = spec((4, half, chunk), lambda i, *_: (0, 0, i))
+    return call(
+        kernel, (steps,), ins, in_specs, outs, (halves, halves, *[whole(o) for o in outs[2:]]), [pltpu.VMEM((rows, LANES), BF), pltpu.VMEM((rows, 4 * chunk), F32), pltpu.VMEM((4 * chunk, n_col), BF),
+         pltpu.VMEM((4 * chunk, LANES), BF)],
+        prefetch=1, cost=1932000000
     )
 
 
@@ -863,8 +871,7 @@
         blocks, scaled, product = [], [], 0.0
         for k in range(4):
             here = pl.ds(pl.multiple_of(offs_ref[k], LANES), block)
-            cols = slice(k % 2 * block, (k % 2 + 1) * block)
-            value = own_ref[k // 2][:, cols] + got_ref[k // 2][:, cols].astype(F32)
+            value = own_ref[k] + got_ref[k].astype(F32)
             value = value + dot_t(low_ref[...], a_ref[k * block : (k + 1) * block, :])
             blocks.append(x_ref[:, here].astype(F32))
             scaled.append(value * gain_ref[:, here])
@@ -881,7 +888,7 @@
     return call(
         kernel, (1,), (offs, rank, own, got, grad_low, a, x, gain, grad_hidden),
         [whole(own), whole(got), mine(grad_low), whole(a), mine(x), whole(gain), whole(grad_hidden)],
-        out, whole(out), prefetch=2, nbytes=20 * half * width,
+        out, whole(out), prefetch=2, nbytes=20 * half * width, cost=862500000
     )
 
 
@@ -899,7 +906,7 @@
 
     return call(
         kernel, (2,), (rank, own, far), [whole(own), whole(far)], jax.ShapeDtypeStruct((2 * half, width), F32),
-        spec((half, width), lambda i, *_: (i, 0)), prefetch=1, nbytes=16 * half * width,
+        spec((half, width), lambda i, *_: (i, 0)), prefetch=1, nbytes=16 * half * width, cost=517500000
     )
 
 
@@ -920,7 +927,7 @@
     last = spec((block, unit_cols), lambda i: (0, 0))
     return call(
         kernel, (rows // BLK,), (units, *down, down_a), [rowed(unit_cols), last, last, last, last, whole(down_a)],
-        jax.ShapeDtypeStruct((rows, width + LANES), BF), rowed(width + LANES), [pltpu.VMEM((BLK, LANES), F32)],
+        jax.ShapeDtypeStruct((rows, width + LANES), BF), rowed(width + LANES), [pltpu.VMEM((BLK, LANES), F32)], cost=1621500000
     )
 
 
@@ -942,7 +949,7 @@
     return call(
         kernel, (rows // BLK,), (offs, hidden, own, got, down_b),
         [rowed(hidden), rowed(own), rowed(got), whole(down_b)], out, rowed(out),
-        prefetch=1, nbytes=12 * rows * width,
+        prefetch=1, nbytes=12 * rows * width, cost=862500000
     )
 
 
@@ -975,30 +982,40 @@
 
     ins = (inv, rank, *xor_own, *xor_both, *halves, *out_a, *wide)
     out = jax.ShapeDtypeStruct((owners * rank_r, n), BF)
-    return call(kernel, (1,), ins, [whole(v) for v in ins[2:]], out, whole(out), prefetch=2)
-
-
-def spread_gradients(every, landed, n_adapters, rank_r, n_wide, n_small, unit_part, part):
-    n = landed.shape[1]
+    return call(kernel, (1,), ins, [whole(v) for v in ins[2:]], out, whole(out), prefetch=2, cost=552000000
+    )
+
+
+def spread_gradients(every, landed, n_adapters, rank_r, unit_part, part):
     senders = landed.shape[0] // (4 * rank_r)
-
-    def kernel(every_ref, x_ref, out_ref, swap_ref):
+    at = [0, unit_part, 2 * unit_part] + [3 * unit_part + i * part for i in range(9)]
+
+    def kernel(every_ref, x_ref, aq, bq, ao, bo, ag, bg, ad, bd):
         sums = []
         for f in range(4):
             total = 0.0
             for i in range(senders):
-                at = (f * senders + i) * rank_r
-                total = total + x_ref[at : at + rank_r, :].astype(F32)
+                row = (f * senders + i) * rank_r
+                total = total + x_ref[row : row + rank_r, :].astype(F32)
             sums.append(total)
         for a in range(n_adapters):
             total = 0.0
             for f in range(4):
                 total = total + jnp.where(every_ref[f] == a, sums[f], 0.0)
-            out_ref[a] = total
-            swap_ref[a] = total.T
-
-    outs = (jax.ShapeDtypeStruct((n_adapters, rank_r, n), F32), jax.ShapeDtypeStruct((n_adapters, n, rank_r), F32))
-    return call(kernel, (1,), (every, landed), [whole(landed)], outs, tuple(whole(o) for o in outs), prefetch=1)
+            cut = lambda i: total[:, at[i] : at[i + 1]]
+            for out, i in ((aq, 3), (ao, 10), (ag, 6), (ad, 2)):
+                out[a] = cut(i)
+            bo[a], bd[a] = cut(5), cut(4)
+            for j in range(3):
+                bq[a, j] = cut(7 + j)
+            for j in range(2):
+                bg[a, :, j, :] = cut(j)
+
+    shape = lambda *dims: jax.ShapeDtypeStruct((n_adapters, *dims), F32)
+    row = shape(rank_r, part)
+    outs = (row, shape(3, rank_r, part), row, row, row, shape(rank_r, 2, unit_part), shape(rank_r, unit_part), row)
+    return call(kernel, (1,), (every, landed), [whole(landed)], outs, tuple(whole(o) for o in outs), prefetch=1, cost=500250000
+    )
 
 
 def body(
@@ -1118,20 +1135,19 @@
     next_q1 = shift(sent_q1, -1, n_c)
     next_q2 = shift(sent_q2, -2, n_c)
 
-    gate_up_w = four((after(gate_up_own, mixed_own), after(gate_up_far[1], down_got))) if shared else four(gate_up_far)
     down_w = four((after(down_own, mixed_own), down_got)) if shared else four(down_far)
-    if shared:
-        mixed_far, gate_up_far = lax.optimization_barrier((mixed_far, gate_up_far))
     hidden, normed_ffn, low_ffn, low_out = out_projection(
         offs, rank, tok, mixed_own, mixed_far, out_w, out_a_own, out_a_far, out_b, gain_two, ffn_a
     )
+    gate_up_w = four((after(gate_up_own, mixed_own), after(gate_up_far[1], hidden))) if shared else four(gate_up_far)
     units, grad_gate, grad_up, far, own, own_low = feed_forward(
         rank, normed_ffn, low_ffn, cot, grad_low_down, gate_up_w, down_w, ffn_b, down_a
     )
     got = other(far)
     down_part = down_partial(after(units, far), down_w, down_a)
-    qkv_w = [jnp.concatenate([after(qkv_four[i], far), qkv_four[i + 1]], axis=0) for i in (0, 2)]
-    got, down_part, qkv_w = lax.optimization_barrier((got, down_part, qkv_w))
+    gate_g, up_g, units_g = after((grad_gate, grad_up, units), far)
+    tables_ffn = [t_dot(low_ffn, gate_g), t_dot(low_ffn, up_g), t_dot(grad_low_down, units_g)]
+    got, down_part, tables_ffn = lax.optimization_barrier((got, down_part, tables_ffn))
     grad_hidden, grad_hidden_b, grad_low_ffn, grad_low_out, gm_own, gm_send = middle(
         rank, own, got, own_low, hidden, cot, gain_two, ffn_a, out_b, out_w, out_a_own, out_a_far
     )
@@ -1178,9 +1194,8 @@
     table_out_a = [t_dot(grad_low_out, rows_of(mixed_own)), t_dot(grad_low_out, rows_of(mixed_far))]
     table_out_b = t_dot(rows_of(low_out), grad_hidden_b)
     table_ffn_a = t_dot(grad_low_ffn, rows_of(normed_ffn))
-    tables_ffn = [t_dot(low_ffn, grad_gate), t_dot(low_ffn, grad_up), t_dot(grad_low_down, units)]
-    highs, table_out_a, table_out_b, table_ffn_a, tables_ffn = lax.optimization_barrier(
-        (highs, table_out_a, table_out_b, table_ffn_a, tables_ffn)
+    highs, table_out_a, table_out_b, table_ffn_a = lax.optimization_barrier(
+        (highs, table_out_a, table_out_b, table_ffn_a)
     )
     grad_k, grad_v, next_lanes = attention_dkv_next(
         highs, keys, vals, next_q1, next_q2, next_d1, next_d2, gk_next, grad_k_own, grad_v_own, n_heads
@@ -1189,7 +1204,7 @@
 
     grads = (grad_q, grad_k, grad_v)
     far_in, own_in, part_low_qkv, *tables_b = input_gradient(
-        rank, grads, logits, seg_col, seg_row, row_lanes, own_lanes, next_lanes, across, qkv_w, side_w, qkv_b, low_qkv, n_heads
+        rank, grads, logits, seg_col, seg_row, row_lanes, own_lanes, next_lanes, across, qkv_four, side_w, qkv_b, low_qkv, n_heads
     )
     grad_low_qkv = (part_low_qkv + other(part_low_qkv)).astype(BF)
     got_in = other(far_in)
@@ -1212,16 +1227,12 @@
             jnp.stack(inv).astype(jnp.int32), rank, [table_qkv_a, table_down_b], [table_out_b, table_ffn_a], tables_b,
             table_out_a, tables_ffn, owners,
         )
-        landed = lax.all_to_all(after(packed, grad_tok), ("fsdp", "ctx", "tp"), 0, 0, tiled=True)
+        landed = lax.all_to_all(packed, ("fsdp", "ctx", "tp"), 0, 0, tiled=True)
         part, unit_part = width // owners, unit_cols * n_t // owners
-        by_row, by_column = spread_gradients(every, landed, a_qkv.shape[0], rank_r, 3, 8, unit_part, part)
-        at = [0, unit_part, 2 * unit_part] + [3 * unit_part + i * part for i in range(9)]
-        cut = lambda i: by_row[:, :, at[i] : at[i + 1]]
-        cut_t = lambda i: by_column[:, at[i] : at[i + 1]]
-        return (
-            block_output[None], grad_tokens[None], cut_t(3), jnp.stack([cut(7), cut(8), cut(9)], axis=2), cut_t(10),
-            cut(5), cut_t(6), jnp.stack([cut(0), cut(1)], axis=2), cut_t(2), cut(4),
-        )
+        done = spread_gradients(every, landed, a_qkv.shape[0], rank_r, unit_part, part)
+        done = [v.transpose(0, 2, 1) if i in (0, 2, 4, 6) else v for i, v in enumerate(done)]
+        done[1] = done[1].transpose(0, 2, 1, 3)
+        return (block_output[None], grad_tokens[None], *done)
     early, early_sizes = pack([
         by_tp(*table_out_a), natural(table_out_b), natural(table_ffn_a), *[place(t) for t in tables_ffn],
     ])

time: 424 us -> 406 us (0.958)
  local copies, waits for them, and re-layouts: 59.5 us -> 50.5 us
  other arithmetic: 36 us -> 28 us
  waiting for transfers between devices: 80.6 us -> 86.6 us
    ppermute x7, waiting for transfers between devices: 20.8 us -> 35.5 us  [shift(): return lax.ppermute(values, 'ctx', pairs)]
    ppermute x5, waiting for transfers between devices: 12.1 us -> 1.07 us  [far_blocks(): got = lax.ppermute(own, 'fsdp', [(i, i ^ bit) for i in range(size)])]
    concatenate x2 -> x0, other arithmetic: 8.02 us -> none  [body(): jnp.concatenate([after(qkv_four[i], far), qkv_four[i + 1]], axis=0)]
    ppermute x6, waiting for transfers between devices: 0.02 us -> 5.7 us  [four(): lax.ppermute(part, 'fsdp', [(i, i ^ 1) for i in range(n_f)])]
    slice x3 -> x0, local copies, waits for them, and re-layouts: 4.25 us -> none  [the longest x2 2.39 us: body(): cut_t = lambda i: by_column[:, at[i]:at[i + 1]]]
    unnamed x102 -> x90, local copies, waits for them, and re-layouts: 14 us -> 10.6 us
  transfers between devices with their start and end apart: 30 -> 30, of which waited for: 11 -> 12; matrix products, arithmetic and copies ran while one was open for 22% -> 21% of each run, Pallas kernels for 42% -> 44%
where the time goes in v1:
time: 406 us; the launch traced here: 402 us
  Pallas kernels  182 us (45%)
  waiting for transfers between devices  86.6 us (21%)
  local copies, waits for them, and re-layouts  50.5 us (12%)
  starting transfers between devices  40.3 us (10%)
  other arithmetic  28 us (7%)
  matrix products  13 us (3%)
    pallas_call x18, Pallas kernels, call(): pl.pallas_call(kernel, out_shape=outs, grid_spec=pltpu.PrefetchScalarGrid...  182 us
    ppermute x8, waiting for transfers between devices, other(): return lax.ppermute(values, 'tp', [(0, 1), (1, 0)])  44.3 us
    ppermute x7, waiting for transfers between devices, shift(): return lax.ppermute(values, 'ctx', pairs)  35.5 us
    ppermute x7, starting transfers between devices, shift(): return lax.ppermute(values, 'ctx', pairs)  16.9 us
    dot_general x9, matrix products, t_dot(): lax.dot_general(a, b, (((0,), (0,)), ((), ())), preferred_element_type=F32)  11.8 us
    unnamed x90, local copies, waits for them, and re-layouts  10.6 us
    ppermute x8, starting transfers between devices, other(): return lax.ppermute(values, 'tp', [(0, 1), (1, 0)])  8.93 us
  transfers between devices with their start and end apart: 30, of which 12 were waited for; matrix products, arithmetic and copies ran while one was open for 21% of the time, Pallas kernels for 44%

profile of v1, /device:TPU:0, one launch (start us, length us, event | category | flops | bytes accessed | tf_op | source)
XLA Modules:
  0.0 402.4 jit_solution(18237768294566313688)
XLA Ops:
  23.7 5.8 %fusion.21 = (bf16[384,1,2048]{2,1,0:T(2,128)(2,1)}, bf16[384,1,2048]{2,1,0:T(2,128)(2,1)}) fusion(bf16[384,2,2048]{2,1,0:T(2,128)(2,1)S(1)} %copy-done.8), kind=kLoop, calls=%fused_computation.102 | loop fusion | bytes 6291456 | tf_op jit(solution)/shard_map/slice | solution.py:1083
  41.6 4.8 %copy_bitcast_fusion = (bf16[384,2048]{1,0:T(8,128)(2,1)S(1)}, bf16[384,2048]{1,0:T(8,128)(2,1)S(1)}) fusion(bf16[384,1,2048]{2,1,0:T(2,128)(2,1)} %get-tuple-element.269, bf16[384,1,2048]{2,1,0:T(2,128)(2,1)} %get-tuple-element.268), kind=kLoop, calls=%fused_computation.5 | loop fusion | bytes 6291456 | tf_op jit(solution)/shard_map/squeeze | solution.py:1083
  56.3 5.5 %collective-permute-start.4 = (bf16[320,1536]{1,0:T(8,128)(2,1)}, bf16[320,1536]{1,0:T(8,128)(2,1)}, u32[]{:S(2)}, u32[]{:S(2)}) collective-permute-start(bf16[320,1536]{1,0:T(8,128)(2,1)} %slice.102), channel_id=1, source_target_pairs={{0,2},{2,4},{4,6},{1,3},{3,5},{5,7},{8,10},{10,12},{12,14},{9,11},... | collective-permute-start | bytes 2949128 | tf_op jit(solution)/shard_map/ppermute | solution.py:76
  72.7 9.2 %collective-permute-done.4.refs_2_ = bf16[320,1536]{1,0:T(8,128)(2,1)} collective-permute-done((bf16[320,1536]{1,0:T(8,128)(2,1)}, bf16[320,1536]{1,0:T(8,128)(2,1)}, u32[]{:S(2)}, u32[]{:S(2)}) %collective-permute-start.4) | collective-permute-done | bytes 983072 | tf_op jit(solution)/shard_map/ppermute | solution.py:76
  81.9 11.6 %shard_map.267 = (bf16[512,1536]{1,0:T(8,128)(2,1)}, bf16[512,16]{1,0:T(8,128)(2,1)}, bf16[512,768]{1,0:T(8,128)(2,1)}, bf16[1536,768]{1,0:T(8,128)(2,1)}, bf16[...) custom-call(s32[4]{0:T(128)} %pad_add_fusion.1.refs_0_.offs_ref, bf16[512,1536]{1,0:T(8,128)(2,1)} %bitcast.118, ...), custom_call_target="tpu_custom_call" | custom-call | flops 1 | bytes 1 | tf_op jit(solution)/shard_map/pallas_call | solution.py:89
  97.8 14.6 %shard_map.268 = (bf16[1536,768]{1,0:T(8,128)(2,1)}, bf16[1536,768]{1,0:T(8,128)(2,1)}, f32[1536,128]{1,0:T(8,128)}) custom-call(s32[4]{0:T(128)} %pad_add_fusion.1.refs_0_.offs_ref, bf16[544,1536]{1,0:T(8,128)(2,1)} %collective-permute-done.refs_1_, ...), custom_call_target="tpu_custom_call", output_to_operand_aliasing={{0}: (11, {}), {1}: (12, {}), {2}: (13, {})} | custom-call | flops 1 | bytes 1 | tf_op jit(solution)/shard_map/pallas_call | solution.py:89
  123.8 13.6 %shard_map.270 = (bf16[512,768]{1,0:T(8,128)(2,1)}, f32[512,768]{1,0:T(8,128)}, bf16[512,128]{1,0:T(8,128)(2,1)}, bf16[512,128]{1,0:T(8,128)(2,1)}) custom-call(s32[2]{0:T(128)} %fusion.18.lo_ref, bf16[512,768]{1,0:T(8,128)(2,1)} %get-tuple-element.157.q_ref, bf16[1536,768]{1,0:T(8,128)(2,1)} %get-tuple-element.161.k_ref, ...), custom_call_target="tpu_custom_call" | custom-call | flops 1 | bytes 1 | tf_op jit(solution)/shard_map/pallas_call | solution.py:89
  143.5 12.2 %collective-permute-done.10.mf = bf16[512,768]{1,0:T(8,128)(2,1)S(1)} collective-permute-done((bf16[512,768]{1,0:T(8,128)(2,1)}, bf16[512,768]{1,0:T(8,128)(2,1)S(1)}, u32[]{:S(2)}, u32[]{:S(2)}) %collective-permute-start.10) | collective-permute-done | bytes 786464 | tf_op jit(solution)/shard_map/ppermute | solution.py:1043
  156.7 10.4 %shard_map.271 = (f32[512,1536]{1,0:T(8,128)}, bf16[512,1536]{1,0:T(8,128)(2,1)}, bf16[512,16]{1,0:T(8,128)(2,1)}, bf16[512,16]{1,0:T(8,128)(2,1)}) custom-call(s32[4]{0:T(128)} %pad_add_fusion.1.refs_0_.offs_ref, s32[1]{0:T(128)} %bitcast.4.rank_ref, bf16[512,1536]{1,0:T(8,128)(2,1)} %bitcast.119, bf16[512,768]{1,0:T(8,128)(2,1)} %get-tuple-element.171.mo, ...), custom_call_target="tpu_custom_call" | custom-call | flops 1724999936 | bytes 1 | tf_op jit(solution)/shard_map/pallas_call | solution.py:89
  177.4 26.9 %shard_map.272 = (bf16[512,2048]{1,0:T(8,128)(2,1)}, bf16[512,2048]{1,0:T(8,128)(2,1)}, bf16[512,2048]{1,0:T(8,128)(2,1)}, bf16[256,1664]{1,0:T(8,128)(2,1)}, f32[256,1536]{1,0:T(8,128)}, /*index=5*/f32[256,128]{1,0:T(8,128)}) custom-call(s32[1]{0:T(128)} %bitcast.4.rank_ref, bf16[512,1536]{1,0:T(8,128)(2,1)} %get-tuple-element.186.x_ref, ...), custom_call_target="tpu_custom_call" | custom-call | flops 4657500160 | bytes 1 | tf_op jit(solution)/shard_map/pallas_call | solution.py:89
  205.0 9.5 %shard_map.273.own_ref = bf16[512,1664]{1,0:T(8,128)(2,1)} custom-call(bf16[512,2048]{1,0:T(8,128)(2,1)} %get-tuple-element.206.u_ref, bf16[384,2048]{1,0:T(8,128)(2,1)} %bitcast.122, bf16[384,2048]{1,0:T(8,128)(2,1)} %copy-done.7, bf16[384,2048]{1,0:T(8,128)(2,1)} %collective-permute-done.16.rest_10_.w2, ...), custom_call_target="tpu_custom_call" | custom-call | flops 1621500032 | bytes 1 | tf_op jit(solution)/shard_map/pallas_call | solution.py:89
  218.9 6.7 %collective-permute-done.18.got_ref = bf16[256,1664]{1,0:T(8,128)(2,1)S(1)} collective-permute-done((bf16[256,1664]{1,0:T(8,128)(2,1)}, bf16[256,1664]{1,0:T(8,128)(2,1)S(1)}, u32[]{:S(2)}, u32[]{:S(2)}) %collective-permute-start.18) | collective-permute-done | bytes 852000 | tf_op jit(solution)/shard_map/ppermute | solution.py:1043
  226.5 7.6 %shard_map.274 = (f32[256,1536]{1,0:T(8,128)}, bf16[256,1536]{1,0:T(8,128)(2,1)}, bf16[256,16]{1,0:T(8,128)(2,1)}, bf16[256,16]{1,0:T(8,128)(2,1)}, bf16[256,768]{1,0:T(8,128)(2,1)}, /*index=5*/bf16[256,768]{1,0:T(8,128)(2,1)}) custom-call(s32[1]{0:T(128)} %bitcast.4.rank_ref, f32[256,1536]{1,0:T(8,128)} %get-tuple-element.208.own_ref, ...), custom_call_target="tpu_custom_call" | custom-call | flops 1311000064 | bytes 1 | tf_op jit(solution)/shard_map/pallas_call | solution.py:89
  238.3 6.3 %collective-permute-done.19.far_ref = bf16[256,768]{1,0:T(8,128)(2,1)S(1)} collective-permute-done((bf16[256,768]{1,0:T(8,128)(2,1)}, bf16[256,768]{1,0:T(8,128)(2,1)S(1)}, u32[]{:S(2)}, u32[]{:S(2)}) %collective-permute-start.19) | collective-permute-done | bytes 393248 | tf_op jit(solution)/shard_map/ppermute | solution.py:1043
  253.9 15.3 %shard_map.276 = (bf16[512,768]{1,0:T(8,128)(2,1)}, f32[512,128]{1,0:T(8,128)}, f32[8,128]{1,0:T(8,128)}) custom-call(s32[2]{0:T(128)} %fusion.18.lo_ref, bf16[512,768]{1,0:T(8,128)(2,1)} %get-tuple-element.157.q_ref, bf16[1536,768]{1,0:T(8,128)(2,1)} %get-tuple-element.161.k_ref, bf16[1536,768]{1,0:T(8,128)(2,1)} %get-tuple-element.162.v_ref, ...), custom_call_target="tpu_custom_call" | custom-call | flops 3363749888 | bytes 1 | tf_op jit(solution)/shard_map/pallas_call | solution.py:89
  270.0 13.3 %shard_map.277 = (f32[512,768]{1,0:T(8,128)}, f32[512,768]{1,0:T(8,128)}, f32[512,128]{1,0:T(8,128)}) custom-call(bf16[1536,768]{1,0:T(8,128)(2,1)} %get-tuple-element.161.k_ref, bf16[1536,768]{1,0:T(8,128)(2,1)} %get-tuple-element.162.v_ref, bf16[512,768]{1,0:T(8,128)(2,1)} %get-tuple-element.157.q_ref, bf16[512,896]{1,0:T(8,128)(2,1)} %get-tuple-element.220.d_ref.gd_ref, ...), custom_call_target="tpu_custom_call" | custom-call | flops 2294249984 | bytes 1 | tf_op jit(solution)/shard_map/pallas_call | solution.py:89
  284.7 25.6 %collective-permute-done.24.d2_ref.gd2_ref = bf16[288,896]{1,0:T(8,128)(2,1)S(1)} collective-permute-done((bf16[288,896]{1,0:T(8,128)(2,1)}, bf16[288,896]{1,0:T(8,128)(2,1)S(1)}, u32[]{:S(2)}, u32[]{:S(2)}) %collective-permute-start.24) | collective-permute-done | bytes 516128 | tf_op jit(solution)/shard_map/ppermute | solution.py:76
  312.3 20.4 %shard_map.278 = (bf16[512,768]{1,0:T(8,128)(2,1)}, bf16[512,768]{1,0:T(8,128)(2,1)}, f32[512,128]{1,0:T(8,128)}) custom-call(s32[2]{0:T(128)} %fusion.19.hi_ref, bf16[1536,768]{1,0:T(8,128)(2,1)} %get-tuple-element.161.k_ref, bf16[1536,768]{1,0:T(8,128)(2,1)} %get-tuple-element.162.v_ref, bf16[512,896]{1,0:T(8,128)(2,1)} %copy-done.13, ...), custom_call_target="tpu_custom_call" | custom-call | flops 2932499968 | bytes 1 | tf_op jit(solution)/shard_map/pallas_call | solution.py:89
  333.3 11.2 %shard_map.279 = (bf16[4,256,384]{2,1,0:T(8,128)(2,1)}, f32[4,256,384]{2,1,0:T(8,128)}, f32[512,16]{1,0:T(8,128)}, f32[16,768]{1,0:T(8,128)}, f32[16,768]{1,0:T(8,128)}, /*index=5*/f32[16,768]{1,0:T(8,128)}) custom-call(s32[1]{0:T(128)} %bitcast.4.rank_ref, bf16[512,768]{1,0:T(8,128)(2,1)} %get-tuple-element.216.q_ref, ...), custom_call_target="tpu_custom_call" | custom-call | flops 1932000000 | bytes 1 | tf_op jit(solution)/shard_map/pallas_call | solution.py:89
  346.8 6.3 %collective-permute-done.27 = f32[512,16]{1,0:T(8,128)} collective-permute-done((f32[512,16]{1,0:T(8,128)}, f32[512,16]{1,0:T(8,128)}, u32[]{:S(2)}, u32[]{:S(2)}) %collective-permute-start.27) | collective-permute-done | bytes 32800 | tf_op jit(solution)/shard_map/ppermute | solution.py:1043
  361.9 5.0 %all-to-all-start = ((bf16[32,16,768]{2,1,0:T(8,128)(2,1)}), bf16[32,16,768]{2,1,0:T(8,128)(2,1)}, u32[]{:S(2)}, u32[]{:S(2)}) async-start(bf16[32,16,768]{2,1,0:T(8,128)(2,1)} %bitcast.137), calls=%async_computation | async-start | bytes 1572864 | tf_op jit(solution)/shard_map/all_to_all | solution.py:1230
  370.0 5.0 %shard_map.280.own_ref = bf16[256,1536]{1,0:T(8,128)(2,1)} custom-call(s32[4]{0:T(128)} %pad_add_fusion.1.refs_0_.offs_ref, s32[1]{0:T(128)} %bitcast.4.rank_ref, f32[4,256,384]{2,1,0:T(8,128)} %get-tuple-element.240.own_ref, bf16[4,256,384]{2,1,0:T(8,128)(2,1)} %collective-permute-done.26.got_ref, bf16[512,16]{1,0:T(8,128)(2,1)} %copy-done.24, ...), custom_call_target="tpu_custom_call" | custom-call | flops 862499968 | bytes 1 | tf_op jit(solution)/shard_map/pallas_call | solution.py:89
  380.5 4.9 %shard_map.281 = bf16[512,1536]{1,0:T(8,128)(2,1)} custom-call(s32[4]{0:T(128)} %pad_add_fusion.1.refs_0_.offs_ref, f32[512,1536]{1,0:T(8,128)} %get-tuple-element.185.h_ref, bf16[512,1664]{1,0:T(8,128)(2,1)} %shard_map.273.own_ref, bf16[512,1664]{1,0:T(8,128)(2,1)} %collective-permute-done.20.got_ref, bf16[16,1536]{1,0:T(8,128)(2,1)} %pad_maximum_fusion.12.b_ref), custom_call_target="tpu_custom_call" | custom-call | flops 862499968 | bytes 1 | tf_op jit(solution)/shard_map/pallas_call | solution.py:89
  385.3 9.7 %collective-permute-done.28.far_ref = bf16[256,1536]{1,0:T(8,128)(2,1)S(1)} collective-permute-done((bf16[256,1536]{1,0:T(8,128)(2,1)}, bf16[256,1536]{1,0:T(8,128)(2,1)S(1)}, u32[]{:S(2)}, u32[]{:S(2)}) %collective-permute-start.28) | collective-permute-done | bytes 786464 | tf_op jit(solution)/shard_map/ppermute | solution.py:1043
  (231 shorter events, 138.7 us)
Async XLA Ops:
  0.7 48.4 %collective-permute-start.3 = (bf16[768,384]{1,0:T(8,128)(2,1)}, bf16[768,384]{1,0:T(8,128)(2,1)}, u32[]{:S(2)}, u32[]{:S(2)}) collective-permute-start(bf16[768,384]{1,0:T(8,128)(2,1)} %param.28), channel_id=1, source_target_pairs={{0,1},{1,0},{2,3},{3,2},{4,5},{5,4},{6,7},{7,6},{8,9},{9,8},{10,11... | collective-permute-start | bytes 1769480 | tf_op jit(solution)/shard_map/ppermute | solution.py:1043
  6.6 44.2 %collective-permute-start.1 = (bf16[384,2304]{1,0:T(8,128)(2,1)}, bf16[384,2304]{1,0:T(8,128)(2,1)}, u32[]{:S(2)}, u32[]{:S(2)}) collective-permute-start(bf16[384,2304]{1,0:T(8,128)(2,1)} %pad_maximum_fusion.1.refs_3_.refs_4_.refs_0_), channel_id=1, source_target_pairs={{0,16},{8,24},{16,0},{24,8},{1,17},{9,25},{17,1},{25,9},{2,18},{10... | collective-permute-start | bytes 5308424 | tf_op jit(solution)/shard_map/ppermute | solution.py:43
  8.8 41.4 %collective-permute-start.2 = (bf16[384,13]{0,1:T(8,128)(2,1)S(1)}, bf16[384,13]{0,1:T(8,128)(2,1)}, u32[]{:S(2)}, u32[]{:S(2)}) collective-permute-start(bf16[384,13]{0,1:T(8,128)(2,1)S(1)} %concatenate.68), channel_id=1, source_target_pairs={{0,16},{8,24},{16,0},{24,8},{1,17},{9,25},{17,1},{25,9},{2,18},{10... | collective-permute-start | bytes 29960 | tf_op jit(solution)/shard_map/ppermute | solution.py:43
  12.2 38.7 %collective-permute-start = (bf16[544,1536]{1,0:T(8,128)(2,1)}, bf16[544,1536]{1,0:T(8,128)(2,1)}, u32[]{:S(2)}, u32[]{:S(2)}) collective-permute-start(bf16[544,1536]{1,0:T(8,128)(2,1)} %pad_maximum_fusion.2), channel_id=1, source_target_pairs={{0,2},{2,4},{4,6},{1,3},{3,5},{5,7},{8,10},{10,12},{12,14},{9,11},... | collective-permute-start | bytes 5013512 | tf_op jit(solution)/shard_map/ppermute | solution.py:76
  50.9 31.0 %collective-permute-start.5 = (bf16[384,2304]{1,0:T(8,128)(2,1)}, bf16[384,2304]{1,0:T(8,128)(2,1)}, u32[]{:S(2)}, u32[]{:S(2)}) collective-permute-start(bf16[384,2304]{1,0:T(8,128)(2,1)} %pad_maximum_fusion.1.refs_3_.refs_4_.refs_0_), channel_id=1, source_target_pairs={{0,8},{8,0},{16,24},{24,16},{1,9},{9,1},{17,25},{25,17},{2,10},{10... | collective-permute-start | bytes 5308424 | tf_op jit(solution)/shard_map/ppermute | solution.py:1046
  50.9 31.0 %collective-permute-start.6 = (bf16[384,2304]{1,0:T(8,128)(2,1)}, bf16[384,2304]{1,0:T(8,128)(2,1)}, u32[]{:S(2)}, u32[]{:S(2)}) collective-permute-start(bf16[384,2304]{1,0:T(8,128)(2,1)} %collective-permute-done.1.refs_4_.refs_5_.refs_1_), channel_id=1, source_target_pairs={{0,8},{8,0},{16,24},{24,16},{1,9},{9,1},{17,25},{25,17},{2,10},{10... | collective-permute-start | bytes 5308424 | tf_op jit(solution)/shard_map/ppermute | solution.py:1046
  51.4 42.2 %collective-permute-start.8 = (bf16[1536,384]{1,0:T(8,128)(2,1)S(1)}, bf16[1536,384]{1,0:T(8,128)(2,1)}, u32[]{:S(2)}, u32[]{:S(2)}) collective-permute-start(bf16[1536,384]{1,0:T(8,128)(2,1)S(1)} %pad_maximum_fusion.5), channel_id=1, source_target_pairs={{0,16},{8,24},{16,0},{24,8},{1,17},{9,25},{17,1},{25,9},{2,18},{10... | collective-permute-start | bytes 3538952 | tf_op jit(solution)/shard_map/ppermute | solution.py:43
  56.3 25.6 %collective-permute-start.4 = (bf16[320,1536]{1,0:T(8,128)(2,1)}, bf16[320,1536]{1,0:T(8,128)(2,1)}, u32[]{:S(2)}, u32[]{:S(2)}) collective-permute-start(bf16[320,1536]{1,0:T(8,128)(2,1)} %slice.102), channel_id=1, source_target_pairs={{0,2},{2,4},{4,6},{1,3},{3,5},{5,7},{8,10},{10,12},{12,14},{9,11},... | collective-permute-start | bytes 2949128 | tf_op jit(solution)/shard_map/ppermute | solution.py:76
  66.9 29.3 %collective-permute-start.11 = (bf16[384,1024]{1,0:T(8,128)(2,1)}, bf16[384,1024]{1,0:T(8,128)(2,1)}, u32[]{:S(2)}, u32[]{:S(2)}) collective-permute-start(bf16[384,1024]{1,0:T(8,128)(2,1)} %dynamic-slice_bitcast_fusion), channel_id=1, source_target_pairs={{0,16},{8,24},{16,0},{24,8},{1,17},{9,25},{17,1},{25,9},{2,18},{10... | collective-permute-start | bytes 2359304 | tf_op jit(solution)/shard_map/ppermute | solution.py:43
  95.1 24.5 %collective-permute-start.9 = (bf16[1536,768]{1,0:T(8,128)(2,1)S(1)}, bf16[1536,768]{1,0:T(8,128)(2,1)}, u32[]{:S(2)}, u32[]{:S(2)}) collective-permute-start(bf16[1536,768]{1,0:T(8,128)(2,1)S(1)} %constant_dynamic-update-slice_fusion.3.wo0.wf0), channel_id=1, source_target_pairs={{0,8},{8,0},{16,24},{24,16},{1,9},{9,1},{17,25},{25,17},{2,10},{10... | collective-permute-start | bytes 7077896 | tf_op jit(solution)/shard_map/ppermute | solution.py:52
  96.2 70.8 %collective-permute-start.13 = (bf16[384,4096]{1,0:T(8,128)(2,1)}, bf16[384,4096]{1,0:T(8,128)(2,1)}, u32[]{:S(2)}, u32[]{:S(2)}) collective-permute-start(bf16[384,4096]{1,0:T(8,128)(2,1)} %pad_maximum_fusion.rest_0_.rest_4_), channel_id=1, source_target_pairs={{0,16},{8,24},{16,0},{24,8},{1,17},{9,25},{17,1},{25,9},{2,18},{10... | collective-permute-start | bytes 9437192 | tf_op jit(solution)/shard_map/ppermute | solution.py:43
  112.4 26.7 %collective-permute-start.12 = (bf16[384,1024]{1,0:T(8,128)(2,1)}, bf16[384,1024]{1,0:T(8,128)(2,1)}, u32[]{:S(2)}, u32[]{:S(2)}) collective-permute-start(bf16[384,1024]{1,0:T(8,128)(2,1)} %collective-permute-done.11), channel_id=1, source_target_pairs={{0,2},{2,0},{4,6},{6,4},{1,3},{3,1},{5,7},{7,5},{8,10},{10,8},{12,... | collective-permute-start | bytes 2359304 | tf_op jit(solution)/shard_map/ppermute | solution.py:1128
  137.5 18.3 %collective-permute-start.10 = (bf16[512,768]{1,0:T(8,128)(2,1)}, bf16[512,768]{1,0:T(8,128)(2,1)S(1)}, u32[]{:S(2)}, u32[]{:S(2)}) collective-permute-start(bf16[512,768]{1,0:T(8,128)(2,1)} %get-tuple-element.171.mo), channel_id=1, source_target_pairs={{0,1},{1,0},{2,3},{3,2},{4,5},{5,4},{6,7},{7,6},{8,9},{9,8},{10,11... | collective-permute-start | bytes 2359304 | tf_op jit(solution)/shard_map/ppermute | solution.py:1043
  139.1 38.3 %collective-permute-start.14 = (bf16[384,4096]{1,0:T(8,128)(2,1)}, bf16[384,4096]{1,0:T(8,128)(2,1)}, u32[]{:S(2)}, u32[]{:S(2)}) collective-permute-start(bf16[384,4096]{1,0:T(8,128)(2,1)} %pad_maximum_fusion.rest_0_.rest_4_), channel_id=1, source_target_pairs={{0,8},{8,0},{16,24},{24,16},{1,9},{9,1},{17,25},{25,17},{2,10},{10... | collective-permute-start | bytes 9437192 | tf_op jit(solution)/shard_map/ppermute | solution.py:1046
  169.1 114.2 %collective-permute-start.22 = (bf16[288,896]{1,0:T(8,128)(2,1)}, bf16[288,896]{1,0:T(8,128)(2,1)S(1)}, u32[]{:S(2)}, u32[]{:S(2)}) collective-permute-start(bf16[288,896]{1,0:T(8,128)(2,1)} %pad_maximum_fusion.7), channel_id=1, source_target_pairs={{4,0},{6,2},{5,1},{7,3},{12,8},{14,10},{13,9},{15,11},{20,16},{22,... | collective-permute-start | bytes 1548296 | tf_op jit(solution)/shard_map/ppermute | solution.py:76
  174.8 109.9 %collective-permute-start.21 = (bf16[512,896]{1,0:T(8,128)(2,1)}, bf16[512,896]{1,0:T(8,128)(2,1)S(1)}, u32[]{:S(2)}, u32[]{:S(2)}) collective-permute-start(bf16[512,896]{1,0:T(8,128)(2,1)} %pad_maximum_fusion.6), channel_id=1, source_target_pairs={{2,0},{4,2},{6,4},{3,1},{5,3},{7,5},{10,8},{12,10},{14,12},{11,9},... | collective-permute-start | bytes 2752520 | tf_op jit(solution)/shard_map/ppermute | solution.py:76
  204.3 21.3 %collective-permute-start.18 = (bf16[256,1664]{1,0:T(8,128)(2,1)}, bf16[256,1664]{1,0:T(8,128)(2,1)S(1)}, u32[]{:S(2)}, u32[]{:S(2)}) collective-permute-start(bf16[256,1664]{1,0:T(8,128)(2,1)} %get-tuple-element.199), channel_id=1, source_target_pairs={{0,1},{1,0},{2,3},{3,2},{4,5},{5,4},{6,7},{7,6},{8,9},{9,8},{10,11... | collective-permute-start | bytes 2555912 | tf_op jit(solution)/shard_map/ppermute | solution.py:1043
  249.3 61.0 %collective-permute-start.23 = (bf16[512,896]{1,0:T(8,128)(2,1)}, bf16[512,896]{1,0:T(8,128)(2,1)}, u32[]{:S(2)}, u32[]{:S(2)}) collective-permute-start(bf16[512,896]{1,0:T(8,128)(2,1)} %get-tuple-element.220.d_ref.gd_ref), channel_id=1, source_target_pairs={{2,0},{4,2},{6,4},{3,1},{5,3},{7,5},{10,8},{12,10},{14,12},{11,9},... | collective-permute-start | bytes 2752520 | tf_op jit(solution)/shard_map/ppermute | solution.py:76
  252.3 57.9 %collective-permute-start.24 = (bf16[288,896]{1,0:T(8,128)(2,1)}, bf16[288,896]{1,0:T(8,128)(2,1)S(1)}, u32[]{:S(2)}, u32[]{:S(2)}) collective-permute-start(bf16[288,896]{1,0:T(8,128)(2,1)} %get-tuple-element.219), channel_id=1, source_target_pairs={{4,0},{6,2},{5,1},{7,3},{12,8},{14,10},{13,9},{15,11},{20,16},{22,... | collective-permute-start | bytes 1548296 | tf_op jit(solution)/shard_map/ppermute | solution.py:76
  269.3 87.3 %collective-permute-start.20 = (bf16[512,1664]{1,0:T(8,128)(2,1)S(1)}, bf16[512,1664]{1,0:T(8,128)(2,1)}, u32[]{:S(2)}, u32[]{:S(2)}) collective-permute-start(bf16[512,1664]{1,0:T(8,128)(2,1)S(1)} %copy-done.10), channel_id=1, source_target_pairs={{0,1},{1,0},{2,3},{3,2},{4,5},{5,4},{6,7},{7,6},{8,9},{9,8},{10,11... | collective-permute-start | bytes 5111816 | tf_op jit(solution)/shard_map/ppermute | solution.py:1043
  283.3 49.4 %collective-permute-start.25 = (f32[8,128]{1,0:T(8,128)S(1)}, f32[8,128]{1,0:T(8,128)S(1)}, u32[]{:S(2)}, u32[]{:S(2)}) collective-permute-start(f32[8,128]{1,0:T(8,128)S(1)} %copy-done.40), channel_id=1, source_target_pairs={{2,0},{4,2},{6,4},{3,1},{5,3},{7,5},{10,8},{12,10},{14,12},{11,9},... | collective-permute-start | bytes 12296 | tf_op jit(solution)/shard_map/ppermute | solution.py:76
  345.5 24.5 %collective-permute-start.26 = (bf16[4,256,384]{2,1,0:T(8,128)(2,1)}, bf16[4,256,384]{2,1,0:T(8,128)(2,1)}, u32[]{:S(2)}, u32[]{:S(2)}) collective-permute-start(bf16[4,256,384]{2,1,0:T(8,128)(2,1)} %get-tuple-element.241), channel_id=1, source_target_pairs={{0,1},{1,0},{2,3},{3,2},{4,5},{5,4},{6,7},{7,6},{8,9},{9,8},{10,11... | collective-permute-start | bytes 2359304 | tf_op jit(solution)/shard_map/ppermute | solution.py:1043
  361.9 37.4 %all-to-all-start = ((bf16[32,16,768]{2,1,0:T(8,128)(2,1)}), bf16[32,16,768]{2,1,0:T(8,128)(2,1)}, u32[]{:S(2)}, u32[]{:S(2)}) async-start(bf16[32,16,768]{2,1,0:T(8,128)(2,1)} %bitcast.137), calls=%async_computation | async-start | bytes 1572864 | tf_op jit(solution)/shard_map/all_to_all | solution.py:1230
  374.9 20.1 %collective-permute-start.28 = (bf16[256,1536]{1,0:T(8,128)(2,1)}, bf16[256,1536]{1,0:T(8,128)(2,1)S(1)}, u32[]{:S(2)}, u32[]{:S(2)}) collective-permute-start(bf16[256,1536]{1,0:T(8,128)(2,1)} %shard_map.280.own_ref), channel_id=1, source_target_pairs={{0,1},{1,0},{2,3},{3,2},{4,5},{5,4},{6,7},{7,6},{8,9},{9,8},{10,11... | collective-permute-start | bytes 2359304 | tf_op jit(solution)/shard_map/ppermute | solution.py:1043
  (48 other events, 535.4 us)

commit v2 on v1

--- a/solution.py
+++ b/solution.py
@@ -825,8 +825,8 @@
             total = total + a_ref[:1, :]
             value = jnp.where(lane < n_heads, total * jax.nn.sigmoid(-logit_ref[...]), 0.0)
             gl_ref[...] = value.astype(BF)
-            low = dot_t(q_ref[...], b_ref[:, :cols]) + dot_t(k_ref[...], b_ref[:, cols : 2 * cols])
-            low_ref[...] = low + dot_t(v_ref[...], b_ref[:, 2 * cols :])
+            low = dot_t(b_ref[:, :cols], q_ref[...]) + dot_t(b_ref[:, cols : 2 * cols], k_ref[...])
+            low_ref[...] = low + dot_t(b_ref[:, 2 * cols :], v_ref[...])
             for out, grad in ((tq_ref, q_ref), (tk_ref, k_ref), (tv_ref, v_ref)):
                 out[...] = t_dot(lq_ref[...], grad[...])
 
@@ -852,7 +852,7 @@
     in_specs += [whole(qkv_b), whole(low_qkv)]
     outs = (
         jax.ShapeDtypeStruct((4, half, block), BF), jax.ShapeDtypeStruct((4, half, block), F32),
-        jax.ShapeDtypeStruct((rows, rank_r), F32),
+        jax.ShapeDtypeStruct((rank_r, rows), F32),
         *[jax.ShapeDtypeStruct((rank_r, cols), F32)] * 3,
     )
     halves = spec((4, half, chunk), lambda i, *_: (0, 0, i))
@@ -872,7 +872,9 @@
         for k in range(4):
             here = pl.ds(pl.multiple_of(offs_ref[k], LANES), block)
             value = own_ref[k] + got_ref[k].astype(F32)
-            value = value + dot_t(low_ref[...], a_ref[k * block : (k + 1) * block, :])
+            value = value + lax.dot_general(
+                low_ref[...], a_ref[k * block : (k + 1) * block, :], (((0,), (1,)), ((), ())), preferred_element_type=F32
+            )
             blocks.append(x_ref[:, here].astype(F32))
             scaled.append(value * gain_ref[:, here])
             product = product + jnp.sum(blocks[k] * scaled[k], axis=1, keepdims=True)
@@ -887,7 +889,7 @@
     out = jax.ShapeDtypeStruct((half, width), BF)
     return call(
         kernel, (1,), (offs, rank, own, got, grad_low, a, x, gain, grad_hidden),
-        [whole(own), whole(got), mine(grad_low), whole(a), mine(x), whole(gain), whole(grad_hidden)],
+        [whole(own), whole(got), spec((grad_low.shape[0], half), lambda i, o, r: (0, r[0])), whole(a), mine(x), whole(gain), whole(grad_hidden)],
         out, whole(out), prefetch=2, nbytes=20 * half * width, cost=862500000
     )
 
@@ -1214,12 +1216,8 @@
     grad_tok = token_gradient(offs, rank, own_in, got_in, grad_low_qkv, qkv_a, tok, gain_one, grad_hidden)
     tok_far = other(grad_tok)
     block_output = block_result(offs, hidden, down_part, after(down_other, grad_tok), down_b)
-    grad_tokens = both_halves(rank, grad_tok, tok_far)
-    if not direct:
-        block_output = from_xor(block_output, 1, n_f, f_rank)
-        grad_tokens = from_xor(grad_tokens, 1, n_f, f_rank)
-
-    table_qkv_a, table_down_b = t_dot(grad_low_qkv, normed), t_dot(low_down, cot)
+
+    table_qkv_a, table_down_b = dot(grad_low_qkv, normed), t_dot(low_down, cot)
     if direct:
         bits = n_f.bit_length() - 1
         inv = [sum((((f_rank ^ i) >> j) & 1) << (bits - 1 - j) for j in range(bits)) * block for i in range(n_f)]
@@ -1232,7 +1230,10 @@
         done = spread_gradients(every, landed, a_qkv.shape[0], rank_r, unit_part, part)
         done = [v.transpose(0, 2, 1) if i in (0, 2, 4, 6) else v for i, v in enumerate(done)]
         done[1] = done[1].transpose(0, 2, 1, 3)
+        grad_tokens = both_halves(rank, grad_tok, after(tok_far, done[0]))
         return (block_output[None], grad_tokens[None], *done)
+    block_output = from_xor(block_output, 1, n_f, f_rank)
+    grad_tokens = from_xor(both_halves(rank, grad_tok, tok_far), 1, n_f, f_rank)
     early, early_sizes = pack([
         by_tp(*table_out_a), natural(table_out_b), natural(table_ffn_a), *[place(t) for t in tables_ffn],
     ])

time: 406 us -> 391 us (0.963)
  waiting for transfers between devices: 86.6 us -> 70.4 us
  Pallas kernels: 182 us -> 177 us
    ppermute x8, waiting for transfers between devices: 44.3 us -> 31 us  [other(): return lax.ppermute(values, 'tp', [(0, 1), (1, 0)])]
    ppermute x7, waiting for transfers between devices: 35.5 us -> 27 us  [shift(): return lax.ppermute(values, 'ctx', pairs)]
    all_to_all x1, waiting for transfers between devices: 0.01 us -> 5.65 us  [body(): landed = lax.all_to_all(packed, ('fsdp', 'ctx', 'tp'), 0, 0, tiled=True)]
    pallas_call x18, Pallas kernels: 182 us -> 177 us  [call(): pl.pallas_call(kernel, out_shape=outs, grid_spec=pltpu.PrefetchScalarGrid...]
    dot_general x9 -> x8, matrix products: 11.8 us -> 9.36 us  [t_dot(): lax.dot_general(a, b, (((0,), (0,)), ((), ())), preferred_element_type=F32)]
    unnamed x90 -> x94, local copies, waits for them, and re-layouts: 10.6 us -> 11.6 us
  transfers between devices with their start and end apart: 30 -> 30, of which waited for: 12 -> 12; matrix products, arithmetic and copies ran while one was open for 21% -> 22% of each run, Pallas kernels for 44% -> 45%
where the time goes in v2:
time: 391 us; the launch traced here: 384 us
  Pallas kernels  177 us (45%)
  waiting for transfers between devices  70.4 us (18%)
  local copies, waits for them, and re-layouts  52.1 us (13%)
  starting transfers between devices  41.3 us (11%)
  other arithmetic  27.6 us (7%)
  matrix products  12.9 us (3%)
    pallas_call x18, Pallas kernels, call(): pl.pallas_call(kernel, out_shape=outs, grid_spec=pltpu.PrefetchScalarGrid...  177 us
    ppermute x8, waiting for transfers between devices, other(): return lax.ppermute(values, 'tp', [(0, 1), (1, 0)])  31 us
    ppermute x7, waiting for transfers between devices, shift(): return lax.ppermute(values, 'ctx', pairs)  27 us
    ppermute x7, starting transfers between devices, shift(): return lax.ppermute(values, 'ctx', pairs)  16.9 us
    unnamed x94, local copies, waits for them, and re-layouts  11.6 us
    ppermute x8, starting transfers between devices, other(): return lax.ppermute(values, 'tp', [(0, 1), (1, 0)])  9.73 us
    dot_general x8, matrix products, t_dot(): lax.dot_general(a, b, (((0,), (0,)), ((), ())), preferred_element_type=F32)  9.36 us
  transfers between devices with their start and end apart: 30, of which 12 were waited for; matrix products, arithmetic and copies ran while one was open for 22% of the time, Pallas kernels for 45%

profile of v2, /device:TPU:0, one launch (start us, length us, event | category | flops | bytes accessed | tf_op | source)
XLA Modules:
  0.0 383.7 jit_solution(4495578497466790990)
XLA Ops:
  12.1 4.7 %collective-permute-start = (bf16[544,1536]{1,0:T(8,128)(2,1)}, bf16[544,1536]{1,0:T(8,128)(2,1)}, u32[]{:S(2)}, u32[]{:S(2)}) collective-permute-start(bf16[544,1536]{1,0:T(8,128)(2,1)} %pad_maximum_fusion.2), channel_id=1, source_target_pairs={{0,2},{2,4},{4,6},{1,3},{3,5},{5,7},{8,10},{10,12},{12,14},{9,11},... | collective-permute-start | bytes 5013512 | tf_op jit(solution)/shard_map/ppermute | solution.py:76
  23.7 5.8 %fusion.21 = (bf16[384,1,2048]{2,1,0:T(2,128)(2,1)}, bf16[384,1,2048]{2,1,0:T(2,128)(2,1)}) fusion(bf16[384,2,2048]{2,1,0:T(2,128)(2,1)S(1)} %copy-done.8), kind=kLoop, calls=%fused_computation.102 | loop fusion | bytes 6291456 | tf_op jit(solution)/shard_map/slice | solution.py:1085
  41.6 4.8 %copy_bitcast_fusion = (bf16[384,2048]{1,0:T(8,128)(2,1)S(1)}, bf16[384,2048]{1,0:T(8,128)(2,1)S(1)}) fusion(bf16[384,1,2048]{2,1,0:T(2,128)(2,1)} %get-tuple-element.271, bf16[384,1,2048]{2,1,0:T(2,128)(2,1)} %get-tuple-element.270), kind=kLoop, calls=%fused_computation.5 | loop fusion | bytes 6291456 | tf_op jit(solution)/shard_map/squeeze | solution.py:1085
  56.3 5.5 %collective-permute-start.4 = (bf16[320,1536]{1,0:T(8,128)(2,1)}, bf16[320,1536]{1,0:T(8,128)(2,1)}, u32[]{:S(2)}, u32[]{:S(2)}) collective-permute-start(bf16[320,1536]{1,0:T(8,128)(2,1)} %slice.102), channel_id=1, source_target_pairs={{0,2},{2,4},{4,6},{1,3},{3,5},{5,7},{8,10},{10,12},{12,14},{9,11},... | collective-permute-start | bytes 2949128 | tf_op jit(solution)/shard_map/ppermute | solution.py:76
  72.7 9.2 %collective-permute-done.4.refs_2_ = bf16[320,1536]{1,0:T(8,128)(2,1)} collective-permute-done((bf16[320,1536]{1,0:T(8,128)(2,1)}, bf16[320,1536]{1,0:T(8,128)(2,1)}, u32[]{:S(2)}, u32[]{:S(2)}) %collective-permute-start.4) | collective-permute-done | bytes 983072 | tf_op jit(solution)/shard_map/ppermute | solution.py:76
  81.9 11.6 %shard_map.267 = (bf16[512,1536]{1,0:T(8,128)(2,1)}, bf16[512,16]{1,0:T(8,128)(2,1)}, bf16[512,768]{1,0:T(8,128)(2,1)}, bf16[1536,768]{1,0:T(8,128)(2,1)}, bf16[...) custom-call(s32[4]{0:T(128)} %pad_add_fusion.1.refs_0_.offs_ref, bf16[512,1536]{1,0:T(8,128)(2,1)} %bitcast.118, ...), custom_call_target="tpu_custom_call" | custom-call | flops 1 | bytes 1 | tf_op jit(solution)/shard_map/pallas_call | solution.py:89
  97.8 14.6 %shard_map.268 = (bf16[1536,768]{1,0:T(8,128)(2,1)}, bf16[1536,768]{1,0:T(8,128)(2,1)}, f32[1536,128]{1,0:T(8,128)}) custom-call(s32[4]{0:T(128)} %pad_add_fusion.1.refs_0_.offs_ref, bf16[544,1536]{1,0:T(8,128)(2,1)} %collective-permute-done.refs_1_, ...), custom_call_target="tpu_custom_call", output_to_operand_aliasing={{0}: (11, {}), {1}: (12, {}), {2}: (13, {})} | custom-call | flops 1 | bytes 1 | tf_op jit(solution)/shard_map/pallas_call | solution.py:89
  123.7 13.6 %shard_map.270 = (bf16[512,768]{1,0:T(8,128)(2,1)}, f32[512,768]{1,0:T(8,128)}, bf16[512,128]{1,0:T(8,128)(2,1)}, bf16[512,128]{1,0:T(8,128)(2,1)}) custom-call(s32[2]{0:T(128)} %fusion.18.lo_ref, bf16[512,768]{1,0:T(8,128)(2,1)} %get-tuple-element.158.q_ref, bf16[1536,768]{1,0:T(8,128)(2,1)} %get-tuple-element.162.k_ref, ...), custom_call_target="tpu_custom_call" | custom-call | flops 1 | bytes 1 | tf_op jit(solution)/shard_map/pallas_call | solution.py:89
  143.4 12.3 %collective-permute-done.10.mf = bf16[512,768]{1,0:T(8,128)(2,1)S(1)} collective-permute-done((bf16[512,768]{1,0:T(8,128)(2,1)}, bf16[512,768]{1,0:T(8,128)(2,1)S(1)}, u32[]{:S(2)}, u32[]{:S(2)}) %collective-permute-start.10) | collective-permute-done | bytes 786464 | tf_op jit(solution)/shard_map/ppermute | solution.py:1045
  156.6 10.3 %shard_map.271 = (f32[512,1536]{1,0:T(8,128)}, bf16[512,1536]{1,0:T(8,128)(2,1)}, bf16[512,16]{1,0:T(8,128)(2,1)}, bf16[512,16]{1,0:T(8,128)(2,1)}) custom-call(s32[4]{0:T(128)} %pad_add_fusion.1.refs_0_.offs_ref, s32[1]{0:T(128)} %bitcast.4.rank_ref, bf16[512,1536]{1,0:T(8,128)(2,1)} %bitcast.119, bf16[512,768]{1,0:T(8,128)(2,1)} %get-tuple-element.172.mo, ...), custom_call_target="tpu_custom_call" | custom-call | flops 1724999936 | bytes 1 | tf_op jit(solution)/shard_map/pallas_call | solution.py:89
  177.3 26.9 %shard_map.272 = (bf16[512,2048]{1,0:T(8,128)(2,1)}, bf16[512,2048]{1,0:T(8,128)(2,1)}, bf16[512,2048]{1,0:T(8,128)(2,1)}, bf16[256,1664]{1,0:T(8,128)(2,1)}, f32[256,1536]{1,0:T(8,128)}, /*index=5*/f32[256,128]{1,0:T(8,128)}) custom-call(s32[1]{0:T(128)} %bitcast.4.rank_ref, bf16[512,1536]{1,0:T(8,128)(2,1)} %get-tuple-element.187.x_ref, ...), custom_call_target="tpu_custom_call" | custom-call | flops 4657500160 | bytes 1 | tf_op jit(solution)/shard_map/pallas_call | solution.py:89
  205.0 9.5 %shard_map.273.own_ref = bf16[512,1664]{1,0:T(8,128)(2,1)} custom-call(bf16[512,2048]{1,0:T(8,128)(2,1)} %get-tuple-element.207.u_ref, bf16[384,2048]{1,0:T(8,128)(2,1)} %bitcast.122, bf16[384,2048]{1,0:T(8,128)(2,1)} %copy-done.7, bf16[384,2048]{1,0:T(8,128)(2,1)} %collective-permute-done.16.rest_10_.w2, ...), custom_call_target="tpu_custom_call" | custom-call | flops 1621500032 | bytes 1 | tf_op jit(solution)/shard_map/pallas_call | solution.py:89
  218.8 6.7 %collective-permute-done.18.got_ref = bf16[256,1664]{1,0:T(8,128)(2,1)S(1)} collective-permute-done((bf16[256,1664]{1,0:T(8,128)(2,1)}, bf16[256,1664]{1,0:T(8,128)(2,1)S(1)}, u32[]{:S(2)}, u32[]{:S(2)}) %collective-permute-start.18) | collective-permute-done | bytes 852000 | tf_op jit(solution)/shard_map/ppermute | solution.py:1045
  226.4 7.6 %shard_map.274 = (f32[256,1536]{1,0:T(8,128)}, bf16[256,1536]{1,0:T(8,128)(2,1)}, bf16[256,16]{1,0:T(8,128)(2,1)}, bf16[256,16]{1,0:T(8,128)(2,1)}, bf16[256,768]{1,0:T(8,128)(2,1)}, /*index=5*/bf16[256,768]{1,0:T(8,128)(2,1)}) custom-call(s32[1]{0:T(128)} %bitcast.4.rank_ref, f32[256,1536]{1,0:T(8,128)} %get-tuple-element.209.own_ref, ...), custom_call_target="tpu_custom_call" | custom-call | flops 1311000064 | bytes 1 | tf_op jit(solution)/shard_map/pallas_call | solution.py:89
  238.3 6.3 %collective-permute-done.19.far_ref = bf16[256,768]{1,0:T(8,128)(2,1)S(1)} collective-permute-done((bf16[256,768]{1,0:T(8,128)(2,1)}, bf16[256,768]{1,0:T(8,128)(2,1)S(1)}, u32[]{:S(2)}, u32[]{:S(2)}) %collective-permute-start.19) | collective-permute-done | bytes 393248 | tf_op jit(solution)/shard_map/ppermute | solution.py:1045
  253.9 15.3 %shard_map.276 = (bf16[512,768]{1,0:T(8,128)(2,1)}, f32[512,128]{1,0:T(8,128)}, f32[8,128]{1,0:T(8,128)}) custom-call(s32[2]{0:T(128)} %fusion.18.lo_ref, bf16[512,768]{1,0:T(8,128)(2,1)} %get-tuple-element.158.q_ref, bf16[1536,768]{1,0:T(8,128)(2,1)} %get-tuple-element.162.k_ref, bf16[1536,768]{1,0:T(8,128)(2,1)} %get-tuple-element.163.v_ref, ...), custom_call_target="tpu_custom_call" | custom-call | flops 3363749888 | bytes 1 | tf_op jit(solution)/shard_map/pallas_call | solution.py:89
  269.9 13.3 %shard_map.277 = (f32[512,768]{1,0:T(8,128)}, f32[512,768]{1,0:T(8,128)}, f32[512,128]{1,0:T(8,128)}) custom-call(bf16[1536,768]{1,0:T(8,128)(2,1)} %get-tuple-element.162.k_ref, bf16[1536,768]{1,0:T(8,128)(2,1)} %get-tuple-element.163.v_ref, bf16[512,768]{1,0:T(8,128)(2,1)} %get-tuple-element.158.q_ref, bf16[512,896]{1,0:T(8,128)(2,1)} %get-tuple-element.221.d_ref.gd_ref, ...), custom_call_target="tpu_custom_call" | custom-call | flops 2294249984 | bytes 1 | tf_op jit(solution)/shard_map/pallas_call | solution.py:89
  284.6 17.1 %collective-permute-done.24.d2_ref.gd2_ref = bf16[288,896]{1,0:T(8,128)(2,1)S(1)} collective-permute-done((bf16[288,896]{1,0:T(8,128)(2,1)}, bf16[288,896]{1,0:T(8,128)(2,1)S(1)}, u32[]{:S(2)}, u32[]{:S(2)}) %collective-permute-start.24) | collective-permute-done | bytes 516128 | tf_op jit(solution)/shard_map/ppermute | solution.py:76
  303.7 15.9 %shard_map.278 = (bf16[512,768]{1,0:T(8,128)(2,1)}, bf16[512,768]{1,0:T(8,128)(2,1)}, f32[512,128]{1,0:T(8,128)}) custom-call(s32[2]{0:T(128)} %fusion.19.hi_ref, bf16[1536,768]{1,0:T(8,128)(2,1)} %get-tuple-element.162.k_ref, bf16[1536,768]{1,0:T(8,128)(2,1)} %get-tuple-element.163.v_ref, bf16[512,896]{1,0:T(8,128)(2,1)} %copy-done.13, ...), custom_call_target="tpu_custom_call" | custom-call | flops 2932499968 | bytes 1 | tf_op jit(solution)/shard_map/pallas_call | solution.py:89
  320.3 11.1 %shard_map.279 = (bf16[4,256,384]{2,1,0:T(8,128)(2,1)}, f32[4,256,384]{2,1,0:T(8,128)}, f32[16,512]{1,0:T(8,128)}, f32[16,768]{1,0:T(8,128)}, f32[16,768]{1,0:T(8,128)}, /*index=5*/f32[16,768]{1,0:T(8,128)}) custom-call(s32[1]{0:T(128)} %bitcast.4.rank_ref, bf16[512,768]{1,0:T(8,128)(2,1)} %get-tuple-element.217.q_ref, ...), custom_call_target="tpu_custom_call" | custom-call | flops 1932000000 | bytes 1 | tf_op jit(solution)/shard_map/pallas_call | solution.py:89
  344.5 5.2 %all-to-all-start = ((bf16[32,16,768]{2,1,0:T(8,128)(2,1)}), bf16[32,16,768]{2,1,0:T(8,128)(2,1)S(1)}, u32[]{:S(2)}, u32[]{:S(2)}) async-start(bf16[32,16,768]{2,1,0:T(8,128)(2,1)} %bitcast.137), calls=%async_computation | async-start | bytes 1572864 | tf_op jit(solution)/shard_map/all_to_all | solution.py:1228
  349.8 5.0 %shard_map.280.own_ref = bf16[256,1536]{1,0:T(8,128)(2,1)} custom-call(s32[4]{0:T(128)} %pad_add_fusion.1.refs_0_.offs_ref, s32[1]{0:T(128)} %bitcast.4.rank_ref, f32[4,256,384]{2,1,0:T(8,128)} %get-tuple-element.241.own_ref, bf16[4,256,384]{2,1,0:T(8,128)(2,1)} %collective-permute-done.26.got_ref, bf16[16,512]{1,0:T(8,128)(2,1)} %copy-done.33, ...), custom_call_target="tpu_custom_call" | custom-call | flops 862499968 | bytes 1 | tf_op jit(solution)/shard_map/pallas_call | solution.py:89
  361.2 4.9 %shard_map.281 = bf16[512,1536]{1,0:T(8,128)(2,1)} custom-call(s32[4]{0:T(128)} %pad_add_fusion.1.refs_0_.offs_ref, f32[512,1536]{1,0:T(8,128)} %get-tuple-element.186.h_ref, bf16[512,1664]{1,0:T(8,128)(2,1)} %shard_map.273.own_ref, bf16[512,1664]{1,0:T(8,128)(2,1)} %collective-permute-done.20.got_ref, bf16[16,1536]{1,0:T(8,128)(2,1)} %pad_maximum_fusion.12.b_ref), custom_call_target="tpu_custom_call" | custom-call | flops 862499968 | bytes 1 | tf_op jit(solution)/shard_map/pallas_call | solution.py:89
  366.1 5.7 %all-to-all-done = bf16[32,16,768]{2,1,0:T(8,128)(2,1)S(1)} async-done(((bf16[32,16,768]{2,1,0:T(8,128)(2,1)}), bf16[32,16,768]{2,1,0:T(8,128)(2,1)S(1)}, u32[]{:S(2)}, u32[]{:S(2)}) %all-to-all-start) | async-done | bytes 786464 | tf_op jit(solution)/shard_map/all_to_all | solution.py:1228
  (235 shorter events, 138.4 us)
Async XLA Ops:
  0.7 48.3 %collective-permute-start.3 = (bf16[768,384]{1,0:T(8,128)(2,1)}, bf16[768,384]{1,0:T(8,128)(2,1)}, u32[]{:S(2)}, u32[]{:S(2)}) collective-permute-start(bf16[768,384]{1,0:T(8,128)(2,1)} %param.28), channel_id=1, source_target_pairs={{0,1},{1,0},{2,3},{3,2},{4,5},{5,4},{6,7},{7,6},{8,9},{9,8},{10,11... | collective-permute-start | bytes 1769480 | tf_op jit(solution)/shard_map/ppermute | solution.py:1045
  6.6 44.2 %collective-permute-start.1 = (bf16[384,2304]{1,0:T(8,128)(2,1)}, bf16[384,2304]{1,0:T(8,128)(2,1)}, u32[]{:S(2)}, u32[]{:S(2)}) collective-permute-start(bf16[384,2304]{1,0:T(8,128)(2,1)} %pad_maximum_fusion.1.refs_3_.refs_4_.refs_0_), channel_id=1, source_target_pairs={{0,16},{8,24},{16,0},{24,8},{1,17},{9,25},{17,1},{25,9},{2,18},{10... | collective-permute-start | bytes 5308424 | tf_op jit(solution)/shard_map/ppermute | solution.py:43
  8.8 41.4 %collective-permute-start.2 = (bf16[384,13]{0,1:T(8,128)(2,1)S(1)}, bf16[384,13]{0,1:T(8,128)(2,1)}, u32[]{:S(2)}, u32[]{:S(2)}) collective-permute-start(bf16[384,13]{0,1:T(8,128)(2,1)S(1)} %concatenate.68), channel_id=1, source_target_pairs={{0,16},{8,24},{16,0},{24,8},{1,17},{9,25},{17,1},{25,9},{2,18},{10... | collective-permute-start | bytes 29960 | tf_op jit(solution)/shard_map/ppermute | solution.py:43
  12.1 38.7 %collective-permute-start = (bf16[544,1536]{1,0:T(8,128)(2,1)}, bf16[544,1536]{1,0:T(8,128)(2,1)}, u32[]{:S(2)}, u32[]{:S(2)}) collective-permute-start(bf16[544,1536]{1,0:T(8,128)(2,1)} %pad_maximum_fusion.2), channel_id=1, source_target_pairs={{0,2},{2,4},{4,6},{1,3},{3,5},{5,7},{8,10},{10,12},{12,14},{9,11},... | collective-permute-start | bytes 5013512 | tf_op jit(solution)/shard_map/ppermute | solution.py:76
  50.8 31.0 %collective-permute-start.5 = (bf16[384,2304]{1,0:T(8,128)(2,1)}, bf16[384,2304]{1,0:T(8,128)(2,1)}, u32[]{:S(2)}, u32[]{:S(2)}) collective-permute-start(bf16[384,2304]{1,0:T(8,128)(2,1)} %pad_maximum_fusion.1.refs_3_.refs_4_.refs_0_), channel_id=1, source_target_pairs={{0,8},{8,0},{16,24},{24,16},{1,9},{9,1},{17,25},{25,17},{2,10},{10... | collective-permute-start | bytes 5308424 | tf_op jit(solution)/shard_map/ppermute | solution.py:1048
  50.8 31.0 %collective-permute-start.6 = (bf16[384,2304]{1,0:T(8,128)(2,1)}, bf16[384,2304]{1,0:T(8,128)(2,1)}, u32[]{:S(2)}, u32[]{:S(2)}) collective-permute-start(bf16[384,2304]{1,0:T(8,128)(2,1)} %collective-permute-done.1.refs_4_.refs_5_.refs_1_), channel_id=1, source_target_pairs={{0,8},{8,0},{16,24},{24,16},{1,9},{9,1},{17,25},{25,17},{2,10},{10... | collective-permute-start | bytes 5308424 | tf_op jit(solution)/shard_map/ppermute | solution.py:1048
  51.4 42.2 %collective-permute-start.8 = (bf16[1536,384]{1,0:T(8,128)(2,1)S(1)}, bf16[1536,384]{1,0:T(8,128)(2,1)}, u32[]{:S(2)}, u32[]{:S(2)}) collective-permute-start(bf16[1536,384]{1,0:T(8,128)(2,1)S(1)} %pad_maximum_fusion.5), channel_id=1, source_target_pairs={{0,16},{8,24},{16,0},{24,8},{1,17},{9,25},{17,1},{25,9},{2,18},{10... | collective-permute-start | bytes 3538952 | tf_op jit(solution)/shard_map/ppermute | solution.py:43
  56.3 25.6 %collective-permute-start.4 = (bf16[320,1536]{1,0:T(8,128)(2,1)}, bf16[320,1536]{1,0:T(8,128)(2,1)}, u32[]{:S(2)}, u32[]{:S(2)}) collective-permute-start(bf16[320,1536]{1,0:T(8,128)(2,1)} %slice.102), channel_id=1, source_target_pairs={{0,2},{2,4},{4,6},{1,3},{3,5},{5,7},{8,10},{10,12},{12,14},{9,11},... | collective-permute-start | bytes 2949128 | tf_op jit(solution)/shard_map/ppermute | solution.py:76
  66.9 29.3 %collective-permute-start.11 = (bf16[384,1024]{1,0:T(8,128)(2,1)}, bf16[384,1024]{1,0:T(8,128)(2,1)}, u32[]{:S(2)}, u32[]{:S(2)}) collective-permute-start(bf16[384,1024]{1,0:T(8,128)(2,1)} %dynamic-slice_bitcast_fusion), channel_id=1, source_target_pairs={{0,16},{8,24},{16,0},{24,8},{1,17},{9,25},{17,1},{25,9},{2,18},{10... | collective-permute-start | bytes 2359304 | tf_op jit(solution)/shard_map/ppermute | solution.py:43
  95.1 24.5 %collective-permute-start.9 = (bf16[1536,768]{1,0:T(8,128)(2,1)S(1)}, bf16[1536,768]{1,0:T(8,128)(2,1)}, u32[]{:S(2)}, u32[]{:S(2)}) collective-permute-start(bf16[1536,768]{1,0:T(8,128)(2,1)S(1)} %constant_dynamic-update-slice_fusion.3.wo0.wf0), channel_id=1, source_target_pairs={{0,8},{8,0},{16,24},{24,16},{1,9},{9,1},{17,25},{25,17},{2,10},{10... | collective-permute-start | bytes 7077896 | tf_op jit(solution)/shard_map/ppermute | solution.py:52
  96.2 70.8 %collective-permute-start.13 = (bf16[384,4096]{1,0:T(8,128)(2,1)}, bf16[384,4096]{1,0:T(8,128)(2,1)}, u32[]{:S(2)}, u32[]{:S(2)}) collective-permute-start(bf16[384,4096]{1,0:T(8,128)(2,1)} %pad_maximum_fusion.rest_0_.rest_4_), channel_id=1, source_target_pairs={{0,16},{8,24},{16,0},{24,8},{1,17},{9,25},{17,1},{25,9},{2,18},{10... | collective-permute-start | bytes 9437192 | tf_op jit(solution)/shard_map/ppermute | solution.py:43
  112.4 26.6 %collective-permute-start.12 = (bf16[384,1024]{1,0:T(8,128)(2,1)}, bf16[384,1024]{1,0:T(8,128)(2,1)}, u32[]{:S(2)}, u32[]{:S(2)}) collective-permute-start(bf16[384,1024]{1,0:T(8,128)(2,1)} %collective-permute-done.11), channel_id=1, source_target_pairs={{0,2},{2,0},{4,6},{6,4},{1,3},{3,1},{5,7},{7,5},{8,10},{10,8},{12,... | collective-permute-start | bytes 2359304 | tf_op jit(solution)/shard_map/ppermute | solution.py:1130
  137.4 18.3 %collective-permute-start.10 = (bf16[512,768]{1,0:T(8,128)(2,1)}, bf16[512,768]{1,0:T(8,128)(2,1)S(1)}, u32[]{:S(2)}, u32[]{:S(2)}) collective-permute-start(bf16[512,768]{1,0:T(8,128)(2,1)} %get-tuple-element.172.mo), channel_id=1, source_target_pairs={{0,1},{1,0},{2,3},{3,2},{4,5},{5,4},{6,7},{7,6},{8,9},{9,8},{10,11... | collective-permute-start | bytes 2359304 | tf_op jit(solution)/shard_map/ppermute | solution.py:1045
  139.0 38.3 %collective-permute-start.14 = (bf16[384,4096]{1,0:T(8,128)(2,1)}, bf16[384,4096]{1,0:T(8,128)(2,1)}, u32[]{:S(2)}, u32[]{:S(2)}) collective-permute-start(bf16[384,4096]{1,0:T(8,128)(2,1)} %pad_maximum_fusion.rest_0_.rest_4_), channel_id=1, source_target_pairs={{0,8},{8,0},{16,24},{24,16},{1,9},{9,1},{17,25},{25,17},{2,10},{10... | collective-permute-start | bytes 9437192 | tf_op jit(solution)/shard_map/ppermute | solution.py:1048
  169.1 114.2 %collective-permute-start.22 = (bf16[288,896]{1,0:T(8,128)(2,1)}, bf16[288,896]{1,0:T(8,128)(2,1)S(1)}, u32[]{:S(2)}, u32[]{:S(2)}) collective-permute-start(bf16[288,896]{1,0:T(8,128)(2,1)} %pad_maximum_fusion.7), channel_id=1, source_target_pairs={{4,0},{6,2},{5,1},{7,3},{12,8},{14,10},{13,9},{15,11},{20,16},{22,... | collective-permute-start | bytes 1548296 | tf_op jit(solution)/shard_map/ppermute | solution.py:76
  174.7 109.9 %collective-permute-start.21 = (bf16[512,896]{1,0:T(8,128)(2,1)}, bf16[512,896]{1,0:T(8,128)(2,1)S(1)}, u32[]{:S(2)}, u32[]{:S(2)}) collective-permute-start(bf16[512,896]{1,0:T(8,128)(2,1)} %pad_maximum_fusion.6), channel_id=1, source_target_pairs={{2,0},{4,2},{6,4},{3,1},{5,3},{7,5},{10,8},{12,10},{14,12},{11,9},... | collective-permute-start | bytes 2752520 | tf_op jit(solution)/shard_map/ppermute | solution.py:76
  204.2 21.3 %collective-permute-start.18 = (bf16[256,1664]{1,0:T(8,128)(2,1)}, bf16[256,1664]{1,0:T(8,128)(2,1)S(1)}, u32[]{:S(2)}, u32[]{:S(2)}) collective-permute-start(bf16[256,1664]{1,0:T(8,128)(2,1)} %get-tuple-element.200), channel_id=1, source_target_pairs={{0,1},{1,0},{2,3},{3,2},{4,5},{5,4},{6,7},{7,6},{8,9},{9,8},{10,11... | collective-permute-start | bytes 2555912 | tf_op jit(solution)/shard_map/ppermute | solution.py:1045
  249.2 52.4 %collective-permute-start.23 = (bf16[512,896]{1,0:T(8,128)(2,1)}, bf16[512,896]{1,0:T(8,128)(2,1)}, u32[]{:S(2)}, u32[]{:S(2)}) collective-permute-start(bf16[512,896]{1,0:T(8,128)(2,1)} %get-tuple-element.221.d_ref.gd_ref), channel_id=1, source_target_pairs={{2,0},{4,2},{6,4},{3,1},{5,3},{7,5},{10,8},{12,10},{14,12},{11,9},... | collective-permute-start | bytes 2752520 | tf_op jit(solution)/shard_map/ppermute | solution.py:76
  252.3 49.4 %collective-permute-start.24 = (bf16[288,896]{1,0:T(8,128)(2,1)}, bf16[288,896]{1,0:T(8,128)(2,1)S(1)}, u32[]{:S(2)}, u32[]{:S(2)}) collective-permute-start(bf16[288,896]{1,0:T(8,128)(2,1)} %get-tuple-element.220), channel_id=1, source_target_pairs={{4,0},{6,2},{5,1},{7,3},{12,8},{14,10},{13,9},{15,11},{20,16},{22,... | collective-permute-start | bytes 1548296 | tf_op jit(solution)/shard_map/ppermute | solution.py:76
  269.2 70.1 %collective-permute-start.20 = (bf16[512,1664]{1,0:T(8,128)(2,1)S(1)}, bf16[512,1664]{1,0:T(8,128)(2,1)}, u32[]{:S(2)}, u32[]{:S(2)}) collective-permute-start(bf16[512,1664]{1,0:T(8,128)(2,1)S(1)} %copy-done.10), channel_id=1, source_target_pairs={{0,1},{1,0},{2,3},{3,2},{4,5},{5,4},{6,7},{7,6},{8,9},{9,8},{10,11... | collective-permute-start | bytes 5111816 | tf_op jit(solution)/shard_map/ppermute | solution.py:1045
  283.3 36.4 %collective-permute-start.25 = (f32[8,128]{1,0:T(8,128)S(1)}, f32[8,128]{1,0:T(8,128)S(1)}, u32[]{:S(2)}, u32[]{:S(2)}) collective-permute-start(f32[8,128]{1,0:T(8,128)S(1)} %copy-done.42), channel_id=1, source_target_pairs={{2,0},{4,2},{6,4},{3,1},{5,3},{7,5},{10,8},{12,10},{14,12},{11,9},... | collective-permute-start | bytes 12296 | tf_op jit(solution)/shard_map/ppermute | solution.py:76
  332.9 16.9 %collective-permute-start.26 = (bf16[4,256,384]{2,1,0:T(8,128)(2,1)}, bf16[4,256,384]{2,1,0:T(8,128)(2,1)}, u32[]{:S(2)}, u32[]{:S(2)}) collective-permute-start(bf16[4,256,384]{2,1,0:T(8,128)(2,1)} %get-tuple-element.242), channel_id=1, source_target_pairs={{0,1},{1,0},{2,3},{3,2},{4,5},{5,4},{6,7},{7,6},{8,9},{9,8},{10,11... | collective-permute-start | bytes 2359304 | tf_op jit(solution)/shard_map/ppermute | solution.py:1045
  344.5 27.2 %all-to-all-start = ((bf16[32,16,768]{2,1,0:T(8,128)(2,1)}), bf16[32,16,768]{2,1,0:T(8,128)(2,1)S(1)}, u32[]{:S(2)}, u32[]{:S(2)}) async-start(bf16[32,16,768]{2,1,0:T(8,128)(2,1)} %bitcast.137), calls=%async_computation | async-start | bytes 1572864 | tf_op jit(solution)/shard_map/all_to_all | solution.py:1228
  354.8 24.6 %collective-permute-start.28 = (bf16[256,1536]{1,0:T(8,128)(2,1)}, bf16[256,1536]{1,0:T(8,128)(2,1)S(1)}, u32[]{:S(2)}, u32[]{:S(2)}) collective-permute-start(bf16[256,1536]{1,0:T(8,128)(2,1)} %shard_map.280.own_ref), channel_id=1, source_target_pairs={{0,1},{1,0},{2,3},{3,2},{4,5},{5,4},{6,7},{7,6},{8,9},{9,8},{10,11... | collective-permute-start | bytes 2359304 | tf_op jit(solution)/shard_map/ppermute | solution.py:1045
  (50 other events, 525.7 us)

commit v3 on v2

--- a/solution.py
+++ b/solution.py
@@ -281,35 +281,31 @@
             far_ref[...] = jnp.zeros_like(far_ref)
             row_ref[...] = jnp.zeros_like(row_ref)
 
-        def block(here, at, mask=None, first=False):
+        accs[...] = jnp.zeros_like(accs)
+
+        def block(here, at, mask=None):
             values = pair_ones(v_ref[here, :])
             for side, key in enumerate(pair_of(k_ref[here, :], gk_ref[here, :], pick_k)):
                 s = dot_t(qx[side, at, :], key)
                 if mask is not None:
                     s = jnp.where(mask, s, BIG)
                 ds = (jnp.exp(s) * dot_t(dx[side, at, :], values[side])).astype(BF)
-                acc = dot(ds, key)
-                accs[side, at, :] = acc if first else accs[side, at, :] + acc
+                accs[side, at, :] += dot(ds, key)
+
+        def earlier(kb, at):
+            block(block_at(kb), at)
+
+            @pl.when(kb == n_far - 1)
+            def _():
+                for side in range(2):
+                    moved = jnp.sum(jnp.where(lane == HD * (1 - side), accs[side], 0.0))
+                    far_ref[...] += jnp.where(lane[:8] == 2 * pair + side, moved, 0.0)
 
         low, high = lo_ref[0], jnp.minimum(lo_ref[1], n_before)
-
-        @pl.when(low < n_far)
-        def _():
-            accs[...] = jnp.zeros_like(accs)
-            pl.loop(high, n_far)(lambda kb: block(block_at(kb), both))
-            pl.loop(low, jnp.minimum(high, n_far))(lambda kb: block(block_at(kb), early))
-            for side in range(2):
-                moved = jnp.sum(jnp.where(lane == HD * (1 - side), accs[side], 0.0))
-                far_ref[...] += jnp.where(lane[:8] == 2 * pair + side, moved, 0.0)
-            block(slice(n_before * BLK, (n_before + 1) * BLK), both, causal_from(rows, 0))
-
-        @pl.when(low >= n_far)
-        def _():
-            block(slice(n_before * BLK, (n_before + 1) * BLK), both, causal_from(rows, 0), True)
-
+        pl.loop(low, high)(lambda kb: earlier(kb, early))
+        pl.loop(high, n_before)(lambda kb: earlier(kb, both))
+        block(slice(n_before * BLK, (n_before + 1) * BLK), both, causal_from(rows, 0))
         block(slice((n_before + 1) * BLK, (n_before + 2) * BLK), late, causal_from(BLK, 0))
-        pl.loop(jnp.maximum(high, n_far), n_before)(lambda kb: block(block_at(kb), both))
-        pl.loop(jnp.maximum(low, n_far), high)(lambda kb: block(block_at(kb), early))
         dq_ref[...] = (jnp.where(lane < HD, accs[0], accs[1]) * HD ** (-0.5)).astype(BF)
         for side in range(2):
             total = lane_column(accs[side], HD * (1 - side))
@@ -1137,7 +1133,8 @@
     next_q1 = shift(sent_q1, -1, n_c)
     next_q2 = shift(sent_q2, -2, n_c)
 
-    down_w = four((after(down_own, mixed_own), down_got)) if shared else four(down_far)
+    down_w = four((after(down_own, keys), down_got)) if shared else four(down_far)
+    mixed_far, down_w[2] = lax.optimization_barrier((mixed_far, down_w[2]))
     hidden, normed_ffn, low_ffn, low_out = out_projection(
         offs, rank, tok, mixed_own, mixed_far, out_w, out_a_own, out_a_far, out_b, gain_two, ffn_a
     )

time: 391 us -> 395 us (1.010)
  starting transfers between devices: 41.3 us -> 49 us
  Pallas kernels: 177 us -> 171 us
    all_to_all x1, starting transfers between devices: 5.23 us -> 15.4 us  [body(): landed = lax.all_to_all(packed, ('fsdp', 'ctx', 'tp'), 0, 0, tiled=True)]
    pallas_call x18, Pallas kernels: 177 us -> 171 us  [call(): pl.pallas_call(kernel, out_shape=outs, grid_spec=pltpu.PrefetchScalarGrid...]
    unnamed x94 -> x88, local copies, waits for them, and re-layouts: 11.6 us -> 13.9 us
  transfers between devices with their start and end apart: 30 -> 30, of which waited for: 12 -> 11; matrix products, arithmetic and copies ran while one was open for 22% -> 23% of each run, Pallas kernels for 45% -> 43%
where the time goes in v3:
time: 395 us; the launch traced here: 390 us
  Pallas kernels  171 us (43%)
  waiting for transfers between devices  71.3 us (18%)
  local copies, waits for them, and re-layouts  55.4 us (14%)
  starting transfers between devices  49 us (12%)
  other arithmetic  27.7 us (7%)
  matrix products  12.9 us (3%)
    pallas_call x18, Pallas kernels, call(): pl.pallas_call(kernel, out_shape=outs, grid_spec=pltpu.PrefetchScalarGrid...  171 us
    ppermute x8, waiting for transfers between devices, other(): return lax.ppermute(values, 'tp', [(0, 1), (1, 0)])  33.1 us
    ppermute x7, waiting for transfers between devices, shift(): return lax.ppermute(values, 'ctx', pairs)  26.2 us
    ppermute x7, starting transfers between devices, shift(): return lax.ppermute(values, 'ctx', pairs)  15.7 us
    all_to_all x1, starting transfers between devices, body(): landed = lax.all_to_all(packed, ('fsdp', 'ctx', 'tp'), 0, 0, tiled=True)  15.4 us
    unnamed x88, local copies, waits for them, and re-layouts  13.9 us
    ppermute x8, starting transfers between devices, other(): return lax.ppermute(values, 'tp', [(0, 1), (1, 0)])  9.74 us
    dot_general x8, matrix products, t_dot(): lax.dot_general(a, b, (((0,), (0,)), ((), ())), preferred_element_type=F32)  9.39 us
  transfers between devices with their start and end apart: 30, of which 11 were waited for; matrix products, arithmetic and copies ran while one was open for 23% of the time, Pallas kernels for 43%

profile of v3, /device:TPU:0, one launch (start us, length us, event | category | flops | bytes accessed | tf_op | source)
XLA Modules:
  0.0 389.6 jit_solution(11968858083915128066)
XLA Ops:
  12.1 4.7 %collective-permute-start = (bf16[544,1536]{1,0:T(8,128)(2,1)}, bf16[544,1536]{1,0:T(8,128)(2,1)}, u32[]{:S(2)}, u32[]{:S(2)}) collective-permute-start(bf16[544,1536]{1,0:T(8,128)(2,1)} %pad_maximum_fusion.2), channel_id=1, source_target_pairs={{0,2},{2,4},{4,6},{1,3},{3,5},{5,7},{8,10},{10,12},{12,14},{9,11},... | collective-permute-start | bytes 5013512 | tf_op jit(solution)/shard_map/ppermute | solution.py:76
  23.7 5.3 %fusion.21 = (bf16[384,1,2048]{2,1,0:T(2,128)(2,1)S(1)}, bf16[384,1,2048]{2,1,0:T(2,128)(2,1)}) fusion(bf16[384,2,2048]{2,1,0:T(2,128)(2,1)S(1)} %copy-done.6), kind=kLoop, calls=%fused_computation.102 | loop fusion | bytes 6291456 | tf_op jit(solution)/shard_map/slice | solution.py:1081
  57.6 4.2 %collective-permute-start.4 = (bf16[320,1536]{1,0:T(8,128)(2,1)}, bf16[320,1536]{1,0:T(8,128)(2,1)}, u32[]{:S(2)}, u32[]{:S(2)}) collective-permute-start(bf16[320,1536]{1,0:T(8,128)(2,1)} %slice.102), channel_id=1, source_target_pairs={{0,2},{2,4},{4,6},{1,3},{3,5},{5,7},{8,10},{10,12},{12,14},{9,11},... | collective-permute-start | bytes 2949128 | tf_op jit(solution)/shard_map/ppermute | solution.py:76
  72.7 9.1 %collective-permute-done.4.refs_2_ = bf16[320,1536]{1,0:T(8,128)(2,1)} collective-permute-done((bf16[320,1536]{1,0:T(8,128)(2,1)}, bf16[320,1536]{1,0:T(8,128)(2,1)}, u32[]{:S(2)}, u32[]{:S(2)}) %collective-permute-start.4) | collective-permute-done | bytes 983072 | tf_op jit(solution)/shard_map/ppermute | solution.py:76
  81.9 11.6 %shard_map.267 = (bf16[512,1536]{1,0:T(8,128)(2,1)}, bf16[512,16]{1,0:T(8,128)(2,1)}, bf16[512,768]{1,0:T(8,128)(2,1)}, bf16[1536,768]{1,0:T(8,128)(2,1)}, bf16[...) custom-call(s32[4]{0:T(128)} %pad_add_fusion.1.refs_0_.offs_ref, bf16[512,1536]{1,0:T(8,128)(2,1)} %bitcast.118, ...), custom_call_target="tpu_custom_call" | custom-call | flops 1 | bytes 1 | tf_op jit(solution)/shard_map/pallas_call | solution.py:89
  99.2 14.5 %shard_map.268 = (bf16[1536,768]{1,0:T(8,128)(2,1)}, bf16[1536,768]{1,0:T(8,128)(2,1)}, f32[1536,128]{1,0:T(8,128)}) custom-call(s32[4]{0:T(128)} %pad_add_fusion.1.refs_0_.offs_ref, bf16[544,1536]{1,0:T(8,128)(2,1)} %collective-permute-done.refs_1_, ...), custom_call_target="tpu_custom_call", output_to_operand_aliasing={{0}: (11, {}), {1}: (12, {}), {2}: (13, {})} | custom-call | flops 1 | bytes 1 | tf_op jit(solution)/shard_map/pallas_call | solution.py:89
  119.5 4.2 %shard_map.269 = (bf16[512,128]{1,0:T(8,128)(2,1)}, bf16[1536,128]{1,0:T(8,128)(2,1)}, bf16[512,128]{1,0:T(8,128)(2,1)}, f32[512,128]{1,0:T(8,128)}, f32[8,128]{1,0:T(8,128)}) custom-call(f32[1536,128]{1,0:T(8,128)} %get-tuple-element.169.logit_ref, s32[1536,1]{1,0:T(8,128)} %broadcast_in_dim.55.seg_ref, s32[1,512]{1,0:T(1,128)} %copy-done.32), custom_call_target="tpu_custom_call" | custom-call | flops 1 | bytes 1 | tf_op jit(solution)/shard_map/pallas_call | solution.py:89
  123.7 13.6 %shard_map.270 = (bf16[512,768]{1,0:T(8,128)(2,1)}, f32[512,768]{1,0:T(8,128)}, bf16[512,128]{1,0:T(8,128)(2,1)}, bf16[512,128]{1,0:T(8,128)(2,1)}) custom-call(s32[2]{0:T(128)} %fusion.18.lo_ref, bf16[512,768]{1,0:T(8,128)(2,1)} %get-tuple-element.160.q_ref, bf16[1536,768]{1,0:T(8,128)(2,1)} %get-tuple-element.164.k_ref, ...), custom_call_target="tpu_custom_call" | custom-call | flops 1 | bytes 1 | tf_op jit(solution)/shard_map/pallas_call | solution.py:89
  143.7 13.9 %collective-permute-done.10.mf = bf16[512,768]{1,0:T(8,128)(2,1)S(1)} collective-permute-done((bf16[512,768]{1,0:T(8,128)(2,1)}, bf16[512,768]{1,0:T(8,128)(2,1)S(1)}, u32[]{:S(2)}, u32[]{:S(2)}) %collective-permute-start.10) | collective-permute-done | bytes 786464 | tf_op jit(solution)/shard_map/ppermute | solution.py:1041
  158.5 10.2 %shard_map.271 = (f32[512,1536]{1,0:T(8,128)}, bf16[512,1536]{1,0:T(8,128)(2,1)}, bf16[512,16]{1,0:T(8,128)(2,1)}, bf16[512,16]{1,0:T(8,128)(2,1)}) custom-call(s32[4]{0:T(128)} %pad_add_fusion.1.refs_0_.offs_ref, s32[1]{0:T(128)} %bitcast.4.rank_ref, bf16[512,1536]{1,0:T(8,128)(2,1)} %bitcast.119, bf16[512,768]{1,0:T(8,128)(2,1)} %get-tuple-element.174.mo, ...), custom_call_target="tpu_custom_call" | custom-call | flops 1724999936 | bytes 1 | tf_op jit(solution)/shard_map/pallas_call | solution.py:89
  177.5 26.8 %shard_map.272 = (bf16[512,2048]{1,0:T(8,128)(2,1)}, bf16[512,2048]{1,0:T(8,128)(2,1)}, bf16[512,2048]{1,0:T(8,128)(2,1)}, bf16[256,1664]{1,0:T(8,128)(2,1)}, f32[256,1536]{1,0:T(8,128)}, /*index=5*/f32[256,128]{1,0:T(8,128)}) custom-call(s32[1]{0:T(128)} %bitcast.4.rank_ref, bf16[512,1536]{1,0:T(8,128)(2,1)} %get-tuple-element.192.x_ref, ...), custom_call_target="tpu_custom_call" | custom-call | flops 4657500160 | bytes 1 | tf_op jit(solution)/shard_map/pallas_call | solution.py:89
  205.1 9.5 %shard_map.273.own_ref = bf16[512,1664]{1,0:T(8,128)(2,1)} custom-call(bf16[512,2048]{1,0:T(8,128)(2,1)} %get-tuple-element.211.u_ref, bf16[384,2048]{1,0:T(8,128)(2,1)} %bitcast.36.rest_8_.w0, bf16[384,2048]{1,0:T(8,128)(2,1)} %copy-done.5, bf16[384,2048]{1,0:T(8,128)(2,1)} %collective-permute-done.13.rest_10_.w2, bf16[384,2048]{1,0:T(8,128)(2,1)} %copy-done.9, ...), custom_call_target="tpu_custom_call" | custom-call | flops 1621500032 | bytes 1 | tf_op jit(solution)/shard_map/pallas_call | solution.py:89
  219.0 6.9 %collective-permute-done.18.got_ref = bf16[256,1664]{1,0:T(8,128)(2,1)S(1)} collective-permute-done((bf16[256,1664]{1,0:T(8,128)(2,1)}, bf16[256,1664]{1,0:T(8,128)(2,1)S(1)}, u32[]{:S(2)}, u32[]{:S(2)}) %collective-permute-start.18) | collective-permute-done | bytes 852000 | tf_op jit(solution)/shard_map/ppermute | solution.py:1041
  226.8 7.6 %shard_map.274 = (f32[256,1536]{1,0:T(8,128)}, bf16[256,1536]{1,0:T(8,128)(2,1)}, bf16[256,16]{1,0:T(8,128)(2,1)}, bf16[256,16]{1,0:T(8,128)(2,1)}, bf16[256,768]{1,0:T(8,128)(2,1)}, /*index=5*/bf16[256,768]{1,0:T(8,128)(2,1)}) custom-call(s32[1]{0:T(128)} %bitcast.4.rank_ref, f32[256,1536]{1,0:T(8,128)} %get-tuple-element.213.own_ref, ...), custom_call_target="tpu_custom_call" | custom-call | flops 1311000064 | bytes 1 | tf_op jit(solution)/shard_map/pallas_call | solution.py:89
  238.6 6.6 %collective-permute-done.19.far_ref = bf16[256,768]{1,0:T(8,128)(2,1)S(1)} collective-permute-done((bf16[256,768]{1,0:T(8,128)(2,1)}, bf16[256,768]{1,0:T(8,128)(2,1)S(1)}, u32[]{:S(2)}, u32[]{:S(2)}) %collective-permute-start.19) | collective-permute-done | bytes 393248 | tf_op jit(solution)/shard_map/ppermute | solution.py:1041
  254.5 13.1 %shard_map.276 = (bf16[512,768]{1,0:T(8,128)(2,1)}, f32[512,128]{1,0:T(8,128)}, f32[8,128]{1,0:T(8,128)}) custom-call(s32[2]{0:T(128)} %fusion.18.lo_ref, bf16[512,768]{1,0:T(8,128)(2,1)} %get-tuple-element.160.q_ref, bf16[1536,768]{1,0:T(8,128)(2,1)} %get-tuple-element.164.k_ref, bf16[1536,768]{1,0:T(8,128)(2,1)} %get-tuple-element.165.v_ref, ...), custom_call_target="tpu_custom_call" | custom-call | flops 3363749888 | bytes 1 | tf_op jit(solution)/shard_map/pallas_call | solution.py:89
  268.3 13.4 %shard_map.277 = (f32[512,768]{1,0:T(8,128)}, f32[512,768]{1,0:T(8,128)}, f32[512,128]{1,0:T(8,128)}) custom-call(bf16[1536,768]{1,0:T(8,128)(2,1)} %get-tuple-element.164.k_ref, bf16[1536,768]{1,0:T(8,128)(2,1)} %get-tuple-element.165.v_ref, bf16[512,768]{1,0:T(8,128)(2,1)} %get-tuple-element.160.q_ref, bf16[512,896]{1,0:T(8,128)(2,1)} %get-tuple-element.225.d_ref.gd_ref, ...), custom_call_target="tpu_custom_call" | custom-call | flops 2294249984 | bytes 1 | tf_op jit(solution)/shard_map/pallas_call | solution.py:89
  283.0 17.1 %collective-permute-done.24.d2_ref.gd2_ref = bf16[288,896]{1,0:T(8,128)(2,1)S(1)} collective-permute-done((bf16[288,896]{1,0:T(8,128)(2,1)}, bf16[288,896]{1,0:T(8,128)(2,1)S(1)}, u32[]{:S(2)}, u32[]{:S(2)}) %collective-permute-start.24) | collective-permute-done | bytes 516128 | tf_op jit(solution)/shard_map/ppermute | solution.py:76
  303.1 12.3 %shard_map.278 = (bf16[512,768]{1,0:T(8,128)(2,1)}, bf16[512,768]{1,0:T(8,128)(2,1)}, f32[512,128]{1,0:T(8,128)}) custom-call(s32[2]{0:T(128)} %fusion.19.hi_ref, bf16[1536,768]{1,0:T(8,128)(2,1)} %get-tuple-element.164.k_ref, bf16[1536,768]{1,0:T(8,128)(2,1)} %get-tuple-element.165.v_ref, bf16[512,896]{1,0:T(8,128)(2,1)} %collective-permute-done.21.q1_ref.gq1_ref, ...), custom_call_target="tpu_custom_call" | custom-call | flops 2932499968 | bytes 1 | tf_op jit(solution)/shard_map/pallas_call | solution.py:89
  316.0 11.1 %shard_map.279 = (bf16[4,256,384]{2,1,0:T(8,128)(2,1)}, f32[4,256,384]{2,1,0:T(8,128)}, f32[16,512]{1,0:T(8,128)}, f32[16,768]{1,0:T(8,128)}, f32[16,768]{1,0:T(8,128)}, /*index=5*/f32[16,768]{1,0:T(8,128)}) custom-call(s32[1]{0:T(128)} %bitcast.4.rank_ref, bf16[512,768]{1,0:T(8,128)(2,1)} %get-tuple-element.221.q_ref, ...), custom_call_target="tpu_custom_call" | custom-call | flops 1932000000 | bytes 1 | tf_op jit(solution)/shard_map/pallas_call | solution.py:89
  340.3 15.4 %all-to-all-start = ((bf16[32,16,768]{2,1,0:T(8,128)(2,1)}), bf16[32,16,768]{2,1,0:T(8,128)(2,1)S(1)}, u32[]{:S(2)}, u32[]{:S(2)}) async-start(bf16[32,16,768]{2,1,0:T(8,128)(2,1)} %bitcast.134), calls=%async_computation | async-start | bytes 1572864 | tf_op jit(solution)/shard_map/all_to_all | solution.py:1225
  355.7 5.0 %shard_map.280.own_ref = bf16[256,1536]{1,0:T(8,128)(2,1)} custom-call(s32[4]{0:T(128)} %pad_add_fusion.1.refs_0_.offs_ref, s32[1]{0:T(128)} %bitcast.4.rank_ref, f32[4,256,384]{2,1,0:T(8,128)} %get-tuple-element.245.own_ref, bf16[4,256,384]{2,1,0:T(8,128)(2,1)} %collective-permute-done.26.got_ref, bf16[16,512]{1,0:T(8,128)(2,1)} %copy-done.31, ...), custom_call_target="tpu_custom_call" | custom-call | flops 862499968 | bytes 1 | tf_op jit(solution)/shard_map/pallas_call | solution.py:89
  367.1 4.9 %shard_map.281 = bf16[512,1536]{1,0:T(8,128)(2,1)} custom-call(s32[4]{0:T(128)} %pad_add_fusion.1.refs_0_.offs_ref, f32[512,1536]{1,0:T(8,128)} %get-tuple-element.191.h_ref, bf16[512,1664]{1,0:T(8,128)(2,1)} %shard_map.273.own_ref, bf16[512,1664]{1,0:T(8,128)(2,1)} %collective-permute-done.20.got_ref, bf16[16,1536]{1,0:T(8,128)(2,1)} %pad_maximum_fusion.12.b_ref), custom_call_target="tpu_custom_call" | custom-call | flops 862499968 | bytes 1 | tf_op jit(solution)/shard_map/pallas_call | solution.py:89
  372.0 5.7 %all-to-all-done = bf16[32,16,768]{2,1,0:T(8,128)(2,1)S(1)} async-done(((bf16[32,16,768]{2,1,0:T(8,128)(2,1)}), bf16[32,16,768]{2,1,0:T(8,128)(2,1)S(1)}, u32[]{:S(2)}, u32[]{:S(2)}) %all-to-all-start) | async-done | bytes 786464 | tf_op jit(solution)/shard_map/all_to_all | solution.py:1225
  (229 shorter events, 140.7 us)
Async XLA Ops:
  0.7 50.2 %collective-permute-start.3 = (bf16[768,384]{1,0:T(8,128)(2,1)}, bf16[768,384]{1,0:T(8,128)(2,1)}, u32[]{:S(2)}, u32[]{:S(2)}) collective-permute-start(bf16[768,384]{1,0:T(8,128)(2,1)} %param.28), channel_id=1, source_target_pairs={{0,1},{1,0},{2,3},{3,2},{4,5},{5,4},{6,7},{7,6},{8,9},{9,8},{10,11... | collective-permute-start | bytes 1769480 | tf_op jit(solution)/shard_map/ppermute | solution.py:1041
  6.6 45.5 %collective-permute-start.1 = (bf16[384,2304]{1,0:T(8,128)(2,1)}, bf16[384,2304]{1,0:T(8,128)(2,1)}, u32[]{:S(2)}, u32[]{:S(2)}) collective-permute-start(bf16[384,2304]{1,0:T(8,128)(2,1)} %pad_maximum_fusion.1.refs_3_.refs_4_.refs_0_), channel_id=1, source_target_pairs={{0,16},{8,24},{16,0},{24,8},{1,17},{9,25},{17,1},{25,9},{2,18},{10... | collective-permute-start | bytes 5308424 | tf_op jit(solution)/shard_map/ppermute | solution.py:43
  8.8 43.3 %collective-permute-start.2 = (bf16[384,13]{0,1:T(8,128)(2,1)S(1)}, bf16[384,13]{0,1:T(8,128)(2,1)}, u32[]{:S(2)}, u32[]{:S(2)}) collective-permute-start(bf16[384,13]{0,1:T(8,128)(2,1)S(1)} %concatenate.68), channel_id=1, source_target_pairs={{0,16},{8,24},{16,0},{24,8},{1,17},{9,25},{17,1},{25,9},{2,18},{10... | collective-permute-start | bytes 29960 | tf_op jit(solution)/shard_map/ppermute | solution.py:43
  12.1 40.0 %collective-permute-start = (bf16[544,1536]{1,0:T(8,128)(2,1)}, bf16[544,1536]{1,0:T(8,128)(2,1)}, u32[]{:S(2)}, u32[]{:S(2)}) collective-permute-start(bf16[544,1536]{1,0:T(8,128)(2,1)} %pad_maximum_fusion.2), channel_id=1, source_target_pairs={{0,2},{2,4},{4,6},{1,3},{3,5},{5,7},{8,10},{10,12},{12,14},{9,11},... | collective-permute-start | bytes 5013512 | tf_op jit(solution)/shard_map/ppermute | solution.py:76
  52.1 29.8 %collective-permute-start.5 = (bf16[384,2304]{1,0:T(8,128)(2,1)}, bf16[384,2304]{1,0:T(8,128)(2,1)}, u32[]{:S(2)}, u32[]{:S(2)}) collective-permute-start(bf16[384,2304]{1,0:T(8,128)(2,1)} %pad_maximum_fusion.1.refs_3_.refs_4_.refs_0_), channel_id=1, source_target_pairs={{0,8},{8,0},{16,24},{24,16},{1,9},{9,1},{17,25},{25,17},{2,10},{10... | collective-permute-start | bytes 5308424 | tf_op jit(solution)/shard_map/ppermute | solution.py:1044
  52.2 29.7 %collective-permute-start.6 = (bf16[384,2304]{1,0:T(8,128)(2,1)}, bf16[384,2304]{1,0:T(8,128)(2,1)}, u32[]{:S(2)}, u32[]{:S(2)}) collective-permute-start(bf16[384,2304]{1,0:T(8,128)(2,1)} %collective-permute-done.1.refs_4_.refs_5_.refs_1_), channel_id=1, source_target_pairs={{0,8},{8,0},{16,24},{24,16},{1,9},{9,1},{17,25},{25,17},{2,10},{10... | collective-permute-start | bytes 5308424 | tf_op jit(solution)/shard_map/ppermute | solution.py:1044
  52.7 40.8 %collective-permute-start.8 = (bf16[1536,384]{1,0:T(8,128)(2,1)S(1)}, bf16[1536,384]{1,0:T(8,128)(2,1)}, u32[]{:S(2)}, u32[]{:S(2)}) collective-permute-start(bf16[1536,384]{1,0:T(8,128)(2,1)S(1)} %pad_maximum_fusion.5), channel_id=1, source_target_pairs={{0,16},{8,24},{16,0},{24,8},{1,17},{9,25},{17,1},{25,9},{2,18},{10... | collective-permute-start | bytes 3538952 | tf_op jit(solution)/shard_map/ppermute | solution.py:43
  57.6 24.2 %collective-permute-start.4 = (bf16[320,1536]{1,0:T(8,128)(2,1)}, bf16[320,1536]{1,0:T(8,128)(2,1)}, u32[]{:S(2)}, u32[]{:S(2)}) collective-permute-start(bf16[320,1536]{1,0:T(8,128)(2,1)} %slice.102), channel_id=1, source_target_pairs={{0,2},{2,4},{4,6},{1,3},{3,5},{5,7},{8,10},{10,12},{12,14},{9,11},... | collective-permute-start | bytes 2949128 | tf_op jit(solution)/shard_map/ppermute | solution.py:76
  67.0 30.6 %collective-permute-start.11 = (bf16[384,1024]{1,0:T(8,128)(2,1)}, bf16[384,1024]{1,0:T(8,128)(2,1)}, u32[]{:S(2)}, u32[]{:S(2)}) collective-permute-start(bf16[384,1024]{1,0:T(8,128)(2,1)} %dynamic-slice_bitcast_fusion), channel_id=1, source_target_pairs={{0,16},{8,24},{16,0},{24,8},{1,17},{9,25},{17,1},{25,9},{2,18},{10... | collective-permute-start | bytes 2359304 | tf_op jit(solution)/shard_map/ppermute | solution.py:43
  95.0 24.5 %collective-permute-start.9 = (bf16[1536,768]{1,0:T(8,128)(2,1)S(1)}, bf16[1536,768]{1,0:T(8,128)(2,1)}, u32[]{:S(2)}, u32[]{:S(2)}) collective-permute-start(bf16[1536,768]{1,0:T(8,128)(2,1)S(1)} %constant_dynamic-update-slice_fusion.3.wo0.wf0), channel_id=1, source_target_pairs={{0,8},{8,0},{16,24},{24,16},{1,9},{9,1},{17,25},{25,17},{2,10},{10... | collective-permute-start | bytes 7077896 | tf_op jit(solution)/shard_map/ppermute | solution.py:52
  97.6 71.1 %collective-permute-start.14 = (bf16[384,4096]{1,0:T(8,128)(2,1)}, bf16[384,4096]{1,0:T(8,128)(2,1)}, u32[]{:S(2)}, u32[]{:S(2)}) collective-permute-start(bf16[384,4096]{1,0:T(8,128)(2,1)} %pad_maximum_fusion.rest_0_.rest_4_), channel_id=1, source_target_pairs={{0,16},{8,24},{16,0},{24,8},{1,17},{9,25},{17,1},{25,9},{2,18},{10... | collective-permute-start | bytes 9437192 | tf_op jit(solution)/shard_map/ppermute | solution.py:43
  113.7 25.2 %collective-permute-start.12 = (bf16[384,1024]{1,0:T(8,128)(2,1)}, bf16[384,1024]{1,0:T(8,128)(2,1)}, u32[]{:S(2)}, u32[]{:S(2)}) collective-permute-start(bf16[384,1024]{1,0:T(8,128)(2,1)} %collective-permute-done.11), channel_id=1, source_target_pairs={{0,2},{2,0},{4,6},{6,4},{1,3},{3,1},{5,7},{7,5},{8,10},{10,8},{12,... | collective-permute-start | bytes 2359304 | tf_op jit(solution)/shard_map/ppermute | solution.py:1126
  114.8 42.8 %collective-permute-start.13 = (bf16[384,2048]{1,0:T(8,128)(2,1)}, bf16[384,2048]{1,0:T(8,128)(2,1)}, u32[]{:S(2)}, u32[]{:S(2)}) collective-permute-start(bf16[384,2048]{1,0:T(8,128)(2,1)} %bitcast.36.rest_8_.w0), channel_id=1, source_target_pairs={{0,8},{8,0},{16,24},{24,16},{1,9},{9,1},{17,25},{25,17},{2,10},{10... | collective-permute-start | bytes 4718600 | tf_op jit(solution)/shard_map/ppermute | solution.py:1044
  139.0 37.4 %collective-permute-start.15 = (bf16[384,4096]{1,0:T(8,128)(2,1)}, bf16[384,4096]{1,0:T(8,128)(2,1)}, u32[]{:S(2)}, u32[]{:S(2)}) collective-permute-start(bf16[384,4096]{1,0:T(8,128)(2,1)} %pad_maximum_fusion.rest_0_.rest_4_), channel_id=1, source_target_pairs={{0,8},{8,0},{16,24},{24,16},{1,9},{9,1},{17,25},{25,17},{2,10},{10... | collective-permute-start | bytes 9437192 | tf_op jit(solution)/shard_map/ppermute | solution.py:1044
  170.7 111.0 %collective-permute-start.22 = (bf16[288,896]{1,0:T(8,128)(2,1)}, bf16[288,896]{1,0:T(8,128)(2,1)S(1)}, u32[]{:S(2)}, u32[]{:S(2)}) collective-permute-start(bf16[288,896]{1,0:T(8,128)(2,1)} %pad_maximum_fusion.7), channel_id=1, source_target_pairs={{4,0},{6,2},{5,1},{7,3},{12,8},{14,10},{13,9},{15,11},{20,16},{22,... | collective-permute-start | bytes 1548296 | tf_op jit(solution)/shard_map/ppermute | solution.py:76
  172.0 111.0 %collective-permute-start.21 = (bf16[512,896]{1,0:T(8,128)(2,1)}, bf16[512,896]{1,0:T(8,128)(2,1)}, u32[]{:S(2)}, u32[]{:S(2)}) collective-permute-start(bf16[512,896]{1,0:T(8,128)(2,1)} %pad_maximum_fusion.6), channel_id=1, source_target_pairs={{2,0},{4,2},{6,4},{3,1},{5,3},{7,5},{10,8},{12,10},{14,12},{11,9},... | collective-permute-start | bytes 2752520 | tf_op jit(solution)/shard_map/ppermute | solution.py:76
  204.4 21.5 %collective-permute-start.18 = (bf16[256,1664]{1,0:T(8,128)(2,1)}, bf16[256,1664]{1,0:T(8,128)(2,1)S(1)}, u32[]{:S(2)}, u32[]{:S(2)}) collective-permute-start(bf16[256,1664]{1,0:T(8,128)(2,1)} %get-tuple-element.204), channel_id=1, source_target_pairs={{0,1},{1,0},{2,3},{3,2},{4,5},{5,4},{6,7},{7,6},{8,9},{9,8},{10,11... | collective-permute-start | bytes 2555912 | tf_op jit(solution)/shard_map/ppermute | solution.py:1041
  249.9 50.2 %collective-permute-start.23 = (bf16[512,896]{1,0:T(8,128)(2,1)}, bf16[512,896]{1,0:T(8,128)(2,1)S(1)}, u32[]{:S(2)}, u32[]{:S(2)}) collective-permute-start(bf16[512,896]{1,0:T(8,128)(2,1)} %get-tuple-element.225.d_ref.gd_ref), channel_id=1, source_target_pairs={{2,0},{4,2},{6,4},{3,1},{5,3},{7,5},{10,8},{12,10},{14,12},{11,9},... | collective-permute-start | bytes 2752520 | tf_op jit(solution)/shard_map/ppermute | solution.py:76
  252.9 47.2 %collective-permute-start.24 = (bf16[288,896]{1,0:T(8,128)(2,1)}, bf16[288,896]{1,0:T(8,128)(2,1)S(1)}, u32[]{:S(2)}, u32[]{:S(2)}) collective-permute-start(bf16[288,896]{1,0:T(8,128)(2,1)} %get-tuple-element.224), channel_id=1, source_target_pairs={{4,0},{6,2},{5,1},{7,3},{12,8},{14,10},{13,9},{15,11},{20,16},{22,... | collective-permute-start | bytes 1548296 | tf_op jit(solution)/shard_map/ppermute | solution.py:76
  267.6 67.5 %collective-permute-start.20 = (bf16[512,1664]{1,0:T(8,128)(2,1)S(1)}, bf16[512,1664]{1,0:T(8,128)(2,1)}, u32[]{:S(2)}, u32[]{:S(2)}) collective-permute-start(bf16[512,1664]{1,0:T(8,128)(2,1)S(1)} %copy-done.8), channel_id=1, source_target_pairs={{0,1},{1,0},{2,3},{3,2},{4,5},{5,4},{6,7},{7,6},{8,9},{9,8},{10,11... | collective-permute-start | bytes 5111816 | tf_op jit(solution)/shard_map/ppermute | solution.py:1041
  281.7 33.7 %collective-permute-start.25 = (f32[8,128]{1,0:T(8,128)S(1)}, f32[8,128]{1,0:T(8,128)S(1)}, u32[]{:S(2)}, u32[]{:S(2)}) collective-permute-start(f32[8,128]{1,0:T(8,128)S(1)} %copy-done.39), channel_id=1, source_target_pairs={{2,0},{4,2},{6,4},{3,1},{5,3},{7,5},{10,8},{12,10},{14,12},{11,9},... | collective-permute-start | bytes 12296 | tf_op jit(solution)/shard_map/ppermute | solution.py:76
  328.6 27.1 %collective-permute-start.26 = (bf16[4,256,384]{2,1,0:T(8,128)(2,1)}, bf16[4,256,384]{2,1,0:T(8,128)(2,1)}, u32[]{:S(2)}, u32[]{:S(2)}) collective-permute-start(bf16[4,256,384]{2,1,0:T(8,128)(2,1)} %get-tuple-element.246), channel_id=1, source_target_pairs={{0,1},{1,0},{2,3},{3,2},{4,5},{5,4},{6,7},{7,6},{8,9},{9,8},{10,11... | collective-permute-start | bytes 2359304 | tf_op jit(solution)/shard_map/ppermute | solution.py:1041
  340.3 37.4 %all-to-all-start = ((bf16[32,16,768]{2,1,0:T(8,128)(2,1)}), bf16[32,16,768]{2,1,0:T(8,128)(2,1)S(1)}, u32[]{:S(2)}, u32[]{:S(2)}) async-start(bf16[32,16,768]{2,1,0:T(8,128)(2,1)} %bitcast.134), calls=%async_computation | async-start | bytes 1572864 | tf_op jit(solution)/shard_map/all_to_all | solution.py:1225
  360.7 24.6 %collective-permute-start.28 = (bf16[256,1536]{1,0:T(8,128)(2,1)}, bf16[256,1536]{1,0:T(8,128)(2,1)S(1)}, u32[]{:S(2)}, u32[]{:S(2)}) collective-permute-start(bf16[256,1536]{1,0:T(8,128)(2,1)} %shard_map.280.own_ref), channel_id=1, source_target_pairs={{0,1},{1,0},{2,3},{3,2},{4,5},{5,4},{6,7},{7,6},{8,9},{9,8},{10,11... | collective-permute-start | bytes 2359304 | tf_op jit(solution)/shard_map/ppermute | solution.py:1041
  (47 other events, 496.4 us)

commit v4 on v3

--- a/solution.py
+++ b/solution.py
@@ -424,8 +424,7 @@
             one, two = (q1_ref, gq1_ref, d1_ref, gd1_ref), (q2_ref, gq2_ref, d2_ref, gd2_ref)
             pl.loop(0, jnp.minimum(few, 2))(lambda j: block(one, block_at(j), both))
             pl.loop(few, jnp.minimum(many, 2))(lambda j: block(one, block_at(j), late))
-            pl.when(few > 2)(lambda: block(two, early, both))
-            pl.when((few <= 2) & (many > 2))(lambda: block(two, early, late))
+            pl.when(many > 2)(lambda: block(two, early, both))
             pl.when(many > 3)(lambda: block(two, slice(BLK, tail), both))
             for side in range(2):
                 value = lane_column(dks[side], HD * (1 - side) + 3)

time: 395 us -> 397 us (level)
  starting transfers between devices: 49 us -> 36.1 us
  Pallas kernels: 171 us -> 180 us
  waiting for transfers between devices: 71.3 us -> 75.8 us
    all_to_all x1, starting transfers between devices: 15.4 us -> 2.63 us  [body(): landed = lax.all_to_all(packed, ('fsdp', 'ctx', 'tp'), 0, 0, tiled=True)]
    pallas_call x18, Pallas kernels: 171 us -> 180 us  [call(): pl.pallas_call(kernel, out_shape=outs, grid_spec=pltpu.PrefetchScalarGrid...]
    ppermute x7, waiting for transfers between devices: 26.2 us -> 30.7 us  [shift(): return lax.ppermute(values, 'ctx', pairs)]
  transfers between devices with their start and end apart: 30 -> 30, of which waited for: 11 -> 11; matrix products, arithmetic and copies ran while one was open for 23% -> 23% of each run, Pallas kernels for 43% -> 45%
where the time goes in v4:
time: 397 us; the launch traced here: 390 us
  Pallas kernels  180 us (45%)
  waiting for transfers between devices  75.8 us (19%)
  local copies, waits for them, and re-layouts  55.4 us (14%)
  starting transfers between devices  36.1 us (9%)
  other arithmetic  27.7 us (7%)
  matrix products  12.9 us (3%)
    pallas_call x18, Pallas kernels, call(): pl.pallas_call(kernel, out_shape=outs, grid_spec=pltpu.PrefetchScalarGrid...  180 us
    ppermute x8, waiting for transfers between devices, other(): return lax.ppermute(values, 'tp', [(0, 1), (1, 0)])  33.1 us
    ppermute x7, waiting for transfers between devices, shift(): return lax.ppermute(values, 'ctx', pairs)  30.7 us
    ppermute x7, starting transfers between devices, shift(): return lax.ppermute(values, 'ctx', pairs)  15.7 us
    unnamed x88, local copies, waits for them, and re-layouts  13.9 us
    ppermute x8, starting transfers between devices, other(): return lax.ppermute(values, 'tp', [(0, 1), (1, 0)])  9.62 us
    dot_general x8, matrix products, t_dot(): lax.dot_general(a, b, (((0,), (0,)), ((), ())), preferred_element_type=F32)  9.39 us
  transfers between devices with their start and end apart: 30, of which 11 were waited for; matrix products, arithmetic and copies ran while one was open for 23% of the time, Pallas kernels for 45%

profile of v4, /device:TPU:0, one launch (start us, length us, event | category | flops | bytes accessed | tf_op | source)
XLA Modules:
  0.0 390.1 jit_solution(16003059297370423926)
XLA Ops:
  12.1 4.7 %collective-permute-start = (bf16[544,1536]{1,0:T(8,128)(2,1)}, bf16[544,1536]{1,0:T(8,128)(2,1)}, u32[]{:S(2)}, u32[]{:S(2)}) collective-permute-start(bf16[544,1536]{1,0:T(8,128)(2,1)} %pad_maximum_fusion.2), channel_id=1, source_target_pairs={{0,2},{2,4},{4,6},{1,3},{3,5},{5,7},{8,10},{10,12},{12,14},{9,11},... | collective-permute-start | bytes 5013512 | tf_op jit(solution)/shard_map/ppermute | solution.py:76
  23.7 5.3 %fusion.21 = (bf16[384,1,2048]{2,1,0:T(2,128)(2,1)S(1)}, bf16[384,1,2048]{2,1,0:T(2,128)(2,1)}) fusion(bf16[384,2,2048]{2,1,0:T(2,128)(2,1)S(1)} %copy-done.6), kind=kLoop, calls=%fused_computation.102 | loop fusion | bytes 6291456 | tf_op jit(solution)/shard_map/slice | solution.py:1080
  57.6 4.2 %collective-permute-start.4 = (bf16[320,1536]{1,0:T(8,128)(2,1)}, bf16[320,1536]{1,0:T(8,128)(2,1)}, u32[]{:S(2)}, u32[]{:S(2)}) collective-permute-start(bf16[320,1536]{1,0:T(8,128)(2,1)} %slice.102), channel_id=1, source_target_pairs={{0,2},{2,4},{4,6},{1,3},{3,5},{5,7},{8,10},{10,12},{12,14},{9,11},... | collective-permute-start | bytes 2949128 | tf_op jit(solution)/shard_map/ppermute | solution.py:76
  72.7 9.1 %collective-permute-done.4.refs_2_ = bf16[320,1536]{1,0:T(8,128)(2,1)} collective-permute-done((bf16[320,1536]{1,0:T(8,128)(2,1)}, bf16[320,1536]{1,0:T(8,128)(2,1)}, u32[]{:S(2)}, u32[]{:S(2)}) %collective-permute-start.4) | collective-permute-done | bytes 983072 | tf_op jit(solution)/shard_map/ppermute | solution.py:76
  81.9 11.6 %shard_map.267 = (bf16[512,1536]{1,0:T(8,128)(2,1)}, bf16[512,16]{1,0:T(8,128)(2,1)}, bf16[512,768]{1,0:T(8,128)(2,1)}, bf16[1536,768]{1,0:T(8,128)(2,1)}, bf16[...) custom-call(s32[4]{0:T(128)} %pad_add_fusion.1.refs_0_.offs_ref, bf16[512,1536]{1,0:T(8,128)(2,1)} %bitcast.118, ...), custom_call_target="tpu_custom_call" | custom-call | flops 1 | bytes 1 | tf_op jit(solution)/shard_map/pallas_call | solution.py:89
  99.2 14.5 %shard_map.268 = (bf16[1536,768]{1,0:T(8,128)(2,1)}, bf16[1536,768]{1,0:T(8,128)(2,1)}, f32[1536,128]{1,0:T(8,128)}) custom-call(s32[4]{0:T(128)} %pad_add_fusion.1.refs_0_.offs_ref, bf16[544,1536]{1,0:T(8,128)(2,1)} %collective-permute-done.refs_1_, ...), custom_call_target="tpu_custom_call", output_to_operand_aliasing={{0}: (11, {}), {1}: (12, {}), {2}: (13, {})} | custom-call | flops 1 | bytes 1 | tf_op jit(solution)/shard_map/pallas_call | solution.py:89
  119.5 4.2 %shard_map.269 = (bf16[512,128]{1,0:T(8,128)(2,1)}, bf16[1536,128]{1,0:T(8,128)(2,1)}, bf16[512,128]{1,0:T(8,128)(2,1)}, f32[512,128]{1,0:T(8,128)}, f32[8,128]{1,0:T(8,128)}) custom-call(f32[1536,128]{1,0:T(8,128)} %get-tuple-element.169.logit_ref, s32[1536,1]{1,0:T(8,128)} %broadcast_in_dim.55.seg_ref, s32[1,512]{1,0:T(1,128)} %copy-done.32), custom_call_target="tpu_custom_call" | custom-call | flops 1 | bytes 1 | tf_op jit(solution)/shard_map/pallas_call | solution.py:89
  123.7 13.6 %shard_map.270 = (bf16[512,768]{1,0:T(8,128)(2,1)}, f32[512,768]{1,0:T(8,128)}, bf16[512,128]{1,0:T(8,128)(2,1)}, bf16[512,128]{1,0:T(8,128)(2,1)}) custom-call(s32[2]{0:T(128)} %fusion.18.lo_ref, bf16[512,768]{1,0:T(8,128)(2,1)} %get-tuple-element.160.q_ref, bf16[1536,768]{1,0:T(8,128)(2,1)} %get-tuple-element.164.k_ref, ...), custom_call_target="tpu_custom_call" | custom-call | flops 1 | bytes 1 | tf_op jit(solution)/shard_map/pallas_call | solution.py:89
  143.7 13.9 %collective-permute-done.10.mf = bf16[512,768]{1,0:T(8,128)(2,1)S(1)} collective-permute-done((bf16[512,768]{1,0:T(8,128)(2,1)}, bf16[512,768]{1,0:T(8,128)(2,1)S(1)}, u32[]{:S(2)}, u32[]{:S(2)}) %collective-permute-start.10) | collective-permute-done | bytes 786464 | tf_op jit(solution)/shard_map/ppermute | solution.py:1040
  158.5 10.2 %shard_map.271 = (f32[512,1536]{1,0:T(8,128)}, bf16[512,1536]{1,0:T(8,128)(2,1)}, bf16[512,16]{1,0:T(8,128)(2,1)}, bf16[512,16]{1,0:T(8,128)(2,1)}) custom-call(s32[4]{0:T(128)} %pad_add_fusion.1.refs_0_.offs_ref, s32[1]{0:T(128)} %bitcast.4.rank_ref, bf16[512,1536]{1,0:T(8,128)(2,1)} %bitcast.119, bf16[512,768]{1,0:T(8,128)(2,1)} %get-tuple-element.174.mo, ...), custom_call_target="tpu_custom_call" | custom-call | flops 1724999936 | bytes 1 | tf_op jit(solution)/shard_map/pallas_call | solution.py:89
  177.5 26.8 %shard_map.272 = (bf16[512,2048]{1,0:T(8,128)(2,1)}, bf16[512,2048]{1,0:T(8,128)(2,1)}, bf16[512,2048]{1,0:T(8,128)(2,1)}, bf16[256,1664]{1,0:T(8,128)(2,1)}, f32[256,1536]{1,0:T(8,128)}, /*index=5*/f32[256,128]{1,0:T(8,128)}) custom-call(s32[1]{0:T(128)} %bitcast.4.rank_ref, bf16[512,1536]{1,0:T(8,128)(2,1)} %get-tuple-element.192.x_ref, ...), custom_call_target="tpu_custom_call" | custom-call | flops 4657500160 | bytes 1 | tf_op jit(solution)/shard_map/pallas_call | solution.py:89
  205.1 9.5 %shard_map.273.own_ref = bf16[512,1664]{1,0:T(8,128)(2,1)} custom-call(bf16[512,2048]{1,0:T(8,128)(2,1)} %get-tuple-element.211.u_ref, bf16[384,2048]{1,0:T(8,128)(2,1)} %bitcast.36.rest_8_.w0, bf16[384,2048]{1,0:T(8,128)(2,1)} %copy-done.5, bf16[384,2048]{1,0:T(8,128)(2,1)} %collective-permute-done.13.rest_10_.w2, bf16[384,2048]{1,0:T(8,128)(2,1)} %copy-done.9, ...), custom_call_target="tpu_custom_call" | custom-call | flops 1621500032 | bytes 1 | tf_op jit(solution)/shard_map/pallas_call | solution.py:89
  219.0 6.9 %collective-permute-done.18.got_ref = bf16[256,1664]{1,0:T(8,128)(2,1)S(1)} collective-permute-done((bf16[256,1664]{1,0:T(8,128)(2,1)}, bf16[256,1664]{1,0:T(8,128)(2,1)S(1)}, u32[]{:S(2)}, u32[]{:S(2)}) %collective-permute-start.18) | collective-permute-done | bytes 852000 | tf_op jit(solution)/shard_map/ppermute | solution.py:1040
  226.8 7.6 %shard_map.274 = (f32[256,1536]{1,0:T(8,128)}, bf16[256,1536]{1,0:T(8,128)(2,1)}, bf16[256,16]{1,0:T(8,128)(2,1)}, bf16[256,16]{1,0:T(8,128)(2,1)}, bf16[256,768]{1,0:T(8,128)(2,1)}, /*index=5*/bf16[256,768]{1,0:T(8,128)(2,1)}) custom-call(s32[1]{0:T(128)} %bitcast.4.rank_ref, f32[256,1536]{1,0:T(8,128)} %get-tuple-element.213.own_ref, ...), custom_call_target="tpu_custom_call" | custom-call | flops 1311000064 | bytes 1 | tf_op jit(solution)/shard_map/pallas_call | solution.py:89
  238.6 6.6 %collective-permute-done.19.far_ref = bf16[256,768]{1,0:T(8,128)(2,1)S(1)} collective-permute-done((bf16[256,768]{1,0:T(8,128)(2,1)}, bf16[256,768]{1,0:T(8,128)(2,1)S(1)}, u32[]{:S(2)}, u32[]{:S(2)}) %collective-permute-start.19) | collective-permute-done | bytes 393248 | tf_op jit(solution)/shard_map/ppermute | solution.py:1040
  246.0 3.9 shard_map.275
  254.5 13.1 %shard_map.276 = (bf16[512,768]{1,0:T(8,128)(2,1)}, f32[512,128]{1,0:T(8,128)}, f32[8,128]{1,0:T(8,128)}) custom-call(s32[2]{0:T(128)} %fusion.18.lo_ref, bf16[512,768]{1,0:T(8,128)(2,1)} %get-tuple-element.160.q_ref, bf16[1536,768]{1,0:T(8,128)(2,1)} %get-tuple-element.164.k_ref, bf16[1536,768]{1,0:T(8,128)(2,1)} %get-tuple-element.165.v_ref, ...), custom_call_target="tpu_custom_call" | custom-call | flops 3363749888 | bytes 1 | tf_op jit(solution)/shard_map/pallas_call | solution.py:89
  268.3 13.4 %shard_map.277 = (f32[512,768]{1,0:T(8,128)}, f32[512,768]{1,0:T(8,128)}, f32[512,128]{1,0:T(8,128)}) custom-call(bf16[1536,768]{1,0:T(8,128)(2,1)} %get-tuple-element.164.k_ref, bf16[1536,768]{1,0:T(8,128)(2,1)} %get-tuple-element.165.v_ref, bf16[512,768]{1,0:T(8,128)(2,1)} %get-tuple-element.160.q_ref, bf16[512,896]{1,0:T(8,128)(2,1)} %get-tuple-element.225.d_ref.gd_ref, ...), custom_call_target="tpu_custom_call" | custom-call | flops 2294249984 | bytes 1 | tf_op jit(solution)/shard_map/pallas_call | solution.py:89
  283.0 21.5 %collective-permute-done.24.d2_ref.gd2_ref = bf16[288,896]{1,0:T(8,128)(2,1)S(1)} collective-permute-done((bf16[288,896]{1,0:T(8,128)(2,1)}, bf16[288,896]{1,0:T(8,128)(2,1)S(1)}, u32[]{:S(2)}, u32[]{:S(2)}) %collective-permute-start.24) | collective-permute-done | bytes 516128 | tf_op jit(solution)/shard_map/ppermute | solution.py:76
  307.6 21.2 %shard_map.278 = (bf16[512,768]{1,0:T(8,128)(2,1)}, bf16[512,768]{1,0:T(8,128)(2,1)}, f32[512,128]{1,0:T(8,128)}) custom-call(s32[2]{0:T(128)} %fusion.19.hi_ref, bf16[1536,768]{1,0:T(8,128)(2,1)} %get-tuple-element.164.k_ref, bf16[1536,768]{1,0:T(8,128)(2,1)} %get-tuple-element.165.v_ref, bf16[512,896]{1,0:T(8,128)(2,1)} %collective-permute-done.21.q1_ref.gq1_ref, ...), custom_call_target="tpu_custom_call" | custom-call | flops 2932499968 | bytes 1 | tf_op jit(solution)/shard_map/pallas_call | solution.py:89
  329.4 11.1 %shard_map.279 = (bf16[4,256,384]{2,1,0:T(8,128)(2,1)}, f32[4,256,384]{2,1,0:T(8,128)}, f32[16,512]{1,0:T(8,128)}, f32[16,768]{1,0:T(8,128)}, f32[16,768]{1,0:T(8,128)}, /*index=5*/f32[16,768]{1,0:T(8,128)}) custom-call(s32[1]{0:T(128)} %bitcast.4.rank_ref, bf16[512,768]{1,0:T(8,128)(2,1)} %get-tuple-element.221.q_ref, ...), custom_call_target="tpu_custom_call" | custom-call | flops 1932000000 | bytes 1 | tf_op jit(solution)/shard_map/pallas_call | solution.py:89
  356.3 5.0 %shard_map.280.own_ref = bf16[256,1536]{1,0:T(8,128)(2,1)} custom-call(s32[4]{0:T(128)} %pad_add_fusion.1.refs_0_.offs_ref, s32[1]{0:T(128)} %bitcast.4.rank_ref, f32[4,256,384]{2,1,0:T(8,128)} %get-tuple-element.245.own_ref, bf16[4,256,384]{2,1,0:T(8,128)(2,1)} %collective-permute-done.26.got_ref, bf16[16,512]{1,0:T(8,128)(2,1)} %copy-done.31, ...), custom_call_target="tpu_custom_call" | custom-call | flops 862499968 | bytes 1 | tf_op jit(solution)/shard_map/pallas_call | solution.py:89
  367.6 4.9 %shard_map.281 = bf16[512,1536]{1,0:T(8,128)(2,1)} custom-call(s32[4]{0:T(128)} %pad_add_fusion.1.refs_0_.offs_ref, f32[512,1536]{1,0:T(8,128)} %get-tuple-element.191.h_ref, bf16[512,1664]{1,0:T(8,128)(2,1)} %shard_map.273.own_ref, bf16[512,1664]{1,0:T(8,128)(2,1)} %collective-permute-done.20.got_ref, bf16[16,1536]{1,0:T(8,128)(2,1)} %pad_maximum_fusion.12.b_ref), custom_call_target="tpu_custom_call" | custom-call | flops 862499968 | bytes 1 | tf_op jit(solution)/shard_map/pallas_call | solution.py:89
  372.5 5.8 %all-to-all-done = bf16[32,16,768]{2,1,0:T(8,128)(2,1)S(1)} async-done(((bf16[32,16,768]{2,1,0:T(8,128)(2,1)}), bf16[32,16,768]{2,1,0:T(8,128)(2,1)S(1)}, u32[]{:S(2)}, u32[]{:S(2)}) %all-to-all-start) | async-done | bytes 786464 | tf_op jit(solution)/shard_map/all_to_all | solution.py:1224
  (229 shorter events, 139.2 us)
Async XLA Ops:
  0.7 50.2 %collective-permute-start.3 = (bf16[768,384]{1,0:T(8,128)(2,1)}, bf16[768,384]{1,0:T(8,128)(2,1)}, u32[]{:S(2)}, u32[]{:S(2)}) collective-permute-start(bf16[768,384]{1,0:T(8,128)(2,1)} %param.28), channel_id=1, source_target_pairs={{0,1},{1,0},{2,3},{3,2},{4,5},{5,4},{6,7},{7,6},{8,9},{9,8},{10,11... | collective-permute-start | bytes 1769480 | tf_op jit(solution)/shard_map/ppermute | solution.py:1040
  6.6 45.5 %collective-permute-start.1 = (bf16[384,2304]{1,0:T(8,128)(2,1)}, bf16[384,2304]{1,0:T(8,128)(2,1)}, u32[]{:S(2)}, u32[]{:S(2)}) collective-permute-start(bf16[384,2304]{1,0:T(8,128)(2,1)} %pad_maximum_fusion.1.refs_3_.refs_4_.refs_0_), channel_id=1, source_target_pairs={{0,16},{8,24},{16,0},{24,8},{1,17},{9,25},{17,1},{25,9},{2,18},{10... | collective-permute-start | bytes 5308424 | tf_op jit(solution)/shard_map/ppermute | solution.py:43
  8.8 43.3 %collective-permute-start.2 = (bf16[384,13]{0,1:T(8,128)(2,1)S(1)}, bf16[384,13]{0,1:T(8,128)(2,1)}, u32[]{:S(2)}, u32[]{:S(2)}) collective-permute-start(bf16[384,13]{0,1:T(8,128)(2,1)S(1)} %concatenate.68), channel_id=1, source_target_pairs={{0,16},{8,24},{16,0},{24,8},{1,17},{9,25},{17,1},{25,9},{2,18},{10... | collective-permute-start | bytes 29960 | tf_op jit(solution)/shard_map/ppermute | solution.py:43
  12.1 40.0 %collective-permute-start = (bf16[544,1536]{1,0:T(8,128)(2,1)}, bf16[544,1536]{1,0:T(8,128)(2,1)}, u32[]{:S(2)}, u32[]{:S(2)}) collective-permute-start(bf16[544,1536]{1,0:T(8,128)(2,1)} %pad_maximum_fusion.2), channel_id=1, source_target_pairs={{0,2},{2,4},{4,6},{1,3},{3,5},{5,7},{8,10},{10,12},{12,14},{9,11},... | collective-permute-start | bytes 5013512 | tf_op jit(solution)/shard_map/ppermute | solution.py:76
  52.1 29.8 %collective-permute-start.5 = (bf16[384,2304]{1,0:T(8,128)(2,1)}, bf16[384,2304]{1,0:T(8,128)(2,1)}, u32[]{:S(2)}, u32[]{:S(2)}) collective-permute-start(bf16[384,2304]{1,0:T(8,128)(2,1)} %pad_maximum_fusion.1.refs_3_.refs_4_.refs_0_), channel_id=1, source_target_pairs={{0,8},{8,0},{16,24},{24,16},{1,9},{9,1},{17,25},{25,17},{2,10},{10... | collective-permute-start | bytes 5308424 | tf_op jit(solution)/shard_map/ppermute | solution.py:1043
  52.2 29.7 %collective-permute-start.6 = (bf16[384,2304]{1,0:T(8,128)(2,1)}, bf16[384,2304]{1,0:T(8,128)(2,1)}, u32[]{:S(2)}, u32[]{:S(2)}) collective-permute-start(bf16[384,2304]{1,0:T(8,128)(2,1)} %collective-permute-done.1.refs_4_.refs_5_.refs_1_), channel_id=1, source_target_pairs={{0,8},{8,0},{16,24},{24,16},{1,9},{9,1},{17,25},{25,17},{2,10},{10... | collective-permute-start | bytes 5308424 | tf_op jit(solution)/shard_map/ppermute | solution.py:1043
  52.7 40.8 %collective-permute-start.8 = (bf16[1536,384]{1,0:T(8,128)(2,1)S(1)}, bf16[1536,384]{1,0:T(8,128)(2,1)}, u32[]{:S(2)}, u32[]{:S(2)}) collective-permute-start(bf16[1536,384]{1,0:T(8,128)(2,1)S(1)} %pad_maximum_fusion.5), channel_id=1, source_target_pairs={{0,16},{8,24},{16,0},{24,8},{1,17},{9,25},{17,1},{25,9},{2,18},{10... | collective-permute-start | bytes 3538952 | tf_op jit(solution)/shard_map/ppermute | solution.py:43
  57.6 24.2 %collective-permute-start.4 = (bf16[320,1536]{1,0:T(8,128)(2,1)}, bf16[320,1536]{1,0:T(8,128)(2,1)}, u32[]{:S(2)}, u32[]{:S(2)}) collective-permute-start(bf16[320,1536]{1,0:T(8,128)(2,1)} %slice.102), channel_id=1, source_target_pairs={{0,2},{2,4},{4,6},{1,3},{3,5},{5,7},{8,10},{10,12},{12,14},{9,11},... | collective-permute-start | bytes 2949128 | tf_op jit(solution)/shard_map/ppermute | solution.py:76
  67.0 30.6 %collective-permute-start.11 = (bf16[384,1024]{1,0:T(8,128)(2,1)}, bf16[384,1024]{1,0:T(8,128)(2,1)}, u32[]{:S(2)}, u32[]{:S(2)}) collective-permute-start(bf16[384,1024]{1,0:T(8,128)(2,1)} %dynamic-slice_bitcast_fusion), channel_id=1, source_target_pairs={{0,16},{8,24},{16,0},{24,8},{1,17},{9,25},{17,1},{25,9},{2,18},{10... | collective-permute-start | bytes 2359304 | tf_op jit(solution)/shard_map/ppermute | solution.py:43
  95.0 24.5 %collective-permute-start.9 = (bf16[1536,768]{1,0:T(8,128)(2,1)S(1)}, bf16[1536,768]{1,0:T(8,128)(2,1)}, u32[]{:S(2)}, u32[]{:S(2)}) collective-permute-start(bf16[1536,768]{1,0:T(8,128)(2,1)S(1)} %constant_dynamic-update-slice_fusion.3.wo0.wf0), channel_id=1, source_target_pairs={{0,8},{8,0},{16,24},{24,16},{1,9},{9,1},{17,25},{25,17},{2,10},{10... | collective-permute-start | bytes 7077896 | tf_op jit(solution)/shard_map/ppermute | solution.py:52
  97.6 71.1 %collective-permute-start.14 = (bf16[384,4096]{1,0:T(8,128)(2,1)}, bf16[384,4096]{1,0:T(8,128)(2,1)}, u32[]{:S(2)}, u32[]{:S(2)}) collective-permute-start(bf16[384,4096]{1,0:T(8,128)(2,1)} %pad_maximum_fusion.rest_0_.rest_4_), channel_id=1, source_target_pairs={{0,16},{8,24},{16,0},{24,8},{1,17},{9,25},{17,1},{25,9},{2,18},{10... | collective-permute-start | bytes 9437192 | tf_op jit(solution)/shard_map/ppermute | solution.py:43
  113.7 25.2 %collective-permute-start.12 = (bf16[384,1024]{1,0:T(8,128)(2,1)}, bf16[384,1024]{1,0:T(8,128)(2,1)}, u32[]{:S(2)}, u32[]{:S(2)}) collective-permute-start(bf16[384,1024]{1,0:T(8,128)(2,1)} %collective-permute-done.11), channel_id=1, source_target_pairs={{0,2},{2,0},{4,6},{6,4},{1,3},{3,1},{5,7},{7,5},{8,10},{10,8},{12,... | collective-permute-start | bytes 2359304 | tf_op jit(solution)/shard_map/ppermute | solution.py:1125
  114.8 42.8 %collective-permute-start.13 = (bf16[384,2048]{1,0:T(8,128)(2,1)}, bf16[384,2048]{1,0:T(8,128)(2,1)}, u32[]{:S(2)}, u32[]{:S(2)}) collective-permute-start(bf16[384,2048]{1,0:T(8,128)(2,1)} %bitcast.36.rest_8_.w0), channel_id=1, source_target_pairs={{0,8},{8,0},{16,24},{24,16},{1,9},{9,1},{17,25},{25,17},{2,10},{10... | collective-permute-start | bytes 4718600 | tf_op jit(solution)/shard_map/ppermute | solution.py:1043
  137.4 20.2 %collective-permute-start.10 = (bf16[512,768]{1,0:T(8,128)(2,1)}, bf16[512,768]{1,0:T(8,128)(2,1)S(1)}, u32[]{:S(2)}, u32[]{:S(2)}) collective-permute-start(bf16[512,768]{1,0:T(8,128)(2,1)} %get-tuple-element.174.mo), channel_id=1, source_target_pairs={{0,1},{1,0},{2,3},{3,2},{4,5},{5,4},{6,7},{7,6},{8,9},{9,8},{10,11... | collective-permute-start | bytes 2359304 | tf_op jit(solution)/shard_map/ppermute | solution.py:1040
  139.0 37.4 %collective-permute-start.15 = (bf16[384,4096]{1,0:T(8,128)(2,1)}, bf16[384,4096]{1,0:T(8,128)(2,1)}, u32[]{:S(2)}, u32[]{:S(2)}) collective-permute-start(bf16[384,4096]{1,0:T(8,128)(2,1)} %pad_maximum_fusion.rest_0_.rest_4_), channel_id=1, source_target_pairs={{0,8},{8,0},{16,24},{24,16},{1,9},{9,1},{17,25},{25,17},{2,10},{10... | collective-permute-start | bytes 9437192 | tf_op jit(solution)/shard_map/ppermute | solution.py:1043
  170.7 111.0 %collective-permute-start.22 = (bf16[288,896]{1,0:T(8,128)(2,1)}, bf16[288,896]{1,0:T(8,128)(2,1)S(1)}, u32[]{:S(2)}, u32[]{:S(2)}) collective-permute-start(bf16[288,896]{1,0:T(8,128)(2,1)} %pad_maximum_fusion.7), channel_id=1, source_target_pairs={{4,0},{6,2},{5,1},{7,3},{12,8},{14,10},{13,9},{15,11},{20,16},{22,... | collective-permute-start | bytes 1548296 | tf_op jit(solution)/shard_map/ppermute | solution.py:76
  172.0 111.0 %collective-permute-start.21 = (bf16[512,896]{1,0:T(8,128)(2,1)}, bf16[512,896]{1,0:T(8,128)(2,1)}, u32[]{:S(2)}, u32[]{:S(2)}) collective-permute-start(bf16[512,896]{1,0:T(8,128)(2,1)} %pad_maximum_fusion.6), channel_id=1, source_target_pairs={{2,0},{4,2},{6,4},{3,1},{5,3},{7,5},{10,8},{12,10},{14,12},{11,9},... | collective-permute-start | bytes 2752520 | tf_op jit(solution)/shard_map/ppermute | solution.py:76
  204.4 21.5 %collective-permute-start.18 = (bf16[256,1664]{1,0:T(8,128)(2,1)}, bf16[256,1664]{1,0:T(8,128)(2,1)S(1)}, u32[]{:S(2)}, u32[]{:S(2)}) collective-permute-start(bf16[256,1664]{1,0:T(8,128)(2,1)} %get-tuple-element.204), channel_id=1, source_target_pairs={{0,1},{1,0},{2,3},{3,2},{4,5},{5,4},{6,7},{7,6},{8,9},{9,8},{10,11... | collective-permute-start | bytes 2555912 | tf_op jit(solution)/shard_map/ppermute | solution.py:1040
  249.9 54.6 %collective-permute-start.23 = (bf16[512,896]{1,0:T(8,128)(2,1)}, bf16[512,896]{1,0:T(8,128)(2,1)S(1)}, u32[]{:S(2)}, u32[]{:S(2)}) collective-permute-start(bf16[512,896]{1,0:T(8,128)(2,1)} %get-tuple-element.225.d_ref.gd_ref), channel_id=1, source_target_pairs={{2,0},{4,2},{6,4},{3,1},{5,3},{7,5},{10,8},{12,10},{14,12},{11,9},... | collective-permute-start | bytes 2752520 | tf_op jit(solution)/shard_map/ppermute | solution.py:76
  252.9 51.6 %collective-permute-start.24 = (bf16[288,896]{1,0:T(8,128)(2,1)}, bf16[288,896]{1,0:T(8,128)(2,1)S(1)}, u32[]{:S(2)}, u32[]{:S(2)}) collective-permute-start(bf16[288,896]{1,0:T(8,128)(2,1)} %get-tuple-element.224), channel_id=1, source_target_pairs={{4,0},{6,2},{5,1},{7,3},{12,8},{14,10},{13,9},{15,11},{20,16},{22,... | collective-permute-start | bytes 1548296 | tf_op jit(solution)/shard_map/ppermute | solution.py:76
  267.6 80.8 %collective-permute-start.20 = (bf16[512,1664]{1,0:T(8,128)(2,1)S(1)}, bf16[512,1664]{1,0:T(8,128)(2,1)}, u32[]{:S(2)}, u32[]{:S(2)}) collective-permute-start(bf16[512,1664]{1,0:T(8,128)(2,1)S(1)} %copy-done.8), channel_id=1, source_target_pairs={{0,1},{1,0},{2,3},{3,2},{4,5},{5,4},{6,7},{7,6},{8,9},{9,8},{10,11... | collective-permute-start | bytes 5111816 | tf_op jit(solution)/shard_map/ppermute | solution.py:1040
  281.7 47.1 %collective-permute-start.25 = (f32[8,128]{1,0:T(8,128)S(1)}, f32[8,128]{1,0:T(8,128)S(1)}, u32[]{:S(2)}, u32[]{:S(2)}) collective-permute-start(f32[8,128]{1,0:T(8,128)S(1)} %copy-done.39), channel_id=1, source_target_pairs={{2,0},{4,2},{6,4},{3,1},{5,3},{7,5},{10,8},{12,10},{14,12},{11,9},... | collective-permute-start | bytes 12296 | tf_op jit(solution)/shard_map/ppermute | solution.py:76
  353.7 24.6 %all-to-all-start = ((bf16[32,16,768]{2,1,0:T(8,128)(2,1)}), bf16[32,16,768]{2,1,0:T(8,128)(2,1)S(1)}, u32[]{:S(2)}, u32[]{:S(2)}) async-start(bf16[32,16,768]{2,1,0:T(8,128)(2,1)} %bitcast.134), calls=%async_computation | async-start | bytes 1572864 | tf_op jit(solution)/shard_map/all_to_all | solution.py:1224
  361.3 24.6 %collective-permute-start.28 = (bf16[256,1536]{1,0:T(8,128)(2,1)}, bf16[256,1536]{1,0:T(8,128)(2,1)S(1)}, u32[]{:S(2)}, u32[]{:S(2)}) collective-permute-start(bf16[256,1536]{1,0:T(8,128)(2,1)} %shard_map.280.own_ref), channel_id=1, source_target_pairs={{0,1},{1,0},{2,3},{3,2},{4,5},{5,4},{6,7},{7,6},{8,9},{9,8},{10,11... | collective-permute-start | bytes 2359304 | tf_op jit(solution)/shard_map/ppermute | solution.py:1040
  (47 other events, 494.8 us)
